TPU v7x, 32 devices: a whole 2x2x4 slice. The times are simulated.
32 devices in a mesh: seq: 8 (over z, x), fsdp: 4 (over y, core).
Axes of the slice: x: 2, y: 2, z: 4, core: 2. Of those that a mesh axis runs over, the one named last changes fastest.
Arguments:
- tokens: bfloat16 [4, 2048, 1536], P('fsdp', 'seq'), may hold values from -6 to 6
- lengths: int32 [4], P('fsdp'), may hold values from 512 to 2048, as said below
- norm_gain: bfloat16 [1536], P('fsdp'), may hold values from 0.099609375 to 1.8984375
- in_weight: bfloat16 [1536, 6448], P('fsdp'), may hold values from -0.15625 to 0.15625
- conv_weight: bfloat16 [4, 3328], P(None, 'fsdp'), may hold values from -3 to 3
- conv_bias: bfloat16 [3328], P('fsdp'), may hold values from -0.5 to 0.5
- dt_bias: bfloat16 [48], P('fsdp'), may hold values from -4.5 to -3.5
- decay_log: bfloat16 [48], P('fsdp'), may hold values from -9 to 0
- skip_gain: bfloat16 [48], P('fsdp'), may hold values from 0.5 to 1.5
- gated_gain: bfloat16 [3072], P('fsdp'), may hold values from 0.099609375 to 1.8984375
- out_weight: bfloat16 [3072, 1536], P('fsdp'), may hold values from -0.109375 to 0.109375
- cotangent: bfloat16 [4, 2048, 1536], P('fsdp', 'seq'), may hold values from -6 to 6
Outputs:
- mixed: bfloat16 [4, 2048, 1536], P('fsdp', 'seq')
- input_grad: float32 [4, 2048, 1536], P('fsdp', 'seq')
- norm_gain_grad: float32 [1536], P('fsdp')
- in_weight_grad: float32 [1536, 6448], P('fsdp')
- conv_weight_grad: float32 [4, 3328], P(None, 'fsdp')
- conv_bias_grad: float32 [3328], P('fsdp')
- dt_bias_grad: float32 [48], P('fsdp')
- decay_log_grad: float32 [48], P('fsdp')
- skip_gain_grad: float32 [48], P('fsdp')
- gated_gain_grad: float32 [3072], P('fsdp')
- out_weight_grad: float32 [3072, 1536], P('fsdp')
Inputs may be any that keep to these rules, and one draw needn't show every extreme that they name: `lengths`: each slot's valid positions come first; some slot has all 2048 valid.
All inputs are finite; a program needn't handle non-finite values.
Results may differ from a plain program's by a relative error of at most 0.012.
The roundings to bfloat16 on the way count: a program that leaves them out, or rounds other values in their place, can miss the bound.
Values may be sent and summed in bfloat16 or wider, within the bound.
No kernel may reach another device: no remote copies, remote signals or barrier semaphores. Data moves between devices by JAX's collectives and lax.ppermute only.
A program may use at most 256 MiB of HBM per device.

v0:
```python
import jax
import jax.numpy as jnp
from jax import lax
from jax.sharding import PartitionSpec as P

epsilon = 1e-05
triple = lax.Precision.HIGH


def from_behind(value, axis, by):
    count = lax.axis_size(axis)
    pairs = [(i, i + by) for i in range(count) if 0 <= i + by < count]
    return lax.ppermute(value, axis, pairs)


def carried_in(value, axis, combine, identity, reverse):
    count, position = (lax.axis_size(axis), lax.axis_index(axis))
    everything = jax.tree.map(lambda part: lax.all_gather(part, axis), value)
    start = jax.tree.map(
        lambda part, zero: jnp.broadcast_to(jnp.asarray(zero, part.dtype), part.shape),
        value,
        identity,
    )

    def lap(k, before):
        at = count - 1 - k if reverse else k
        reached = at > position if reverse else at < position
        new = combine(before, jax.tree.map(lambda part: part[at], everything))
        return jax.tree.map(lambda a, b: jnp.where(reached, a, b), new, before)

    return lax.fori_loop(0, count, lap, start)


def rms_scale(inputs, gain):
    inv_rms = lax.rsqrt(jnp.mean(inputs * inputs, axis=-1, keepdims=True) + epsilon)
    return inputs * inv_rms * gain


def convolve(extended, conv_w, conv_b):
    taps = conv_w.shape[0]
    count = extended.shape[1] - taps + 1
    summed = conv_b + jnp.zeros(extended[:, :count].shape, jnp.float32)
    for offset in range(taps):
        summed = summed + extended[:, offset : offset + count] * conv_w[offset]
    return jax.nn.silu(summed)


def local_scan(values, b_rows, c_rows, step_raw, dt_b, decay_l):
    step_size = jax.nn.softplus(step_raw + dt_b)
    log_decay = jnp.cumsum(-step_size * jnp.exp(decay_l), axis=1)
    count = values.shape[1]
    places = jnp.arange(count)
    lower = (places[:, None] >= places[None, :])[None, :, :, None]
    gaps = log_decay[:, :, None, :] - log_decay[:, None, :, :]
    weights = jnp.where(lower, jnp.exp(jnp.where(lower, gaps, 0.0)), 0.0)
    intersection = jnp.einsum("stn,sun->stu", c_rows, b_rows, precision=triple)
    mixing = weights * intersection[..., None] * step_size[:, None, :, :]
    local_out = jnp.einsum("stuh,suhp->sthp", mixing, values, precision=triple)
    to_end = jnp.exp(log_decay[:, -1:, :] - log_decay) * step_size
    local_state = jnp.einsum("sqh,sqhp,sqn->shpn", to_end, values, b_rows, precision=triple)
    return (local_out, local_state, jnp.exp(log_decay[:, -1, :]), jnp.exp(log_decay))


def finish(local_out, c_rows, decay_in, state_in, values, skip_g, gate_part, gated_g):
    carried_out = decay_in[..., None] * jnp.einsum(
        "sqn,shpn->sqhp", c_rows, state_in, precision=triple
    )
    mixed_heads = local_out + carried_out + skip_g[:, None] * values
    flat = mixed_heads.reshape(gate_part.shape)
    return rms_scale(flat * jax.nn.silu(gate_part), gated_g)


def chain(earlier, later):
    return (earlier[0] * later[0], later[0][..., None, None] * earlier[1] + later[1])


def per_device(
    tokens,
    lengths,
    norm_gain,
    in_weight,
    conv_weight,
    conv_bias,
    dt_bias,
    decay_log,
    skip_gain,
    gated_gain,
    out_weight,
    cotangent,
):
    gathered = (
        lax.all_gather(norm_gain, "fsdp", axis=0, tiled=True),
        lax.all_gather(in_weight, "fsdp", axis=0, tiled=True),
        lax.all_gather(conv_weight, "fsdp", axis=1, tiled=True),
        lax.all_gather(conv_bias, "fsdp", axis=0, tiled=True),
        lax.all_gather(dt_bias, "fsdp", axis=0, tiled=True),
        lax.all_gather(decay_log, "fsdp", axis=0, tiled=True),
        lax.all_gather(skip_gain, "fsdp", axis=0, tiled=True),
        lax.all_gather(gated_gain, "fsdp", axis=0, tiled=True),
        lax.all_gather(out_weight, "fsdp", axis=0, tiled=True),
    )
    full_in = gathered[1]
    full_out = gathered[8]
    norm_f, conv_wf, conv_bf, dtb_f, decay_f, skip_f, ggain_f = [
        gathered[index].astype(jnp.float32) for index in (0, 2, 3, 4, 5, 6, 7)
    ]
    slots, seg, width = tokens.shape
    inner = full_out.shape[0]
    heads = dtb_f.shape[0]
    head_size = inner // heads
    conv_width = conv_wf.shape[1]
    state_width = (conv_width - inner) // 2
    taps = conv_wf.shape[0]
    places = lax.axis_index("seq") * seg + jnp.arange(seg)
    valid = (places[None, :] < lengths[:, None]).astype(jnp.float32)
    inputs = tokens.astype(jnp.float32)
    normed_f, pull_norm = jax.vjp(rms_scale, inputs, norm_f)
    normed = normed_f.astype(jnp.bfloat16)
    projected = jnp.einsum(
        "sqd,dp->sqp", normed, full_in, preferred_element_type=jnp.float32
    ).astype(jnp.bfloat16)
    gate_part = projected[..., :inner].astype(jnp.float32)
    conv_in = projected[..., inner : inner + conv_width]
    step_raw = projected[..., inner + conv_width :].astype(jnp.float32)
    previous = from_behind(conv_in[:, seg - (taps - 1) :], "seq", 1)
    extended = jnp.concatenate([previous, conv_in], axis=1).astype(jnp.float32)
    activated_f, pull_conv = jax.vjp(convolve, extended, conv_wf, conv_bf)
    activated = lax.optimization_barrier(activated_f.astype(jnp.bfloat16)).astype(jnp.float32)
    values = activated[..., :inner].reshape(slots, seg, heads, head_size)
    b_rows = activated[..., inner : inner + state_width]
    c_rows = activated[..., inner + state_width :]
    scanned, pull_local = jax.vjp(local_scan, values, b_rows, c_rows, step_raw, dtb_f, decay_f)
    local_out, local_state, whole_decay, decay_in = scanned
    identity = (
        jnp.ones((slots, heads), jnp.float32),
        jnp.zeros((slots, heads, head_size, state_width), jnp.float32),
    )
    state_in = carried_in((whole_decay, local_state), "seq", chain, identity, False)[1]
    gated_f, pull_finish = jax.vjp(
        finish, local_out, c_rows, decay_in, state_in, values, skip_f, gate_part, ggain_f
    )
    gated_out = gated_f.astype(jnp.bfloat16)
    branch = jnp.einsum("sqi,id->sqd", gated_out, full_out, preferred_element_type=jnp.float32)
    mixed = (valid[..., None] * (inputs + branch)).astype(jnp.bfloat16)
    back_in, back_out = (
        lax.all_gather(in_weight, "fsdp", axis=0, tiled=True),
        lax.all_gather(out_weight, "fsdp", axis=0, tiled=True),
    )
    upstream = valid[..., None] * cotangent.astype(jnp.float32)
    back_branch = upstream.astype(jnp.bfloat16)
    grad_out_w = jnp.einsum(
        "sqi,sqd->id", gated_out, back_branch, preferred_element_type=jnp.float32
    )
    back_gated = jnp.einsum(
        "sqd,id->sqi", back_branch, back_out, preferred_element_type=jnp.float32
    )
    d_local, d_crows_one, d_decay_in, d_state_local, d_values_one, d_skip, d_gate, d_ggain = (
        pull_finish(back_gated)
    )
    state_after = carried_in((whole_decay, d_state_local), "seq", chain, identity, True)[1]
    d_whole = jnp.sum(state_after * state_in, axis=(2, 3))
    d_values_two, d_brows, d_crows_two, d_step, d_dtb, d_decay = pull_local(
        (d_local, state_after, d_whole, d_decay_in)
    )
    d_active = jnp.concatenate(
        [
            (d_values_one + d_values_two).reshape(slots, seg, inner),
            d_brows,
            d_crows_one + d_crows_two,
        ],
        axis=-1,
    )
    d_extended, d_conv_w, d_conv_b = pull_conv(d_active)
    returned = from_behind(d_extended[:, : taps - 1].astype(jnp.bfloat16), "seq", -1).astype(
        jnp.float32
    )
    d_conv_in = d_extended[:, taps - 1 :] + jnp.pad(returned, ((0, 0), (seg - taps + 1, 0), (0, 0)))
    back_projected = jnp.concatenate([d_gate, d_conv_in, d_step], axis=-1).astype(jnp.bfloat16)
    grad_in_w = jnp.einsum(
        "sqd,sqp->dp", normed, back_projected, preferred_element_type=jnp.float32
    )
    back_normed = jnp.einsum(
        "sqp,dp->sqd", back_projected, back_in, preferred_element_type=jnp.float32
    )
    d_inputs, d_norm = pull_norm(back_normed)
    input_grad = upstream + d_inputs
    shares = (
        lax.psum_scatter(d_norm, "fsdp", scatter_dimension=0, tiled=True),
        lax.psum_scatter(grad_in_w, "fsdp", scatter_dimension=0, tiled=True),
        lax.psum_scatter(d_conv_w, "fsdp", scatter_dimension=1, tiled=True),
        lax.psum_scatter(d_conv_b, "fsdp", scatter_dimension=0, tiled=True),
        lax.psum_scatter(d_dtb, "fsdp", scatter_dimension=0, tiled=True),
        lax.psum_scatter(d_decay, "fsdp", scatter_dimension=0, tiled=True),
        lax.psum_scatter(d_skip, "fsdp", scatter_dimension=0, tiled=True),
        lax.psum_scatter(d_ggain, "fsdp", scatter_dimension=0, tiled=True),
        lax.psum_scatter(grad_out_w, "fsdp", scatter_dimension=0, tiled=True),
    )
    totals = lax.psum(
        (
            shares[0],
            shares[1],
            shares[2],
            shares[3],
            shares[4],
            shares[5],
            shares[6],
            shares[7],
            shares[8],
        ),
        "seq",
    )
    return (
        mixed,
        input_grad,
        totals[0],
        totals[1],
        totals[2],
        totals[3],
        totals[4],
        totals[5],
        totals[6],
        totals[7],
        totals[8],
    )


def solution(mesh):
    placed = (
        P("fsdp", "seq", None),
        P("fsdp"),
        P("fsdp"),
        P("fsdp", None),
        P(None, "fsdp"),
        P("fsdp"),
        P("fsdp"),
        P("fsdp"),
        P("fsdp"),
        P("fsdp"),
        P("fsdp", None),
        P("fsdp", "seq", None),
    )
    return jax.shard_map(
        per_device,
        mesh=mesh,
        in_specs=placed,
        out_specs=(
            P("fsdp", "seq", None),
            P("fsdp", "seq", None),
            P("fsdp"),
            P("fsdp", None),
            P(None, "fsdp"),
            P("fsdp"),
            P("fsdp"),
            P("fsdp"),
            P("fsdp"),
            P("fsdp"),
            P("fsdp", None),
        ),
        check_vma=False,
    )
```

profile of v0, /device:TPU:0, one launch (start us, length us, event | category | flops | bytes accessed | tf_op | source)
XLA Modules:
  0.0 1545.3 jit_solution(13398759697782761256)
XLA Ops:
  8.1 6.2 all-gather.3
  22.8 7.5 all-reduce.24
  32.0 105.5 %all-gather.10.cloned.1.call-done = bf16[1536,6448]{0,1:T(8,128)(2,1)} async-done(((bf16[384,6448]{0,1:T(8,128)(2,1)}), bf16[1536,6448]{0,1:T(8,128)(2,1)}) %all-gather.10.cloned.1.call-update) | async-done | bytes 19808272 | tf_op jit(solution)/shard_map/all_gather | solution.py:93
  137.4 9.9 fusion.6
  193.9 19.5 %all_gather.53 = f32[8,1,48]{2,1,0:T(1,128)} all-gather(f32[1,1,48]{2,1,0:T(1,128)} %get-tuple-element.423), channel_id=1, replica_groups=mesh['seq'=8,'fsdp'=4] {'seq'}, dimensions={0}, use_global_device_ids=true | all-gather | bytes 1728 | tf_op jit(solution)/shard_map/all_gather | solution.py:18
  218.8 130.8 %all-gather.14.cloned.1.call-done = f32[384,64,128]{2,1,0:T(8,128)} async-done(((f32[48,64,128]{2,1,0:T(8,128)}), f32[384,64,128]{2,1,0:T(8,128)}) %all-gather.14.cloned.1.call-update) | async-done | bytes 12582928 | tf_op jit(solution)/shard_map/all_gather | solution.py:18
  349.6 36.0 %while.30 = (s32[]{:T(128)}, f32[1,48,64,128]{3,2,1,0:T(8,128)}, s32[]{:T(128)}, f32[8,1,48]{2,1,0:T(1,128)}, f32[8,1,48,64,128]{4,3,2,1,0:T(8,128)}, /*index=5*/s32[]{:T(128)}, s32[]{:T(128)}) while((s32[]{:T(128)}, f32[1,48,64,128]{3,2,1,0:T(8,128)}, s32[]{:T(128)}, f32[8,1,48]{2,1,0:T(1,128)}, f32[8,1,48,64,128]{4,3,2,1,0:T(8,128)}, ...), condition=%wide.region_4.5_spmd.clone, body=%wide.region_3.4_spmd.clone.sunk | while | flops 1572868 | bytes 4719281 | solution.py:31
  388.6 9.6 fusion.34
  413.6 10.0 fusion.35
  423.7 5.9 multiply_reduce_fusion.5
  440.9 12.7 fusion.76
  457.6 14.9 fusion.8
  491.6 125.8 %all-gather.16.cloned.1.call-done = f32[384,64,128]{2,1,0:T(8,128)} async-done(((f32[48,64,128]{2,1,0:T(8,128)}), f32[384,64,128]{2,1,0:T(8,128)}) %all-gather.16.cloned.1.call-update) | async-done | bytes 12582928 | tf_op jit(solution)/shard_map/all_gather | solution.py:18
  617.4 38.9 %while.31 = (s32[]{:T(128)}, f32[1,48,64,128]{3,2,1,0:T(8,128)}, s32[]{:T(128)}, f32[8,1,48]{2,1,0:T(1,128)}, f32[8,1,48,64,128]{4,3,2,1,0:T(8,128)}, /*index=5*/s32[]{:T(128)}, s32[]{:T(128)}, s32[]{:T(128)}, s32[]{:T(128)}) while((s32[]{:T(128)}, f32[1,48,64,128]{3,2,1,0:T(8,128)}, s32[]{:T(128)}, f32[8,1,48]{2,1,0:T(1,128)}, ...), condition=%wide.region_8.9_spmd.clone, body=%wide.region_7.8_spmd.clone.sunk | while | flops 1572872 | bytes 4719343 | solution.py:31
  676.3 11.0 fusion.33
  712.4 18.5 %fusion.61 = f32[1536,6448]{0,1:T(8,128)} fusion(bf16[256,48]{1,0:T(8,128)(2,1)} %bitcast.336, bf16[256,3328]{1,0:T(8,128)(2,1)} %fusion.42, bf16[256,3072]{1,0:T(8,128)(2,1)} %get-tuple-element.412, bf16[1,256,1536]{2,1,0:T(8,128)(2,1)} %param.16, f32[1536]{0:T(1024)S(1)} %reshape.620, f32[256]{0:T(256)S(1)} %fusion.111), kind=kOutput, calls=%fused_computation.114 | convolution fusion | flops 5082390528 | bytes 43711488 | tf_op jit(solution)/shard_map/sqd,sqp->dp/dot_general | solution.py:179
  733.6 23.9 %reduce-scatter.8.cloned.1.call-done = f32[768,1536]{1,0:T(8,128)} async-done(((f32[3072,1536]{1,0:T(8,128)}), f32[768,1536]{1,0:T(8,128)}) %reduce-scatter.8.cloned.1.call-update) | async-done | bytes 4718608 | tf_op jit(solution)/shard_map/reduce_scatter | solution.py:196
  757.6 279.1 %reduce-scatter.6.cloned.1.call-done = f32[384,6448]{0,1:T(8,128)} async-done(((f32[1536,6448]{0,1:T(8,128)}), f32[384,6448]{0,1:T(8,128)}) %reduce-scatter.6.cloned.1.call-update) | async-done | bytes 9904144 | tf_op jit(solution)/shard_map/reduce_scatter | solution.py:189
  1039.9 7.5 fusion.39
  1047.6 10.0 fusion.44
  1057.6 12.3 all-reduce.23
  1073.2 39.6 %all-reduce.21 = (f32[384]{0:T(512)}, f32[4,832]{1,0:T(4,128)}, f32[832]{0:T(1024)}, f32[12]{0:T(128)}, f32[12]{0:T(128)}, /*index=5*/f32[12]{0:T(128)}, f32[768]{0:T(1024)}) all-reduce(f32[384]{0:T(512)S(1)} %dynamic-slice.5, f32[4,832]{1,0:T(4,128)S(1)} %copy.211, ...), channel_id=1, replica_groups=mesh['seq'=8,'fsdp'=4] {'seq'}, use_global_device_ids=true, to_apply=%region_21.22 | all-reduce | flops 5348 | bytes 42784 | tf_op jit(solution)/shard_map/psum | solution.py:198
  1112.8 414.5 %all-reduce.27.cloned.1.call-done = (f32[384,6448]{0,1:T(8,128)}, f32[768,1536]{1,0:T(8,128)}) async-done(((f32[384,6448]{0,1:T(8,128)}, f32[768,1536]{1,0:T(8,128)}), (f32[384,6448]{0,1:T(8,128)}, f32[768,1536]{1,0:T(8,128)})) %all-reduce.27.cloned.1.call-update) | async-done | bytes 14622736 | tf_op jit(solution)/shard_map/psum | solution.py:198
  1527.4 8.5 copy.231
  (294 shorter events, 241.6 us)
Async XLA Ops:
  7.2 12.7 copy-start.52
  7.2 14.6 copy-start.59
  7.2 14.8 copy-start.60
  7.2 15.1 copy-start.61
  7.2 15.3 copy-start.53
  7.3 24.4 %copy-start.11 = (bf16[1,256,1536]{2,1,0:T(8,128)(2,1)S(1)}, bf16[1,256,1536]{2,1,0:T(8,128)(2,1)}, u32[]{:S(2)}) copy-start(bf16[1,256,1536]{2,1,0:T(8,128)(2,1)} %param.16) | copy-start | bytes 2359300
  7.3 130.2 %all-gather.10.cloned.1.call-start = ((), (), s32[]{:S(2)}) async-start(), calls=%async_computation.3 | async-start | bytes 24760320 | tf_op jit(solution)/shard_map/all_gather | solution.py:93
  8.0 341.6 %all-gather.14.cloned.1.call-start = ((), (), s32[]{:S(2)}) async-start(), calls=%async_computation.7 | async-start | bytes 14155776 | tf_op jit(solution)/shard_map/all_gather | solution.py:18
  30.3 117.0 %copy-start.62 = (bf16[48]{0:T(256)(128)(2,1)}, bf16[48]{0:T(256)(128)(2,1)S(1)}, u32[]{:S(2)}) copy-start(bf16[48]{0:T(256)(128)(2,1)S(1)} %get-tuple-element.398) | copy-start | bytes 292
  30.9 125.8 %copy-start.40 = (f32[48]{0:T(128)}, f32[48]{0:T(128)S(1)}, u32[]{:S(2)}) copy-start(f32[48]{0:T(128)S(1)} %convert_element_type.95) | copy-start | bytes 580
  31.9 115.4 %copy-start.44 = (f32[256]{0:T(256)}, f32[256]{0:T(256)S(1)}, u32[]{:S(2)}) copy-start(f32[256]{0:T(256)S(1)} %fusion.46) | copy-start | bytes 3076
  31.9 115.4 %copy-start.55 = (f32[48]{0:T(128)}, f32[48]{0:T(128)S(1)}, u32[]{:S(2)}) copy-start(f32[48]{0:T(128)S(1)} %convert_exponential_fusion) | copy-start | bytes 580
  147.3 12.2 copy-start.10
  151.4 8.1 collective-permute-start
  174.5 239.1 %all-gather.12.cloned.1.call-start = ((), (), s32[]{:S(2)}) async-start(), calls=%async_computation.4 | async-start | bytes 11796480 | tf_op jit(solution)/shard_map/all_gather | solution.py:100
  175.2 442.2 %all-gather.16.cloned.1.call-start = ((), (), s32[]{:S(2)}) async-start(), calls=%async_computation.8 | async-start | bytes 14155776 | tf_op jit(solution)/shard_map/all_gather | solution.py:18
  440.8 316.7 %reduce-scatter.8.cloned.1.call-start = ((), (), s32[]{:S(2)}) async-start(), calls=%async_computation.6 | async-start | bytes 23592960 | tf_op jit(solution)/shard_map/reduce_scatter | solution.py:196
  453.6 583.1 %reduce-scatter.6.cloned.1.call-start = ((), (), s32[]{:S(2)}) async-start(), calls=%async_computation.5 | async-start | bytes 49520640 | tf_op jit(solution)/shard_map/reduce_scatter | solution.py:189
  704.1 6.0 collective-permute-start.1
  731.0 341.1 %reduce-scatter.10.cloned.1.call-start = ((), (), s32[]{:S(2)}) async-start(), calls=%async_computation.9 | async-start | bytes 2129920
  733.6 793.8 %all-reduce.27.cloned.1.call-start = ((), (), s32[]{:S(2)}) async-start(), calls=%async_computation.10 | async-start | bytes 29245440 | tf_op jit(solution)/shard_map/psum | solution.py:198
  1047.5 22.8 %copy-start.45 = (f32[256]{0:T(256)S(1)}, f32[256]{0:T(256)}, u32[]{:S(2)}) copy-start(f32[256]{0:T(256)} %copy-done.44) | copy-start | bytes 3076
  1047.5 22.8 %copy-start.13 = (bf16[1,256,1536]{2,1,0:T(8,128)(2,1)S(1)}, bf16[1,256,1536]{2,1,0:T(8,128)(2,1)}, u32[]{:S(2)}) copy-start(bf16[1,256,1536]{2,1,0:T(8,128)(2,1)} %param.16) | copy-start | bytes 2359300
  1047.5 22.8 %copy-start.20 = (bf16[1,256,1536]{2,1,0:T(8,128)(2,1)S(1)}, bf16[1,256,1536]{2,1,0:T(8,128)(2,1)}, u32[]{:S(2)}) copy-start(bf16[1,256,1536]{2,1,0:T(8,128)(2,1)} %param.27) | copy-start | bytes 2359300
  (51 other events, 259.3 us)
Sparse Core Ops, SparseCore 0:
  9.7 127.6 all-gather.9
  174.6 174.9 all-gather.13
  351.1 62.4 all-gather.11
  441.0 176.4 all-gather.15
  619.9 137.6 reduce-scatter.7
  760.2 276.4 reduce-scatter.5
  1039.8 29.6 reduce-scatter.9
  1074.4 452.8 all-reduce.26
where the time goes:
time: 1550 us
  waiting for transfers between devices  1090 us (70%)
  matrix products  135 us (9%)
  other arithmetic  113 us (7%)
  blocking collectives  95.7 us (6%)
  local copies, waits for them, and re-layouts  88.4 us (6%)
  between operations  20.3 us (1%)
    psum x1, waiting for transfers between devices, per_device(): lax.psum((shares[0], shares[1], shares[2], shares[3], shares[4], shares[5...  415 us
    reduce_scatter x1, waiting for transfers between devices, per_device(): lax.psum_scatter(grad_in_w, 'fsdp', scatter_dimension=0, tiled=True)  279 us
    all_gather x2, waiting for transfers between devices, carried_in(): everything = jax.tree.map(lambda part: lax.all_gather(part, axis), value)  257 us
    all_gather x1, waiting for transfers between devices, per_device(): lax.all_gather(in_weight, 'fsdp', axis=0, tiled=True)  105 us
    select_n x16, other arithmetic, lap(): return jax.tree.map(lambda a, b: jnp.where(reached, a, b), new, before)  56.7 us
    psum x1, blocking collectives, per_device(): lax.psum((shares[0], shares[1], shares[2], shares[3], shares[4], shares[5...  39.6 us
    dot_general x3, matrix products, local_scan(): local_out = jnp.einsum('stuh,suhp->sthp', mixing, values, precision=triple)  35.5 us
  transfers between devices with their start and end apart: 10, of which 8 were waited for; matrix products, arithmetic and copies ran while one was open for 17% of the time, Pallas kernels for 0%

commit v1 on v0

v1 whole, which is shorter than its diff:
```python
import functools

import jax
import jax.numpy as jnp
from jax import lax
from jax.experimental import pallas as pl
from jax.experimental.pallas import tpu as pltpu
from jax.sharding import PartitionSpec as P

epsilon = 1e-05
bf16, f32 = jnp.bfloat16, jnp.float32
best = lax.Precision.HIGHEST
halo = 16
lanes = 128
head_size = 64


def dot(a, b, ca=1, cb=0, precision=None):
    return lax.dot_general(
        a, b, (((ca,), (cb,)), ((), ())), preferred_element_type=f32, precision=precision
    )


def sigmoid(v):
    return 1.0 / (1.0 + jnp.exp(-v))


def iota(shape, axis):
    return lax.broadcasted_iota(jnp.int32, shape, axis)


def spread(columns, pair):
    first, second = 2 * pair, 2 * pair + 1
    rows = columns.shape[0]
    return jnp.where(
        iota((rows, lanes), 1) < head_size,
        columns[:, first : first + 1],
        columns[:, second : second + 1],
    )


def of_heads(pair):
    return (iota((lanes, lanes), 1) == 2 * pair + iota((lanes, lanes), 0) // head_size).astype(f32)


def convolved(pc_ref, taps_ref, at):
    x = pc_ref[0, :, at : at + lanes].astype(f32)
    tapped = [pltpu.roll(x, 3 - k, 0)[halo:] for k in range(3)] + [x[halo:]]
    pre = taps_ref[4:5, at : at + lanes]
    for k in range(4):
        pre = pre + tapped[k] * taps_ref[k : k + 1, at : at + lanes]
    return tapped, pre


def forward_kernel(pc_ref, taps_ref, rate_ref, act_ref, y_ref, s_ref, lac_ref, dtc_ref, lar_ref, dtr_ref, *, channels, state):
    width = channels + 2 * state
    for at in range(0, width, lanes):
        _, pre = convolved(pc_ref, taps_ref, at)
        act_ref[0, :, at : at + lanes] = (pre * sigmoid(pre)).astype(bf16)
    seg = act_ref.shape[1]
    z = pc_ref[0, halo:, width : width + lanes].astype(f32) + rate_ref[0:1]
    dtc = jnp.maximum(z, 0.0) + jnp.log1p(jnp.exp(-jnp.abs(z)))
    lower = iota((seg, seg), 0) >= iota((seg, seg), 1)
    lac = dot(lower.astype(f32), -dtc * rate_ref[1:2], precision=best)
    rows = lar_ref.shape[1]
    lar, dtr = lac.T[:rows], dtc.T[:rows]
    lac_ref[0], dtc_ref[0], lar_ref[0], dtr_ref[0] = lac, dtc, lar, dtr
    b_rows = act_ref[0, :, channels : channels + state]
    c_rows = act_ref[0, :, channels + state : width]
    both = dot(c_rows, b_rows, 1, 1)
    to_end = jnp.exp(lac[seg - 1 : seg] - lac) * dtc
    for pair in range(channels // lanes):
        at = pair * lanes
        values = act_ref[0, :, at : at + lanes]
        parts = []
        for side in range(2):
            h = 2 * pair + side
            mix = jnp.where(lower, jnp.exp(lac[:, h : h + 1] - lar[h : h + 1]), 0.0) * both * dtr[h : h + 1]
            parts.append(dot(mix.astype(bf16), values[:, side * head_size : (side + 1) * head_size]))
        y_ref[0, :, at : at + lanes] = jnp.concatenate(parts, axis=1)
        weighted = (spread(to_end, pair) * values.astype(f32)).astype(bf16)
        s_ref[0, at : at + lanes] = dot(weighted, b_rows, 0, 0).astype(bf16)


def finish_kernel(y_ref, act_ref, lac_ref, sin_ref, gate_ref, bg_ref, vec_ref, y_out, stat_ref, *, channels, state):
    seg = y_ref.shape[1]
    c_rows = act_ref[0, :, channels + state : channels + 2 * state]
    decay = jnp.exp(lac_ref[0])
    first = jnp.zeros((seg, 1), f32)
    second = jnp.zeros((seg, 1), f32)
    for pair in range(channels // lanes):
        at = pair * lanes
        here = slice(at, at + lanes)
        carried = dot(c_rows, sin_ref[0, here], 1, 1)
        y = y_ref[0, :, here] + spread(decay, pair) * carried
        y_out[0, :, here] = y
        gate = gate_ref[0, :, here].astype(f32)
        heads = y + vec_ref[0:1, here] * act_ref[0, :, here].astype(f32)
        gated = heads * gate * sigmoid(gate)
        first = first + jnp.sum(gated * gated, axis=1, keepdims=True)
        second = second + jnp.sum(gated * bg_ref[0, :, here] * vec_ref[1:2, here], axis=1, keepdims=True)
    lane = iota((seg, lanes), 1)
    both = jnp.where(lane == 0, first, jnp.where(lane == 1, second, 0.0))
    stat_ref[0] = both.T[:8]


def norm_kernel(y_ref, act_ref, lac_ref, gate_ref, bg_ref, vec_ref, stat_ref, out_ref, dgate_ref, dy_ref, pos_ref, dsin_ref, dskip_ref, *, channels, state, inner):
    seg = y_ref.shape[1]
    stats = stat_ref[0].T
    inv = lax.rsqrt(stats[:, 0:1] * (1.0 / inner) + epsilon)
    lean = inv * inv * inv * (stats[:, 1:2] * (1.0 / inner))
    c_rows = act_ref[0, :, channels + state : channels + 2 * state]
    decay = jnp.exp(lac_ref[0])
    pos = jnp.zeros((seg, lanes), f32)

    @pl.when(pl.program_id(0) == 0)
    def _():
        dskip_ref[...] = jnp.zeros_like(dskip_ref)

    for pair in range(channels // lanes):
        at = pair * lanes
        here = slice(at, at + lanes)
        y = y_ref[0, :, here]
        values = act_ref[0, :, here].astype(f32)
        heads = y + vec_ref[0:1, here] * values
        gate = gate_ref[0, :, here].astype(f32)
        sg = sigmoid(gate)
        gated = heads * gate * sg
        gain = vec_ref[1:2, here]
        out_ref[0, :, here] = (gated * inv * gain).astype(bf16)
        dgated = inv * (bg_ref[0, :, here] * gain) - gated * lean
        dgate_ref[0, :, here] = (dgated * heads * (sg * (1.0 + gate * (1.0 - sg)))).astype(bf16)
        dy = dgated * gate * sg
        dy_ref[0, :, here] = dy
        pos = pos + dot(dy * y, of_heads(pair), precision=best)
        dsin_ref[0, here] = dot((spread(decay, pair) * dy).astype(bf16), c_rows, 0, 0).astype(bf16)
        dskip_ref[0:1, here] += jnp.sum(dy * values, axis=0, keepdims=True)
    pos_ref[0] = pos


def backward_kernel(act_ref, dy_ref, lac_ref, lar_ref, dtr_ref, sin_ref, r_ref, dbc_ref, *, channels, state):
    seg = dy_ref.shape[1]
    b_rows = act_ref[0, :, channels : channels + state]
    c_rows = act_ref[0, :, channels + state : channels + 2 * state]
    both = dot(c_rows, b_rows, 1, 1)
    lower = iota((seg, seg), 0) >= iota((seg, seg), 1)
    lac, lar, dtr = lac_ref[0], lar_ref[0], dtr_ref[0]
    decay = jnp.exp(lac)
    dboth = jnp.zeros((seg, seg), f32)
    dc = jnp.zeros((seg, state), f32)
    for pair in range(channels // lanes):
        at = pair * lanes
        here = slice(at, at + lanes)
        values = act_ref[0, :, here]
        dy = dy_ref[0, :, here]
        dyl = dy.astype(bf16)
        parts = []
        for side in range(2):
            h = 2 * pair + side
            own = slice(side * head_size, (side + 1) * head_size)
            weights = jnp.where(lower, jnp.exp(lac[:, h : h + 1] - lar[h : h + 1]), 0.0)
            parts.append(dot((weights * both).astype(bf16), dyl[:, own], 0, 0))
            dboth = dboth + dot(dyl[:, own], values[:, own], 1, 1) * (weights * dtr[h : h + 1])
        r_ref[0, :, here] = jnp.concatenate(parts, axis=1)
        dc = dc + dot((spread(decay, pair) * dy).astype(bf16), sin_ref[0, here])
    dlow = dboth.astype(bf16)
    dbc_ref[0, :, :state] = dot(dlow, c_rows, 0, 0)
    dbc_ref[0, :, state:] = dc + dot(dlow, b_rows)


def carry_kernel(pc_ref, taps_ref, rate_ref, act_ref, dy_ref, r_ref, pos_ref, lac_ref, dtc_ref, g_ref, sin_ref, s_ref, dbc_ref, vec_ref, dpre_ref, first_ref, dstep_ref, dbc_out, dtaps_ref, drate_ref, *, channels, state):
    seg = dy_ref.shape[1]
    width = channels + 2 * state
    b_rows = act_ref[0, :, channels : channels + state]
    lac, dtc = lac_ref[0], dtc_ref[0]
    last = lac[seg - 1 : seg]
    to_last = jnp.exp(last - lac)
    neg = jnp.zeros((seg, lanes), f32)
    db = jnp.zeros((seg, state), f32)
    through = jnp.zeros((1, lanes), f32)
    local = jnp.zeros((1, lanes), f32)

    @pl.when(pl.program_id(0) == 0)
    def _():
        dtaps_ref[...] = jnp.zeros_like(dtaps_ref)
        drate_ref[...] = jnp.zeros_like(drate_ref)

    for pair in range(channels // lanes):
        at = pair * lanes
        here = slice(at, at + lanes)
        grad = g_ref[0, here]
        values = act_ref[0, :, here].astype(f32)
        reach = spread(to_last, pair)
        step = spread(dtc, pair)
        r = r_ref[0, :, here] + reach * dot(b_rows, grad, 1, 1)
        owners = of_heads(pair)
        neg = neg + dot(values * r, owners, precision=best)
        db = db + dot((reach * step * values).astype(bf16), grad)
        wide = grad.astype(f32)
        through = through + jnp.sum(dot(wide * sin_ref[0, here].astype(f32), owners, 0, 0, best), axis=0, keepdims=True)
        local = local + jnp.sum(dot(wide * s_ref[0, here].astype(f32), owners, 0, 0, best), axis=0, keepdims=True)
        tapped, pre = convolved(pc_ref, taps_ref, at)
        sg = sigmoid(pre)
        dpre = (step * r + vec_ref[0:1, here] * dy_ref[0, :, here]) * (sg * (1.0 + pre * (1.0 - sg)))
        dpre_ref[0, :, here] = dpre
        for k in range(4):
            dtaps_ref[k : k + 1, here] += jnp.sum(dpre * tapped[k], axis=0, keepdims=True)
        dtaps_ref[4:5, here] += jnp.sum(dpre, axis=0, keepdims=True)
    first_ref[0] = dpre_ref[0, :8]
    dbc_out[0, :, :state] = dbc_ref[0, :, :state] + db
    dbc_out[0, :, state:] = dbc_ref[0, :, state:]
    seed = jnp.exp(last) * through + local
    upper = (iota((seg, seg), 0) <= iota((seg, seg), 1)).astype(f32)
    q = dot(upper, pos_ref[0] - dtc * neg, precision=best) + seed
    rates = rate_ref[1:2]
    z = pc_ref[0, halo:, width : width + lanes].astype(f32) + rate_ref[0:1]
    draw = (neg - rates * q) * sigmoid(z)
    dstep_ref[0] = draw.astype(bf16)
    drate_ref[0:1] += jnp.sum(draw, axis=0, keepdims=True)
    drate_ref[1:2] += jnp.sum(q * (-dtc * rates), axis=0, keepdims=True)


def returned_kernel(dpre_ref, next_ref, taps_ref, out_ref):
    seg = dpre_ref.shape[1]
    for at in range(0, dpre_ref.shape[2], lanes):
        here = slice(at, at + lanes)
        x = jnp.concatenate([dpre_ref[0, :, here], next_ref[0, :, here]], axis=0)
        total = x[:seg] * taps_ref[3:4, here]
        for k in range(3):
            by = 3 - k
            total = total + pltpu.roll(x, seg + 8 - by, 0)[:seg] * taps_ref[k : k + 1, here]
        out_ref[0, :, here] = total.astype(bf16)


def call(kernel, slots, ins, outs, name, flops=0, **statics):
    def spec(shape, per):
        if per:
            return pl.BlockSpec((1,) + tuple(shape[1:]), lambda s: (s,) + (0,) * (len(shape) - 1))
        return pl.BlockSpec(tuple(shape), lambda s: (0,) * len(shape))

    moved = sum(a.size * a.dtype.itemsize for a, _ in ins)
    for shape, dtype, _ in outs:
        size = 1
        for d in shape:
            size *= d
        moved += size * jnp.dtype(dtype).itemsize
    return pl.pallas_call(
        functools.partial(kernel, **statics),
        grid=(slots,),
        in_specs=[spec(a.shape, per) for a, per in ins],
        out_specs=[spec(shape, per) for shape, _, per in outs],
        out_shape=[jax.ShapeDtypeStruct(shape, dtype) for shape, dtype, _ in outs],
        compiler_params=pltpu.CompilerParams(vmem_limit_bytes=40 << 20),
        cost_estimate=pl.CostEstimate(flops=flops, bytes_accessed=moved, transcendentals=0),
        name=name,
    )(*[a for a, _ in ins])


def swap(value, axis, by):
    count = lax.axis_size(axis)
    return lax.ppermute(value, axis, [(i, i ^ by) for i in range(count)])


def all_slots(value, axis):
    count = lax.axis_size(axis)
    pieces, by = {0: value}, count // 2
    while by:
        for j in list(pieces):
            pieces[j ^ by] = swap(pieces[j], axis, by)
        by //= 2
    return jnp.concatenate([pieces[j] for j in range(count)], axis=0)


def to_owner(parts, axis):
    count = lax.axis_size(axis)
    parts, by = list(parts), 1
    left = list(range(count))
    while by < count:
        keep = [j for j in left if not j & by]
        new = {}
        for j in keep:
            new[j] = parts[j] + swap(parts[j ^ by].astype(bf16), axis, by).astype(f32)
        parts = [new.get(j) for j in range(count)]
        left = keep
        by *= 2
    return parts[0]


def over_owners(value, axis):
    count, by = lax.axis_size(axis), 1
    while by < count:
        other = swap(value, axis, by)
        value = value + jnp.stack([other[j ^ by] for j in range(count)])
        by *= 2
    return value


def exchange(value, axis):
    return lax.all_to_all(value, axis, 0, 0)


def per_device(tokens, lengths, norm_gain, in_weight, conv_weight, conv_bias, dt_bias, decay_log, skip_gain, gated_gain, out_weight, cotangent):
    nf, nq = lax.axis_size("fsdp"), lax.axis_size("seq")
    me, place = lax.axis_index("fsdp"), lax.axis_index("seq")
    _, seg, width = tokens.shape
    rows = in_weight.shape[0]
    channels = out_weight.shape[0]
    inner = channels * nf
    heads = dt_bias.shape[0]
    conv_own = conv_weight.shape[1]
    state = (conv_own * nf - inner) // 2
    share = 2 * state // nf
    slots = nf

    small = jnp.concatenate([conv_weight, conv_bias[None]], axis=0)
    small = jnp.pad(small, ((0, 3), (0, 0)))
    norm_all = lax.all_gather(norm_gain, "fsdp", axis=0, tiled=True).astype(f32)
    taps_all = lax.all_gather(small, "fsdp", axis=1, tiled=True).astype(f32)
    taps = jnp.concatenate([lax.dynamic_slice_in_dim(taps_all, me * channels, channels, 1), taps_all[:, inner:]], axis=1)
    taps_share = lax.dynamic_slice_in_dim(taps_all, inner + me * share, share, 1)
    rate = jnp.stack([dt_bias.astype(f32), jnp.exp(decay_log.astype(f32))])
    rate = jnp.pad(rate, ((0, 6), (0, lanes - heads)))
    vec = jnp.stack([jnp.repeat(skip_gain.astype(f32), head_size), gated_gain.astype(f32)])
    vec = jnp.pad(vec, ((0, 6), (0, 0)))

    w_value = in_weight[:, inner : 2 * inner].reshape(rows, nf, channels)
    w_rows = jnp.broadcast_to(in_weight[:, 2 * inner : 2 * inner + 2 * state][:, None], (rows, nf, 2 * state))
    w_step = jnp.pad(in_weight[:, 2 * inner + 2 * state :].reshape(rows, nf, heads), ((0, 0), (0, 0), (0, lanes - heads)))
    w_conv = jnp.concatenate([w_value, w_rows, w_step], axis=2).transpose(1, 0, 2)
    w_conv = exchange(w_conv, "fsdp").reshape(width, -1)

    inputs = tokens[0].astype(f32)
    inv = lax.rsqrt(jnp.mean(inputs * inputs, axis=-1, keepdims=True) + epsilon)
    normed_own = (inputs * inv * norm_all).astype(bf16)
    before = lax.ppermute(normed_own[seg - halo :], "seq", [(i, i + 1) for i in range(nq - 1)])
    normed = all_slots(jnp.concatenate([before, normed_own], axis=0)[None], "fsdp")

    valid = (place * seg + jnp.arange(seg) < lengths[0]).astype(f32)[:, None]
    upstream = valid * cotangent[0].astype(f32)
    w_gate = in_weight[:, :inner].reshape(rows, nf, channels).transpose(1, 0, 2)
    w_gate, later, _ = lax.optimization_barrier((w_gate, upstream.astype(bf16), w_conv))
    w_gate = exchange(w_gate, "fsdp").reshape(width, channels)
    back_branch = all_slots(later[None], "fsdp")

    def project(x, w):
        return lax.dot_general(x, w, (((2,), (0,)), ((), ())), preferred_element_type=f32)

    pc = project(normed, w_conv).astype(bf16)
    main = normed[:, halo:]
    cw = channels + 2 * state
    raw = pc[:, halo:, cw:].astype(f32) + rate[0]
    total = jnp.sum(jax.nn.softplus(raw), axis=1)[:, :heads] * -rate[1, :heads]
    piece = slots * channels // nq
    whole = jnp.repeat(jnp.exp(total).reshape(-1), head_size).reshape(nq, piece)
    whole = exchange(whole, "seq")[..., None]

    tall = 16
    statics = dict(channels=channels, state=state)
    act, y_local, s_local, lac, dtc, lar, dtr = call(
        forward_kernel,
        slots,
        [(pc, True), (taps, False), (rate, False)],
        [
            ((slots, seg, cw), bf16, True),
            ((slots, seg, channels), f32, True),
            ((slots, channels, state), bf16, True),
            ((slots, seg, lanes), f32, True),
            ((slots, seg, lanes), f32, True),
            ((slots, tall, seg), f32, True),
            ((slots, tall, seg), f32, True),
        ],
        "forward",
        flops=2 * slots * seg * seg * channels,
        **statics,
    )
    everything = exchange(s_local.reshape(nq, piece, state), "seq").astype(f32)
    carried, reached = jnp.zeros((piece, state), f32), []
    for i in range(nq):
        reached.append(carried.astype(bf16))
        carried = whole[i] * carried + everything[i]
    s_in = exchange(jnp.stack(reached), "seq").reshape(slots, channels, state)

    gate = project(main, w_gate).astype(bf16)
    bg = lax.dot_general(back_branch, out_weight, (((2,), (1,)), ((), ())), preferred_element_type=f32)
    y, stats = call(
        finish_kernel,
        slots,
        [(y_local, True), (act, True), (lac, True), (s_in, True), (gate, True), (bg, True), (vec, False)],
        [((slots, seg, channels), f32, True), ((slots, 8, seg), f32, True)],
        "finish",
        **statics,
    )
    stats = over_owners(stats, "fsdp")
    gated_out, dgate, dy, pos, dsin, dskip = call(
        norm_kernel,
        slots,
        [(y, True), (act, True), (lac, True), (gate, True), (bg, True), (vec, False), (stats, True)],
        [
            ((slots, seg, channels), bf16, True),
            ((slots, seg, channels), bf16, True),
            ((slots, seg, channels), f32, True),
            ((slots, seg, lanes), f32, True),
            ((slots, channels, state), bf16, True),
            ((8, channels), f32, False),
        ],
        "norm",
        inner=inner,
        **statics,
    )
    everything = exchange(dsin.reshape(nq, piece, state), "seq").astype(f32)
    carried, reached = jnp.zeros((piece, state), f32), [None] * nq
    for i in reversed(range(nq)):
        reached[i] = carried.astype(bf16)
        carried = whole[i] * carried + everything[i]
    g_end = exchange(jnp.stack(reached), "seq").reshape(slots, channels, state)

    r_local, dbc = call(
        backward_kernel,
        slots,
        [(act, True), (dy, True), (lac, True), (lar, True), (dtr, True), (s_in, True)],
        [((slots, seg, channels), f32, True), ((slots, seg, 2 * state), f32, True)],
        "backward",
        flops=4 * slots * seg * seg * channels,
        **statics,
    )
    dpre, first, dstep, dbc, dtaps, drate = call(
        carry_kernel,
        slots,
        [
            (pc, True), (taps, False), (rate, False), (act, True), (dy, True), (r_local, True), (pos, True),
            (lac, True), (dtc, True), (g_end, True), (s_in, True), (s_local, True), (dbc, True), (vec, False),
        ],
        [
            ((slots, seg, channels), f32, True),
            ((slots, 8, channels), f32, True),
            ((slots, seg, lanes), bf16, True),
            ((slots, seg, 2 * state), f32, True),
            ((8, channels), f32, False),
            ((8, lanes), f32, False),
        ],
        "carry",
        **statics,
    )
    behind = [(i, i - 1) for i in range(1, nq)]
    after = lax.ppermute(first, "seq", behind)
    (dvalue,) = call(
        returned_kernel,
        slots,
        [(dpre, True), (after, True), (taps[:, :channels], False)],
        [((slots, seg, channels), bf16, True)],
        "returned",
    )

    mine = dbc.astype(bf16).reshape(slots, seg, nf, share)
    d_act = None
    for j in range(nf):
        part = lax.dynamic_index_in_dim(mine, me ^ j, 2, False)
        part = swap(part, "fsdp", j) if j else part
        part = jnp.stack([part[m ^ j] for m in range(slots)]).astype(f32)
        d_act = part if d_act is None else d_act + part
    xs = lax.dynamic_slice_in_dim(pc, channels + me * share, share, 2)[:, halo - 3 :].astype(f32)
    tapped = [xs[:, k : k + seg] for k in range(4)]
    pre = taps_share[4] + sum(tapped[k] * taps_share[k] for k in range(4))
    sg = sigmoid(pre)
    dpre_s = d_act * (sg * (1.0 + pre * (1.0 - sg)))
    dtaps_s = jnp.stack([jnp.sum(dpre_s * t, axis=(0, 1)) for t in tapped] + [jnp.sum(dpre_s, axis=(0, 1))])
    after_s = lax.ppermute(dpre_s[:, :3], "seq", behind)
    longer = jnp.concatenate([dpre_s, after_s], axis=1)
    dshare = sum(longer[:, 3 - k : 3 - k + seg] * taps_share[k] for k in range(4)).astype(bf16)
    dlast = jnp.concatenate([dshare, dstep[..., :heads]], axis=2)

    def grad_of(x, dz):
        return lax.dot_general(x, dz, (((0, 1), (0, 1)), ((), ())), preferred_element_type=f32)

    per = channels // rows
    block = jnp.concatenate(
        [
            dtaps[:5].T.reshape(per, rows, 5).transpose(1, 0, 2).reshape(rows, 5 * per),
            jnp.pad(dtaps_s.T, ((0, rows - share), (0, 0))),
            jnp.pad(
                jnp.stack([drate[0, :heads], drate[1, :heads], jnp.sum(dskip[0].reshape(heads, head_size), axis=1)], axis=1),
                ((0, rows - heads), (0, 0)),
            ),
        ],
        axis=1,
    )
    extra = block.shape[1]
    block = jnp.pad(block, ((0, 0), (0, lanes - share - heads - extra)))
    gw_last = jnp.concatenate([grad_of(main, dlast), jnp.tile(block, (nf, 1))], axis=1)

    def summed(g):
        g = g.astype(bf16).reshape(nf, nq, rows // nq, -1).transpose(1, 0, 2, 3).reshape(width, -1)
        g = lax.psum_scatter(g, "seq", scatter_dimension=0, tiled=True).reshape(nf, rows // nq, -1)
        g = exchange(g, "fsdp")
        g = lax.all_gather(g, "seq", axis=1)
        return g.reshape(nf, rows, -1)

    g_out = grad_of(gated_out, back_branch).astype(bf16)
    g_out = lax.psum_scatter(g_out, "seq", scatter_dimension=0, tiled=True)
    g_out = lax.all_gather(g_out, "seq", axis=0, tiled=True).astype(f32)
    s_gate = summed(grad_of(main, dgate)).astype(f32)
    s_value = summed(grad_of(main, dvalue)).astype(f32)
    s_last = summed(gw_last).astype(f32)

    def spread_columns(s):
        return s.transpose(1, 0, 2).reshape(rows, -1)

    g_in = jnp.concatenate(
        [
            spread_columns(s_gate),
            spread_columns(s_value),
            spread_columns(s_last[..., :share]),
            spread_columns(s_last[..., share : share + heads]),
        ],
        axis=1,
    )
    got = s_last[..., share + heads : share + heads + extra]
    tap_grads = jnp.concatenate(
        [
            got[..., : 5 * per].reshape(nf, rows, per, 5).transpose(0, 2, 1, 3).reshape(inner, 5),
            got[:, :share, 5 * per : 5 * per + 5].reshape(2 * state, 5),
        ],
        axis=0,
    )
    tap_grads = lax.dynamic_slice_in_dim(tap_grads, me * conv_own, conv_own, 0).T
    head_grads = lax.dynamic_index_in_dim(got, me, 0, False)[:heads, 5 * per + 5 :]

    norm_grad = jnp.sum(g_in * in_weight.astype(f32), axis=1) / norm_gain.astype(f32)
    gated_grad = jnp.sum(g_out * out_weight.astype(f32), axis=1) / gated_gain.astype(f32)

    branch = project(gated_out, out_weight)
    branch = to_owner([branch[j] for j in range(slots)], "fsdp")
    mixed = (valid * (inputs + branch)).astype(bf16)

    w_share = lax.dynamic_slice_in_dim(w_conv, channels + me * share, share, 1)
    w_last = jnp.concatenate([w_share, w_conv[:, cw : cw + heads]], axis=1)

    def back(dz, w):
        return lax.dot_general(dz, w, (((2,), (1,)), ((), ())), preferred_element_type=f32)

    bn = back(dgate, w_gate) + back(dvalue, w_conv[:, :channels]) + back(dlast, w_last)
    bn = to_owner([bn[j] for j in range(slots)], "fsdp") * norm_all
    lean = jnp.mean(bn * inputs, axis=-1, keepdims=True)
    input_grad = upstream + inv * bn - inputs * (inv * inv * inv) * lean
    return (
        mixed[None],
        input_grad[None],
        norm_grad,
        g_in,
        tap_grads[:4],
        tap_grads[4],
        head_grads[:, 0],
        head_grads[:, 1],
        head_grads[:, 2],
        gated_grad,
        g_out,
    )


def solution(mesh):
    whole, rows = P("fsdp", "seq", None), P("fsdp", None)
    one, columns = P("fsdp"), P(None, "fsdp")
    return jax.shard_map(
        per_device,
        mesh=mesh,
        in_specs=(whole, one, one, rows, columns, one, one, one, one, one, rows, whole),
        out_specs=(whole, whole, one, rows, columns, one, one, one, one, one, rows),
        check_vma=False,
    )
```

time: 1550 us -> 747 us (0.48)
  waiting for transfers between devices: 1090 us -> 317 us
  matrix products: 135 us -> 56.3 us
  Pallas kernels: 0 us -> 57.8 us
  starting transfers between devices: 5.75 us -> 61.8 us
  other arithmetic: 113 us -> 63.1 us
  blocking collectives: 95.7 us -> 80 us
    psum x1 -> x0, waiting for transfers between devices: 415 us -> none  [per_device(): lax.psum((shares[0], shares[1], shares[2], shares[3], shares[4], shares[5...]
    all_gather x4 -> x3, waiting for transfers between devices: 368 us -> 92.2 us  [the longest x2 89.7 us: summed(): g = lax.all_gather(g, 'seq', axis=1)]
    reduce_scatter x2 -> x4, waiting for transfers between devices: 303 us -> 107 us  [the longest x3 107 us: summed(): lax.psum_scatter(g, 'seq', scatter_dimension=0, tiled=True)]
    dot_general x18 -> x11, matrix products: 135 us -> 56.3 us  [the longest x3 19.1 us: project(): lax.dot_general(x, w, (((2,), (0,)), ((), ())), preferred_element_type=f32)]
    all_to_all x0 -> x10, waiting for transfers between devices: none -> 71.2 us  [exchange(): return lax.all_to_all(value, axis, 0, 0)]
    pallas_call x0 -> x6, Pallas kernels: none -> 57.8 us  [call(): pl.pallas_call(functools.partial(kernel, **statics), grid=(slots,), in_sp...]
    select_n x16 -> x0, other arithmetic: 56.7 us -> none  [lap(): return jax.tree.map(lambda a, b: jnp.where(reached, a, b), new, before)]
    all_to_all x0 -> x10, starting transfers between devices: none -> 45.3 us  [exchange(): return lax.all_to_all(value, axis, 0, 0)]
  transfers between devices with their start and end apart: 10 -> 37, of which waited for: 8 -> 19; matrix products, arithmetic and copies ran while one was open for 17% -> 17% of each run, Pallas kernels for 0% -> 6%
where the time goes in v1:
time: 747 us; the launch traced here: 737 us
  waiting for transfers between devices  317 us (42%)
  local copies, waits for them, and re-layouts  84.7 us (11%)
  blocking collectives  80 us (11%)
  other arithmetic  63.1 us (8%)
  starting transfers between devices  61.8 us (8%)
  Pallas kernels  57.8 us (8%)
  matrix products  56.3 us (8%)
  between operations  16.5 us (2%)
    reduce_scatter x3, waiting for transfers between devices, summed(): lax.psum_scatter(g, 'seq', scatter_dimension=0, tiled=True)  107 us
    all_gather x2, waiting for transfers between devices, summed(): g = lax.all_gather(g, 'seq', axis=1)  89.7 us
    all_to_all x10, waiting for transfers between devices, exchange(): return lax.all_to_all(value, axis, 0, 0)  71.2 us
    pallas_call x6, Pallas kernels, call(): pl.pallas_call(functools.partial(kernel, **statics), grid=(slots,), in_sp...  57.8 us
    all_to_all x10, starting transfers between devices, exchange(): return lax.all_to_all(value, axis, 0, 0)  45.3 us
    all_gather x1, blocking collectives, per_device(): norm_all = lax.all_gather(norm_gain, 'fsdp', axis=0, tiled=True).astype(f32)  42.6 us
    unnamed x152, local copies, waits for them, and re-layouts  34.7 us
    all_gather x1, blocking collectives, summed(): g = lax.all_gather(g, 'seq', axis=1)  32.2 us
  transfers between devices with their start and end apart: 37, of which 19 were waited for; matrix products, arithmetic and copies ran while one was open for 17% of the time, Pallas kernels for 6%

profile of v1, /device:TPU:0, one launch (start us, length us, event | category | flops | bytes accessed | tf_op | source)
XLA Modules:
  0.0 737.1 jit_solution(10048794436541219814)
XLA Ops:
  22.6 42.6 %all-gather.3 = bf16[4,1,384]{2,1,0:T(2,128)(2,1)S(1)} all-gather(bf16[1,1,384]{2,1,0:T(2,128)(2,1)S(1)} %reshape.630), channel_id=1, replica_groups=mesh['seq'=8,'fsdp'=4] {'fsdp'}, dimensions={0}, use_global_device_ids=true | all-gather | bytes 3840 | tf_op jit(solution)/shard_map/all_gather | solution.py:317
  72.9 19.5 %collective-permute-done.2 = bf16[1,272,1536]{2,1,0:T(8,128)(2,1)S(1)} collective-permute-done((bf16[1,272,1536]{2,1,0:T(8,128)(2,1)S(1)}, bf16[1,272,1536]{2,1,0:T(8,128)(2,1)S(1)}, u32[]{:S(2)}, u32[]{:S(2)}) %collective-permute-start.2) | collective-permute-done | bytes 835616 | tf_op jit(solution)/shard_map/ppermute | solution.py:261
  98.0 7.0 convolution_convert_fusion.pc_ref
  107.7 6.4 all-to-all-start.1
  115.7 12.9 %forward.1 = (bf16[4,256,1024]{2,1,0:T(8,128)(2,1)S(1)}, f32[4,256,768]{2,1,0:T(8,128)S(1)}, bf16[4,768,128]{2,1,0:T(8,128)(2,1)}, f32[4,256,128]{2,1,0:T(8,128)...) custom-call(bf16[4,272,1152]{2,1,0:T(8,128)(2,1)S(1)} %copy-done.4, ...), custom_call_target="tpu_custom_call" | custom-call | flops 402653184 | bytes 9752576 | tf_op jit(solution)/shard_map/forward/pallas_call | solution.py:247
  148.6 9.8 %all-to-all-done.2 = bf16[8,384,128]{2,1,0:T(8,128)(2,1)S(1)} async-done(((bf16[8,384,128]{2,1,0:T(8,128)(2,1)}), bf16[8,384,128]{2,1,0:T(8,128)(2,1)S(1)}, u32[]{:S(2)}, u32[]{:S(2)}) %all-to-all-start.2) | async-done | bytes 786464 | tf_op jit(solution)/shard_map/all_to_all | solution.py:299
  171.1 20.9 %all-to-all-done.4 = bf16[4,384,768]{2,1,0:T(8,128)(2,1)} async-done(((bf16[4,384,768]{2,1,0:T(8,128)(2,1)}), bf16[4,384,768]{2,1,0:T(8,128)(2,1)}, u32[]{:S(2)}, u32[]{:S(2)}) %all-to-all-start.4) | async-done | bytes 2359328 | tf_op jit(solution)/shard_map/all_to_all | solution.py:299
  195.8 7.0 fusion.12.bg_ref
  208.8 7.1 all-to-all-done.3
  233.5 9.0 %norm.1 = (bf16[4,256,768]{2,1,0:T(8,128)(2,1)S(1)}, bf16[4,256,768]{2,1,0:T(8,128)(2,1)S(1)}, f32[4,256,768]{2,1,0:T(8,128)S(1)}, f32[4,256,128]{2,1,0:T(8,128)...) custom-call(f32[4,256,768]{2,1,0:T(8,128)} %copy-done.9, ...), custom_call_target="tpu_custom_call" | custom-call | bytes 18169856 | tf_op jit(solution)/shard_map/norm/pallas_call | solution.py:247
  266.0 29.1 %all-to-all-done.5 = bf16[8,384,128]{2,1,0:T(8,128)(2,1)} async-done(((bf16[8,384,128]{2,1,0:T(8,128)(2,1)}), bf16[8,384,128]{2,1,0:T(8,128)(2,1)}, u32[]{:S(2)}, u32[]{:S(2)}) %all-to-all-start.5) | async-done | bytes 786464 | tf_op jit(solution)/shard_map/all_to_all | solution.py:299
  310.1 13.7 %backward.1 = (f32[4,256,768]{2,1,0:T(8,128)S(1)}, f32[4,256,256]{2,1,0:T(8,128)S(1)}) custom-call(bf16[4,256,1024]{2,1,0:T(8,128)(2,1)S(1)} %get-tuple-element.37.act_ref, f32[4,256,768]{2,1,0:T(8,128)S(1)} %copy-done.2, f32[4,256,128]{2,1,0:T(8,128)S(1)} %get-tuple-element.38.lac_ref, f32[4,16,256]{2,1,0:T(8,128)S(1)} %get-tuple-element.47.lar_ref, ...), custom_call_target="tpu_custom_call" | custom-call | flops 805306368 | bytes 10878976 | tf_op jit(solution)/shard_map/backward/pallas_call | solution.py:247
  332.2 15.3 %carry.1 = (f32[4,256,768]{2,1,0:T(8,128)S(1)}, f32[4,8,768]{2,1,0:T(8,128)S(1)}, bf16[4,256,128]{2,1,0:T(8,128)(2,1)S(1)}, f32[4,256,256]{2,1,0:T(8,128)S(1)}, ...) custom-call(bf16[4,272,1152]{2,1,0:T(8,128)(2,1)S(1)} %copy-done.5, f32[8,1024]{1,0:T(8,128)S(1)} %pad_maximum_fusion.9.taps_ref, ...), custom_call_target="tpu_custom_call" | custom-call | bytes 20520960 | tf_op jit(solution)/shard_map/carry/pallas_call | solution.py:247
  349.3 6.8 collective-permute-done.12.next_ref
  400.5 11.2 %reduce-scatter.5.cloned.1.call-done = bf16[192,768]{1,0:T(8,128)(2,1)} async-done(((bf16[1536,768]{1,0:T(8,128)(2,1)}), bf16[192,768]{1,0:T(8,128)(2,1)}) %reduce-scatter.5.cloned.1.call-update) | async-done | bytes 294928 | tf_op jit(solution)/shard_map/reduce_scatter | solution.py:493
  422.3 6.2 fusion.81
  435.6 6.3 fusion.80
  443.4 40.7 %reduce-scatter.7.cloned.1.call-done = bf16[192,768]{1,0:T(8,128)(2,1)} async-done(((bf16[1536,768]{1,0:T(8,128)(2,1)}), bf16[192,768]{1,0:T(8,128)(2,1)}) %reduce-scatter.7.cloned.1.call-update) | async-done | bytes 294928 | tf_op jit(solution)/shard_map/reduce_scatter | solution.py:493
  492.2 55.5 %reduce-scatter.9.cloned.1.call-done = bf16[192,128]{1,0:T(8,128)(2,1)} async-done(((bf16[1536,128]{1,0:T(8,128)(2,1)}), bf16[192,128]{1,0:T(8,128)(2,1)}) %reduce-scatter.9.cloned.1.call-update) | async-done | bytes 49168 | tf_op jit(solution)/shard_map/reduce_scatter | solution.py:493
  556.2 32.2 %all-gather.2 = bf16[4,384,128]{2,1,0:T(8,128)(2,1)S(1)} all-gather(bf16[4,48,128]{2,1,0:T(8,128)(2,1)S(1)} %all-to-all-done.9), channel_id=4, replica_groups=mesh['seq'=8,'fsdp'=4] {'seq'}, dimensions={1}, use_global_device_ids=true | all-gather | bytes 442368 | tf_op jit(solution)/shard_map/all_gather | solution.py:495
  608.2 47.3 %all-gather.11.cloned.1.call-done = bf16[4,384,768]{2,1,0:T(8,128)(2,1)} async-done(((bf16[4,48,768]{2,1,0:T(8,128)(2,1)}), bf16[4,384,768]{2,1,0:T(8,128)(2,1)}) %all-gather.11.cloned.1.call-update) | async-done | bytes 2359312 | tf_op jit(solution)/shard_map/all_gather | solution.py:495
  665.9 42.4 %all-gather.13.cloned.1.call-done = bf16[4,384,768]{2,1,0:T(8,128)(2,1)} async-done(((bf16[4,48,768]{2,1,0:T(8,128)(2,1)}), bf16[4,384,768]{2,1,0:T(8,128)(2,1)}) %all-gather.13.cloned.1.call-update) | async-done | bytes 2359312 | tf_op jit(solution)/shard_map/all_gather | solution.py:495
  712.5 6.1 copy.139
  718.6 10.6 %multiply_reduce_fusion = (f32[384]{0:T(512)S(1)}, f32[384,6448]{0,1:T(8,128)}) fusion(bf16[384,6448]{0,1:T(8,128)(2,1)} %param.15, f32[384,48]{0,1:T(8,128)S(1)} %reshape.600, f32[384,256]{0,1:T(8,128)S(1)} %bitcast.231, f32[384,3072]{0,1:T(8,128)} %bitcast.219, f32[384,3072]{0,1:T(8,128)} %bitcast.218), kind=kLoop, calls=%fused_computation.1 | loop fusion | flops 14855808 | bytes 24761856 | tf_op jit(solution)/shard_map/reduce_sum | solution.py:528
  (359 shorter events, 255.2 us)
Async XLA Ops:
  17.6 80.4 %all-to-all-start = ((bf16[4,384,1152]{2,1,0:T(8,128)(2,1)}), bf16[4,384,1152]{2,1,0:T(8,128)(2,1)}, u32[]{:S(2)}, u32[]{:S(2)}) async-start(bf16[4,384,1152]{2,1,0:T(8,128)(2,1)} %fusion.2), calls=%async_computation | async-start | bytes 7077888 | tf_op jit(solution)/shard_map/all_to_all | solution.py:299
  72.8 25.1 %collective-permute-start.1 = (bf16[1,272,1536]{2,1,0:T(8,128)(2,1)S(1)}, bf16[1,272,1536]{2,1,0:T(8,128)(2,1)}, u32[]{:S(2)}, u32[]{:S(2)}) collective-permute-start(bf16[1,272,1536]{2,1,0:T(8,128)(2,1)S(1)} %maximum_bitcast_fusion), channel_id=1, source_target_pairs={{0,1},{1,0},{2,3},{3,2},{4,5},{5,4},{6,7},{7,6},{8,9},{9,8},{10,11... | collective-permute-start | bytes 2506760 | tf_op jit(solution)/shard_map/ppermute | solution.py:261
  107.7 24.0 %all-to-all-start.1 = ((f32[8,1,384]{2,1,0:T(1,128)}), f32[8,1,384]{2,1,0:T(1,128)S(1)}, u32[]{:S(2)}, u32[]{:S(2)}) async-start(f32[8,1,384]{2,1,0:T(1,128)} %all_to_all.44), calls=%async_computation.1 | async-start | bytes 24576 | tf_op jit(solution)/shard_map/all_to_all | solution.py:299
  132.3 26.2 %all-to-all-start.2 = ((bf16[8,384,128]{2,1,0:T(8,128)(2,1)}), bf16[8,384,128]{2,1,0:T(8,128)(2,1)S(1)}, u32[]{:S(2)}, u32[]{:S(2)}) async-start(bf16[8,384,128]{2,1,0:T(8,128)(2,1)} %bitcast.15), calls=%async_computation.2 | async-start | bytes 1572864 | tf_op jit(solution)/shard_map/all_to_all | solution.py:299
  148.6 47.2 %collective-permute-start.4 = (bf16[1,256,1536]{2,1,0:T(8,128)(2,1)}, bf16[1,256,1536]{2,1,0:T(8,128)(2,1)}, u32[]{:S(2)}, u32[]{:S(2)}) collective-permute-start(bf16[1,256,1536]{2,1,0:T(8,128)(2,1)} %bitcast.22), channel_id=1, source_target_pairs={{0,1},{1,0},{2,3},{3,2},{4,5},{5,4},{6,7},{7,6},{8,9},{9,8},{10,11... | collective-permute-start | bytes 2359304 | tf_op jit(solution)/shard_map/ppermute | solution.py:261
  158.5 33.5 %all-to-all-start.4 = ((bf16[4,384,768]{2,1,0:T(8,128)(2,1)}), bf16[4,384,768]{2,1,0:T(8,128)(2,1)}, u32[]{:S(2)}, u32[]{:S(2)}) async-start(bf16[4,384,768]{2,1,0:T(8,128)(2,1)} %bitcast.222), calls=%async_computation.4 | async-start | bytes 4718592 | tf_op jit(solution)/shard_map/all_to_all | solution.py:299
  164.9 30.9 %collective-permute-start.6 = (bf16[1,256,1536]{2,1,0:T(8,128)(2,1)}, bf16[1,256,1536]{2,1,0:T(8,128)(2,1)}, u32[]{:S(2)}, u32[]{:S(2)}) collective-permute-start(bf16[1,256,1536]{2,1,0:T(8,128)(2,1)} %collective-permute-done.5), channel_id=1, source_target_pairs={{0,1},{1,0},{2,3},{3,2},{4,5},{5,4},{6,7},{7,6},{8,9},{9,8},{10,11... | collective-permute-start | bytes 2359304 | tf_op jit(solution)/shard_map/ppermute | solution.py:261
  192.0 23.9 %all-to-all-start.3 = ((bf16[8,384,128]{2,1,0:T(8,128)(2,1)}), bf16[8,384,128]{2,1,0:T(8,128)(2,1)S(1)}, u32[]{:S(2)}, u32[]{:S(2)}) async-start(bf16[8,384,128]{2,1,0:T(8,128)(2,1)} %fusion.55), calls=%async_computation.3 | async-start | bytes 1572864 | tf_op jit(solution)/shard_map/all_to_all | solution.py:299
  195.7 202.5 %reduce-scatter.11.cloned.1.call-start = ((), (), s32[]{:S(2)}) async-start(), calls=%async_computation.17 | async-start | bytes 2654208 | tf_op jit(solution)/shard_map/reduce_scatter | solution.py:499
  254.7 40.4 %all-to-all-start.5 = ((bf16[8,384,128]{2,1,0:T(8,128)(2,1)}), bf16[8,384,128]{2,1,0:T(8,128)(2,1)}, u32[]{:S(2)}, u32[]{:S(2)}) async-start(bf16[8,384,128]{2,1,0:T(8,128)(2,1)} %bitcast.215), calls=%async_computation.5 | async-start | bytes 1572864 | tf_op jit(solution)/shard_map/all_to_all | solution.py:299
  259.0 152.8 %reduce-scatter.5.cloned.1.call-start = ((), (), s32[]{:S(2)}) async-start(), calls=%async_computation.14 | async-start | bytes 2654208 | tf_op jit(solution)/shard_map/reduce_scatter | solution.py:493
  303.1 23.4 %all-to-all-start.6 = ((bf16[8,384,128]{2,1,0:T(8,128)(2,1)}), bf16[8,384,128]{2,1,0:T(8,128)(2,1)}, u32[]{:S(2)}, u32[]{:S(2)}) async-start(bf16[8,384,128]{2,1,0:T(8,128)(2,1)} %broadcast_dynamic-update-slice_fusion), calls=%async_computation.6 | async-start | bytes 1572864 | tf_op jit(solution)/shard_map/all_to_all | solution.py:299
  307.3 176.8 %reduce-scatter.7.cloned.1.call-start = ((), (), s32[]{:S(2)}) async-start(), calls=%async_computation.15 | async-start | bytes 2654208 | tf_op jit(solution)/shard_map/reduce_scatter | solution.py:493
  363.3 184.3 %reduce-scatter.9.cloned.1.call-start = ((), (), s32[]{:S(2)}) async-start(), calls=%async_computation.16 | async-start | bytes 442368 | tf_op jit(solution)/shard_map/reduce_scatter | solution.py:493
  398.1 204.3 %all-gather.9.cloned.1.call-start = ((), (), s32[]{:S(2)}) async-start(), calls=%async_computation.18 | async-start | bytes 2654208 | tf_op jit(solution)/shard_map/all_gather | solution.py:500
  415.8 239.7 %all-gather.11.cloned.1.call-start = ((), (), s32[]{:S(2)}) async-start(), calls=%async_computation.19 | async-start | bytes 2654208 | tf_op jit(solution)/shard_map/all_gather | solution.py:495
  429.4 58.1 %collective-permute-start.10 = (bf16[256,1536]{1,0:T(8,128)(2,1)S(1)}, bf16[256,1536]{1,0:T(8,128)(2,1)}, u32[]{:S(2)}, u32[]{:S(2)}) collective-permute-start(bf16[256,1536]{1,0:T(8,128)(2,1)S(1)} %get-tuple-element.94), channel_id=1, source_target_pairs={{0,1},{1,0},{2,3},{3,2},{4,5},{5,4},{6,7},{7,6},{8,9},{9,8},{10,11... | collective-permute-start | bytes 2359304 | tf_op jit(solution)/shard_map/ppermute | solution.py:261
  442.8 108.9 %collective-permute-start.18 = (bf16[256,1536]{1,0:T(8,128)(2,1)S(1)}, bf16[256,1536]{1,0:T(8,128)(2,1)S(1)}, u32[]{:S(2)}, u32[]{:S(2)}) collective-permute-start(bf16[256,1536]{1,0:T(8,128)(2,1)S(1)} %get-tuple-element.92), channel_id=1, source_target_pairs={{0,1},{1,0},{2,3},{3,2},{4,5},{5,4},{6,7},{7,6},{8,9},{9,8},{10,11... | collective-permute-start | bytes 2359304 | tf_op jit(solution)/shard_map/ppermute | solution.py:261
  442.8 151.8 %collective-permute-start.9 = (bf16[256,1536]{1,0:T(8,128)(2,1)}, bf16[256,1536]{1,0:T(8,128)(2,1)}, u32[]{:S(2)}, u32[]{:S(2)}) collective-permute-start(bf16[256,1536]{1,0:T(8,128)(2,1)} %get-tuple-element.93), channel_id=1, source_target_pairs={{0,1},{1,0},{2,3},{3,2},{4,5},{5,4},{6,7},{7,6},{8,9},{9,8},{10,11... | collective-permute-start | bytes 2359304 | tf_op jit(solution)/shard_map/ppermute | solution.py:261
  484.1 63.6 %all-to-all-start.8 = ((bf16[4,48,768]{2,1,0:T(8,128)(2,1)}), bf16[4,48,768]{2,1,0:T(8,128)(2,1)S(1)}, u32[]{:S(2)}, u32[]{:S(2)}) async-start(bf16[4,48,768]{2,1,0:T(8,128)(2,1)} %bitcast.235), calls=%async_computation.10 | async-start | bytes 589824 | tf_op jit(solution)/shard_map/all_to_all | solution.py:299
  490.2 104.4 %collective-permute-start.11 = (bf16[256,1536]{1,0:T(8,128)(2,1)}, bf16[256,1536]{1,0:T(8,128)(2,1)}, u32[]{:S(2)}, u32[]{:S(2)}) collective-permute-start(bf16[256,1536]{1,0:T(8,128)(2,1)} %fusion.30), channel_id=1, source_target_pairs={{0,2},{1,3},{2,0},{3,1},{4,6},{5,7},{6,4},{7,5},{8,10},{9,11},{10,... | collective-permute-start | bytes 2359304 | tf_op jit(solution)/shard_map/ppermute | solution.py:261
  492.2 100.0 %collective-permute-start.17 = (bf16[256,1536]{1,0:T(8,128)(2,1)}, bf16[256,1536]{1,0:T(8,128)(2,1)}, u32[]{:S(2)}, u32[]{:S(2)}) collective-permute-start(bf16[256,1536]{1,0:T(8,128)(2,1)} %get-tuple-element.91), channel_id=1, source_target_pairs={{0,1},{1,0},{2,3},{3,2},{4,5},{5,4},{6,7},{7,6},{8,9},{9,8},{10,11... | collective-permute-start | bytes 2359304 | tf_op jit(solution)/shard_map/ppermute | solution.py:261
  551.0 157.3 %all-gather.13.cloned.1.call-start = ((), (), s32[]{:S(2)}) async-start(), calls=%async_computation.20 | async-start | bytes 2654208 | tf_op jit(solution)/shard_map/all_gather | solution.py:495
  554.2 38.0 %collective-permute-start.19 = (bf16[256,1536]{1,0:T(8,128)(2,1)}, bf16[256,1536]{1,0:T(8,128)(2,1)}, u32[]{:S(2)}, u32[]{:S(2)}) collective-permute-start(bf16[256,1536]{1,0:T(8,128)(2,1)} %fusion.25), channel_id=1, source_target_pairs={{0,2},{1,3},{2,0},{3,1},{4,6},{5,7},{6,4},{7,5},{8,10},{9,11},{10,... | collective-permute-start | bytes 2359304 | tf_op jit(solution)/shard_map/ppermute | solution.py:261
  (87 other events, 777.8 us)
Sparse Core Ops, SparseCore 0:
  254.8 85.3 reduce-scatter.10
  343.7 67.9 reduce-scatter.4
  415.8 68.2 reduce-scatter.6
  487.2 60.4 reduce-scatter.8
  549.7 52.7 all-gather.8
  604.5 50.9 all-gather.10
  657.7 50.4 all-gather.12

commit v2 on v1

--- a/solution.py
+++ b/solution.py
@@ -39,8 +39,19 @@
     )
 
 
-def of_heads(pair):
-    return (iota((lanes, lanes), 1) == 2 * pair + iota((lanes, lanes), 0) // head_size).astype(f32)
+def per_head(total, products, pair):
+    rows = products.shape[0]
+    lane = iota((rows, lanes), 1)
+    low = jnp.sum(jnp.where(lane < head_size, products, 0.0), axis=1, keepdims=True)
+    high = jnp.sum(jnp.where(lane < head_size, 0.0, products), axis=1, keepdims=True)
+    return total + jnp.where(lane == 2 * pair, low, jnp.where(lane == 2 * pair + 1, high, 0.0))
+
+
+def in_heads(products, pair):
+    rows = jnp.sum(products, axis=1, keepdims=True)
+    low, high = jnp.sum(rows[:head_size]), jnp.sum(rows[head_size:])
+    lane = iota((1, lanes), 1)
+    return jnp.where(lane == 2 * pair, low, jnp.where(lane == 2 * pair + 1, high, 0.0))
 
 
 def convolved(pc_ref, taps_ref, at):
@@ -52,7 +63,59 @@
     return tapped, pre
 
 
-def forward_kernel(pc_ref, taps_ref, rate_ref, act_ref, y_ref, s_ref, lac_ref, dtc_ref, lar_ref, dtr_ref, *, channels, state):
+def pieces_out(ids_ref, out_ref, whole, rows):
+    count = out_ref.shape[0]
+    for p in range(count):
+        out_ref[p ^ (ids_ref[0] % count), :rows] = whole[p * rows : (p + 1) * rows]
+
+
+def pieces_in(ids_ref, ref, rows):
+    count = ref.shape[0]
+    return jnp.concatenate([ref[p ^ (ids_ref[0] % count), :rows] for p in range(count)], axis=0)
+
+
+def normalize_kernel(main_ref, small_ref, gain_ref, out_ref):
+    for ref, at in ((small_ref, 0), (main_ref, halo)):
+        x = ref[0].astype(f32)
+        inv = lax.rsqrt(jnp.mean(x * x, axis=1, keepdims=True) + epsilon)
+        out_ref[0, at : at + x.shape[0]] = (x * inv * gain_ref[...]).astype(bf16)
+
+
+def of_rows(row, ids_ref, rows, count):
+    head = ((ids_ref[0] % count) * rows + iota((rows, lanes), 0)) // head_size
+    return jnp.sum(jnp.where(iota((rows, lanes), 1) == head, row, 0.0), axis=1, keepdims=True)
+
+
+def chain_kernel(ids_ref, *refs, rows, count):
+    n = (len(refs) - 3) // 1
+    ins, out_ref, decay_ref, hold = refs[:n], refs[n], refs[n + 1], refs[n + 2]
+    for j in range(n):
+        hold[ids_ref[0] ^ j] = ins[j][...]
+    carried = jnp.zeros((rows, lanes), f32)
+    for i in range(n):
+        out_ref[ids_ref[0] ^ i] = carried.astype(bf16)
+        row = hold[i, rows : rows + 1].astype(f32) + hold[i, rows + 1 : rows + 2].astype(f32)
+        decay_ref[i] = jnp.broadcast_to(row, (8, lanes))
+        carried = of_rows(row, ids_ref, rows, count) * carried + hold[i, :rows].astype(f32)
+
+
+def back_chain_kernel(ids_ref, *refs, rows, count):
+    n = len(refs) - 3
+    ins, decay_ref, out_ref, hold = refs[:n], refs[n], refs[n + 1], refs[n + 2]
+    for j in range(n):
+        hold[ids_ref[0] ^ j] = ins[j][...]
+    carried = jnp.zeros((rows, lanes), f32)
+    for i in reversed(range(n)):
+        out_ref[ids_ref[0] ^ i] = carried.astype(bf16)
+        carried = of_rows(decay_ref[i, :1], ids_ref, rows, count) * carried + hold[i].astype(f32)
+
+
+def order_kernel(ids_ref, *refs):
+    for j in range(len(refs) - 1):
+        refs[-1][ids_ref[0] ^ j] = refs[j][...]
+
+
+def forward_kernel(ids_ref, pc_ref, taps_ref, rate_ref, act_ref, y_ref, s_ref, lac_ref, dtc_ref, lar_ref, dtr_ref, *, channels, state, rows):
     width = channels + 2 * state
     for at in range(0, width, lanes):
         _, pre = convolved(pc_ref, taps_ref, at)
@@ -62,13 +125,14 @@
     dtc = jnp.maximum(z, 0.0) + jnp.log1p(jnp.exp(-jnp.abs(z)))
     lower = iota((seg, seg), 0) >= iota((seg, seg), 1)
     lac = dot(lower.astype(f32), -dtc * rate_ref[1:2], precision=best)
-    rows = lar_ref.shape[1]
-    lar, dtr = lac.T[:rows], dtc.T[:rows]
+    tall = lar_ref.shape[1]
+    lar, dtr = lac.T[:tall], dtc.T[:tall]
     lac_ref[0], dtc_ref[0], lar_ref[0], dtr_ref[0] = lac, dtc, lar, dtr
     b_rows = act_ref[0, :, channels : channels + state]
     c_rows = act_ref[0, :, channels + state : width]
     both = dot(c_rows, b_rows, 1, 1)
     to_end = jnp.exp(lac[seg - 1 : seg] - lac) * dtc
+    states = []
     for pair in range(channels // lanes):
         at = pair * lanes
         values = act_ref[0, :, at : at + lanes]
@@ -79,7 +143,14 @@
             parts.append(dot(mix.astype(bf16), values[:, side * head_size : (side + 1) * head_size]))
         y_ref[0, :, at : at + lanes] = jnp.concatenate(parts, axis=1)
         weighted = (spread(to_end, pair) * values.astype(f32)).astype(bf16)
-        s_ref[0, at : at + lanes] = dot(weighted, b_rows, 0, 0).astype(bf16)
+        states.append(dot(weighted, b_rows, 0, 0).astype(bf16))
+    pieces_out(ids_ref, s_ref, jnp.concatenate(states, axis=0), rows)
+    whole = jnp.exp(lac[seg - 1 : seg])
+    high = whole.astype(bf16).astype(f32)
+    row = iota((16, lanes), 0)
+    tail = jnp.where(row == 0, high, jnp.where(row == 1, whole - high, 0.0)).astype(bf16)
+    for p in range(s_ref.shape[0]):
+        s_ref[p, rows:] = tail
 
 
 def finish_kernel(y_ref, act_ref, lac_ref, sin_ref, gate_ref, bg_ref, vec_ref, y_out, stat_ref, *, channels, state):
@@ -104,9 +175,11 @@
     stat_ref[0] = both.T[:8]
 
 
-def norm_kernel(y_ref, act_ref, lac_ref, gate_ref, bg_ref, vec_ref, stat_ref, out_ref, dgate_ref, dy_ref, pos_ref, dsin_ref, dskip_ref, *, channels, state, inner):
+def norm_kernel(ids_ref, y_ref, act_ref, lac_ref, gate_ref, bg_ref, vec_ref, *refs, channels, state, inner, rows):
+    stat_refs, (out_ref, dgate_ref, dy_ref, pos_ref, dsin_ref, dskip_ref) = refs[:-6], refs[-6:]
     seg = y_ref.shape[1]
-    stats = stat_ref[0].T
+    stats = sum(ref[0] for ref in stat_refs).T
+    states = []
     inv = lax.rsqrt(stats[:, 0:1] * (1.0 / inner) + epsilon)
     lean = inv * inv * inv * (stats[:, 1:2] * (1.0 / inner))
     c_rows = act_ref[0, :, channels + state : channels + 2 * state]
@@ -132,10 +205,11 @@
         dgate_ref[0, :, here] = (dgated * heads * (sg * (1.0 + gate * (1.0 - sg)))).astype(bf16)
         dy = dgated * gate * sg
         dy_ref[0, :, here] = dy
-        pos = pos + dot(dy * y, of_heads(pair), precision=best)
-        dsin_ref[0, here] = dot((spread(decay, pair) * dy).astype(bf16), c_rows, 0, 0).astype(bf16)
+        pos = per_head(pos, dy * y, pair)
+        states.append(dot((spread(decay, pair) * dy).astype(bf16), c_rows, 0, 0).astype(bf16))
         dskip_ref[0:1, here] += jnp.sum(dy * values, axis=0, keepdims=True)
     pos_ref[0] = pos
+    pieces_out(ids_ref, dsin_ref, jnp.concatenate(states, axis=0), rows)
 
 
 def backward_kernel(act_ref, dy_ref, lac_ref, lar_ref, dtr_ref, sin_ref, r_ref, dbc_ref, *, channels, state):
@@ -168,7 +242,7 @@
     dbc_ref[0, :, state:] = dc + dot(dlow, b_rows)
 
 
-def carry_kernel(pc_ref, taps_ref, rate_ref, act_ref, dy_ref, r_ref, pos_ref, lac_ref, dtc_ref, g_ref, sin_ref, s_ref, dbc_ref, vec_ref, dpre_ref, first_ref, dstep_ref, dbc_out, dtaps_ref, drate_ref, *, channels, state):
+def carry_kernel(ids_ref, pc_ref, taps_ref, rate_ref, act_ref, dy_ref, r_ref, pos_ref, lac_ref, dtc_ref, g_ref, sin_ref, s_ref, dbc_ref, vec_ref, dpre_ref, first_ref, dstep_ref, dbc_out, dtaps_ref, drate_ref, *, channels, state, rows):
     seg = dy_ref.shape[1]
     width = channels + 2 * state
     b_rows = act_ref[0, :, channels : channels + state]
@@ -179,6 +253,7 @@
     db = jnp.zeros((seg, state), f32)
     through = jnp.zeros((1, lanes), f32)
     local = jnp.zeros((1, lanes), f32)
+    states = pieces_in(ids_ref, s_ref, rows)
 
     @pl.when(pl.program_id(0) == 0)
     def _():
@@ -193,12 +268,11 @@
         reach = spread(to_last, pair)
         step = spread(dtc, pair)
         r = r_ref[0, :, here] + reach * dot(b_rows, grad, 1, 1)
-        owners = of_heads(pair)
-        neg = neg + dot(values * r, owners, precision=best)
+        neg = per_head(neg, values * r, pair)
         db = db + dot((reach * step * values).astype(bf16), grad)
         wide = grad.astype(f32)
-        through = through + jnp.sum(dot(wide * sin_ref[0, here].astype(f32), owners, 0, 0, best), axis=0, keepdims=True)
-        local = local + jnp.sum(dot(wide * s_ref[0, here].astype(f32), owners, 0, 0, best), axis=0, keepdims=True)
+        through = through + in_heads(wide * sin_ref[0, here].astype(f32), pair)
+        local = local + in_heads(wide * states[here].astype(f32), pair)
         tapped, pre = convolved(pc_ref, taps_ref, at)
         sg = sigmoid(pre)
         dpre = (step * r + vec_ref[0:1, here] * dy_ref[0, :, here]) * (sg * (1.0 + pre * (1.0 - sg)))
@@ -232,11 +306,14 @@
         out_ref[0, :, here] = total.astype(bf16)
 
 
-def call(kernel, slots, ins, outs, name, flops=0, **statics):
-    def spec(shape, per):
-        if per:
-            return pl.BlockSpec((1,) + tuple(shape[1:]), lambda s: (s,) + (0,) * (len(shape) - 1))
-        return pl.BlockSpec(tuple(shape), lambda s: (0,) * len(shape))
+def call(kernel, grid, ins, outs, name, ids=None, flops=0, scratch=(), **statics):
+    def spec(shape, index):
+        if index == "rows":
+            return pl.BlockSpec((shape[0], shape[1] // grid, shape[2]), lambda s, *i: (0, s, 0))
+        if index is None:
+            return pl.BlockSpec(tuple(shape), lambda s, *i: (0,) * len(shape))
+        block, at = index
+        return pl.BlockSpec((block,) + tuple(shape[1:]), lambda s, *i: (at(s, *i),) + (0,) * (len(shape) - 1))
 
     moved = sum(a.size * a.dtype.itemsize for a, _ in ins)
     for shape, dtype, _ in outs:
@@ -246,14 +323,21 @@
         moved += size * jnp.dtype(dtype).itemsize
     return pl.pallas_call(
         functools.partial(kernel, **statics),
-        grid=(slots,),
-        in_specs=[spec(a.shape, per) for a, per in ins],
-        out_specs=[spec(shape, per) for shape, _, per in outs],
+        grid_spec=pltpu.PrefetchScalarGridSpec(
+            num_scalar_prefetch=0 if ids is None else 1,
+            grid=(grid,),
+            in_specs=[spec(a.shape, index) for a, index in ins],
+            out_specs=[spec(shape, index) for shape, _, index in outs],
+            scratch_shapes=list(scratch),
+        ),
         out_shape=[jax.ShapeDtypeStruct(shape, dtype) for shape, dtype, _ in outs],
-        compiler_params=pltpu.CompilerParams(vmem_limit_bytes=40 << 20),
+        compiler_params=pltpu.CompilerParams(vmem_limit_bytes=24 << 20),
         cost_estimate=pl.CostEstimate(flops=flops, bytes_accessed=moved, transcendentals=0),
         name=name,
-    )(*[a for a, _ in ins])
+    )(*([] if ids is None else [ids]), *[a for a, _ in ins])
+
+
+each = (1, lambda s, *i: s)
 
 
 def swap(value, axis, by):
@@ -286,17 +370,100 @@
     return parts[0]
 
 
-def over_owners(value, axis):
-    count, by = lax.axis_size(axis), 1
+def scatter_sum(value, axis, at):
+    count, place, by = lax.axis_size(axis), lax.axis_index(axis), 1
     while by < count:
-        other = swap(value, axis, by)
-        value = value + jnp.stack([other[j ^ by] for j in range(count)])
+        shape = value.shape
+        value = value.reshape(shape[:at] + (shape[at] // 2, 2) + shape[at + 1 :])
+        bit = (place // by) % 2
+        keep = lax.dynamic_index_in_dim(value, bit, at + 1, False)
+        give = lax.dynamic_index_in_dim(value, 1 - bit, at + 1, False)
+        value = (keep.astype(f32) + swap(give, axis, by).astype(f32)).astype(bf16)
         by *= 2
+    return jnp.squeeze(value, at)
+
+
+def gathered(piece, axis):
+    value, by = piece[None], lax.axis_size(axis) // 2
+    while by:
+        value = jnp.concatenate([value, swap(value, axis, by)], axis=0)
+        by //= 2
     return value
 
 
-def exchange(value, axis):
-    return lax.all_to_all(value, axis, 0, 0)
+def reversed_bits(j, count):
+    out, by = 0, 1
+    while by < count:
+        out = out * 2 + (j // by) % 2
+        by *= 2
+    return out
+
+
+def traded(value, axis):
+    count, me = lax.axis_size(axis), lax.axis_index(axis)
+    parts = [lax.dynamic_index_in_dim(value, me ^ j, 0, False) for j in range(count)]
+    return jnp.stack([swap(part, axis, j) if j else part for j, part in enumerate(parts)])
+
+
+def sent(value, axis):
+    return [swap(value[j], axis, j) if j else value[0] for j in range(lax.axis_size(axis))]
+
+
+def in_order(parts, index):
+    stacked = jnp.stack(parts)
+    return jnp.concatenate([lax.dynamic_index_in_dim(stacked, index ^ a, 0) for a in range(len(parts))])
+
+
+def rows_in_order(parts, index):
+    total = sum(part.shape[0] for part, _ in parts)
+    out = jnp.zeros((total,) + parts[0][0].shape[1:], parts[0][0].dtype)
+    for part, start in parts:
+        out = lax.dynamic_update_slice_in_dim(out, part, start, 0)
+    return out
+
+
+def assemble_kernel(ids_ref, *refs, parts, share, heads, inner):
+    bufs, (last_ref, weight_ref, out_ref, tail_ref, sum_ref) = refs[: len(parts)], refs[len(parts) :]
+    owners = last_ref.shape[1]
+    rows = out_ref.shape[0]
+    total = jnp.zeros((rows, 1), f32)
+
+    def put(at, value):
+        size = value.shape[1]
+        out_ref[:, at : at + size] = value
+        return jnp.sum(value * weight_ref[:, at : at + size].astype(f32), axis=1, keepdims=True)
+
+    for a in range(owners):
+        for ref, (start, step) in zip(bufs, parts, strict=True):
+            total = total + put(start + a * step, ref[0, ids_ref[1] ^ a].astype(f32))
+    lane = iota((rows, lanes), 1)
+    lasts = [last_ref[0, ids_ref[1] ^ a].astype(f32) for a in range(owners)]
+    for a in range(owners):
+        tail_ref[a] = lasts[a]
+    group = lanes // share
+    for block in range(owners // group):
+        value = jnp.zeros((rows, lanes), f32)
+        for b in range(group):
+            moved = lasts[block * group + b]
+            moved = pltpu.roll(moved, b * share, 1) if b else moved
+            value = jnp.where(lane // share == b, moved, value)
+        total = total + put(2 * inner + block * lanes, value)
+    value = jnp.zeros((rows, lanes), f32)
+    for a in range(owners):
+        moved = pltpu.roll(lasts[a], (a * heads - share) % lanes, 1)
+        value = jnp.where(lane // heads == a, moved, value)
+    total = total + put(2 * inner + owners * share, value[:, : owners * heads])
+    sum_ref[...] = total
+
+
+def rows_kernel(ids_ref, *refs, parts):
+    bufs, (weight_ref, out_ref, sum_ref) = refs[: len(parts)], refs[len(parts) :]
+    total = jnp.zeros((out_ref.shape[0], 1), f32)
+    for ref, (start, size) in zip(bufs, parts, strict=True):
+        value = ref[0].astype(f32)
+        out_ref[:, start : start + size] = value
+        total = total + jnp.sum(value * weight_ref[:, start : start + size].astype(f32), axis=1, keepdims=True)
+    sum_ref[...] = total
 
 
 def per_device(tokens, lengths, norm_gain, in_weight, conv_weight, conv_bias, dt_bias, decay_log, skip_gain, gated_gain, out_weight, cotangent):
@@ -312,10 +479,25 @@
     share = 2 * state // nf
     slots = nf
 
-    small = jnp.concatenate([conv_weight, conv_bias[None]], axis=0)
-    small = jnp.pad(small, ((0, 3), (0, 0)))
-    norm_all = lax.all_gather(norm_gain, "fsdp", axis=0, tiled=True).astype(f32)
-    taps_all = lax.all_gather(small, "fsdp", axis=1, tiled=True).astype(f32)
+    ids = jnp.stack([place, me]).astype(jnp.int32)
+    per_slot = nq // slots
+    piece = channels // per_slot
+
+    x_main = all_slots(tokens, "fsdp")
+    before = lax.ppermute(tokens[0, seg - 3 :], "seq", [(i, i + 1) for i in range(nq - 1)])
+
+    def padded(rows_):
+        return jnp.pad(rows_, ((0, 0), (0, width - rows_.shape[1])))
+
+    small = jnp.concatenate(
+        [padded(conv_weight), padded(conv_bias[None]), padded(norm_gain[None]), jnp.zeros((7, width), bf16), before], axis=0
+    )
+    x_small = all_slots(small[None], "fsdp")
+    listed = [x_small[j] for j in range(nf)]
+    norm_all = in_order([part[5, :rows] for part in listed], me).astype(f32).reshape(1, width)
+    taps_all = in_order([part[:5, :conv_own] for part in listed], me).astype(f32)
+    taps_all = taps_all.reshape(nf, 5, conv_own).transpose(1, 0, 2).reshape(5, -1)
+    taps_all = jnp.pad(taps_all, ((0, 3), (0, 0)))
     taps = jnp.concatenate([lax.dynamic_slice_in_dim(taps_all, me * channels, channels, 1), taps_all[:, inner:]], axis=1)
     taps_share = lax.dynamic_slice_in_dim(taps_all, inner + me * share, share, 1)
     rate = jnp.stack([dt_bias.astype(f32), jnp.exp(decay_log.astype(f32))])
@@ -323,23 +505,41 @@
     vec = jnp.stack([jnp.repeat(skip_gain.astype(f32), head_size), gated_gain.astype(f32)])
     vec = jnp.pad(vec, ((0, 6), (0, 0)))
 
-    w_value = in_weight[:, inner : 2 * inner].reshape(rows, nf, channels)
-    w_rows = jnp.broadcast_to(in_weight[:, 2 * inner : 2 * inner + 2 * state][:, None], (rows, nf, 2 * state))
-    w_step = jnp.pad(in_weight[:, 2 * inner + 2 * state :].reshape(rows, nf, heads), ((0, 0), (0, 0), (0, lanes - heads)))
-    w_conv = jnp.concatenate([w_value, w_rows, w_step], axis=2).transpose(1, 0, 2)
-    w_conv = exchange(w_conv, "fsdp").reshape(width, -1)
-
+    half, side = rows // 2, place % 2
+    gives = [lax.dynamic_slice_in_dim(in_weight, inner + (me ^ j) * channels, channels, 1) for j in range(nf)]
+    got = [(gives[0], me * rows)]
+    for j in range(nf - 1, 0, -1):
+        start = (me ^ j) * rows
+        if j == 1:
+            got.append((swap(gives[j], "fsdp", j), start))
+        else:
+            mine = swap(lax.dynamic_slice_in_dim(gives[j], side * half, half, 0), "fsdp", j)
+            got.append((mine, start + side * half))
+            got.append((swap(mine, "seq", 1), start + (1 - side) * half))
+    w_value = rows_in_order(got, me)
+    rest = in_weight[:, 2 * inner :]
+    kept = rest.shape[1]
+    rest = all_slots(jnp.pad(rest, ((0, 0), (0, -kept % lanes)))[None], "fsdp")
+    rest = in_order([rest[j] for j in range(nf)], me).reshape(width, -1)
+    w_rows = rest[:, : 2 * state]
+    w_step = jnp.pad(lax.dynamic_slice_in_dim(rest, 2 * state + me * heads, heads, 1), ((0, 0), (0, lanes - heads)))
+    w_conv = jnp.concatenate([w_value, w_rows, w_step], axis=1)
+
+    (normed,) = call(
+        normalize_kernel,
+        slots,
+        [(x_main, each), (x_small, each), (norm_all, None)],
+        [((slots, halo + seg, width), bf16, each)],
+        "normalize",
+    )
     inputs = tokens[0].astype(f32)
     inv = lax.rsqrt(jnp.mean(inputs * inputs, axis=-1, keepdims=True) + epsilon)
-    normed_own = (inputs * inv * norm_all).astype(bf16)
-    before = lax.ppermute(normed_own[seg - halo :], "seq", [(i, i + 1) for i in range(nq - 1)])
-    normed = all_slots(jnp.concatenate([before, normed_own], axis=0)[None], "fsdp")
-
     valid = (place * seg + jnp.arange(seg) < lengths[0]).astype(f32)[:, None]
     upstream = valid * cotangent[0].astype(f32)
-    w_gate = in_weight[:, :inner].reshape(rows, nf, channels).transpose(1, 0, 2)
-    w_gate, later, _ = lax.optimization_barrier((w_gate, upstream.astype(bf16), w_conv))
-    w_gate = exchange(w_gate, "fsdp").reshape(width, channels)
+
+    gives = [lax.dynamic_slice_in_dim(in_weight, (me ^ j) * channels, channels, 1) for j in range(nf)]
+    gives, later, _ = lax.optimization_barrier((gives, upstream.astype(bf16), got[-2][0]))
+    w_gate = rows_in_order([(swap(g, "fsdp", j) if j else g, (me ^ j) * rows) for j, g in enumerate(gives)], me)
     back_branch = all_slots(later[None], "fsdp")
 
     def project(x, w):
@@ -348,77 +548,95 @@
     pc = project(normed, w_conv).astype(bf16)
     main = normed[:, halo:]
     cw = channels + 2 * state
-    raw = pc[:, halo:, cw:].astype(f32) + rate[0]
-    total = jnp.sum(jax.nn.softplus(raw), axis=1)[:, :heads] * -rate[1, :heads]
-    piece = slots * channels // nq
-    whole = jnp.repeat(jnp.exp(total).reshape(-1), head_size).reshape(nq, piece)
-    whole = exchange(whole, "seq")[..., None]
-
     tall = 16
     statics = dict(channels=channels, state=state)
+    turned = (per_slot, lambda s, i: s ^ (i[0] // per_slot))
     act, y_local, s_local, lac, dtc, lar, dtr = call(
         forward_kernel,
         slots,
-        [(pc, True), (taps, False), (rate, False)],
+        [(pc, each), (taps, None), (rate, None)],
         [
-            ((slots, seg, cw), bf16, True),
-            ((slots, seg, channels), f32, True),
-            ((slots, channels, state), bf16, True),
-            ((slots, seg, lanes), f32, True),
-            ((slots, seg, lanes), f32, True),
-            ((slots, tall, seg), f32, True),
-            ((slots, tall, seg), f32, True),
+            ((slots, seg, cw), bf16, each),
+            ((slots, seg, channels), f32, each),
+            ((nq, piece + 16, state), bf16, turned),
+            ((slots, seg, lanes), f32, each),
+            ((slots, seg, lanes), f32, each),
+            ((slots, tall, seg), f32, each),
+            ((slots, tall, seg), f32, each),
         ],
         "forward",
+        ids=ids,
         flops=2 * slots * seg * seg * channels,
+        rows=piece,
         **statics,
     )
-    everything = exchange(s_local.reshape(nq, piece, state), "seq").astype(f32)
-    carried, reached = jnp.zeros((piece, state), f32), []
-    for i in range(nq):
-        reached.append(carried.astype(bf16))
-        carried = whole[i] * carried + everything[i]
-    s_in = exchange(jnp.stack(reached), "seq").reshape(slots, channels, state)
+
+    def ordered(parts):
+        (out,) = call(order_kernel, 1, [(p, None) for p in parts], [((nq, piece, state), bf16, None)], "order", ids=ids)
+        return out.reshape(slots, channels, state)
+
+    came = sent(s_local, "seq")
+    reached, decays = call(
+        chain_kernel,
+        1,
+        [(part, None) for part in came],
+        [((nq, piece, state), bf16, None), ((nq, 8, lanes), f32, None)],
+        "chain",
+        ids=ids,
+        scratch=[pltpu.VMEM((nq, piece + 16, state), bf16)],
+        rows=piece,
+        count=per_slot,
+    )
+    s_in = ordered(sent(reached, "seq"))
 
     gate = project(main, w_gate).astype(bf16)
     bg = lax.dot_general(back_branch, out_weight, (((2,), (1,)), ((), ())), preferred_element_type=f32)
     y, stats = call(
         finish_kernel,
         slots,
-        [(y_local, True), (act, True), (lac, True), (s_in, True), (gate, True), (bg, True), (vec, False)],
-        [((slots, seg, channels), f32, True), ((slots, 8, seg), f32, True)],
+        [(y_local, each), (act, each), (lac, each), (s_in, each), (gate, each), (bg, each), (vec, None)],
+        [((slots, seg, channels), f32, each), ((slots, 8, seg), f32, each)],
         "finish",
         **statics,
     )
-    stats = over_owners(stats, "fsdp")
+    shares = [(swap(stats, "fsdp", j) if j else stats, (1, lambda s, i, j=j: s ^ j)) for j in range(nf)]
     gated_out, dgate, dy, pos, dsin, dskip = call(
         norm_kernel,
         slots,
-        [(y, True), (act, True), (lac, True), (gate, True), (bg, True), (vec, False), (stats, True)],
+        [(y, each), (act, each), (lac, each), (gate, each), (bg, each), (vec, None)] + shares,
         [
-            ((slots, seg, channels), bf16, True),
-            ((slots, seg, channels), bf16, True),
-            ((slots, seg, channels), f32, True),
-            ((slots, seg, lanes), f32, True),
-            ((slots, channels, state), bf16, True),
-            ((8, channels), f32, False),
+            ((slots, seg, channels), bf16, each),
+            ((slots, seg, channels), bf16, each),
+            ((slots, seg, channels), f32, each),
+            ((slots, seg, lanes), f32, each),
+            ((nq, piece, state), bf16, turned),
+            ((8, channels), f32, None),
         ],
         "norm",
+        ids=ids,
         inner=inner,
+        rows=piece,
         **statics,
     )
-    everything = exchange(dsin.reshape(nq, piece, state), "seq").astype(f32)
-    carried, reached = jnp.zeros((piece, state), f32), [None] * nq
-    for i in reversed(range(nq)):
-        reached[i] = carried.astype(bf16)
-        carried = whole[i] * carried + everything[i]
-    g_end = exchange(jnp.stack(reached), "seq").reshape(slots, channels, state)
+    came = sent(dsin, "seq")
+    (reached,) = call(
+        back_chain_kernel,
+        1,
+        [(part, None) for part in came] + [(decays, None)],
+        [((nq, piece, state), bf16, None)],
+        "back_chain",
+        ids=ids,
+        scratch=[pltpu.VMEM((nq, piece, state), bf16)],
+        rows=piece,
+        count=per_slot,
+    )
+    g_end = ordered(sent(reached, "seq"))
 
     r_local, dbc = call(
         backward_kernel,
         slots,
-        [(act, True), (dy, True), (lac, True), (lar, True), (dtr, True), (s_in, True)],
-        [((slots, seg, channels), f32, True), ((slots, seg, 2 * state), f32, True)],
+        [(act, each), (dy, each), (lac, each), (lar, each), (dtr, each), (s_in, each)],
+        [((slots, seg, channels), f32, each), ((slots, seg, 2 * state), f32, each)],
         "backward",
         flops=4 * slots * seg * seg * channels,
         **statics,
@@ -427,18 +645,20 @@
         carry_kernel,
         slots,
         [
-            (pc, True), (taps, False), (rate, False), (act, True), (dy, True), (r_local, True), (pos, True),
-            (lac, True), (dtc, True), (g_end, True), (s_in, True), (s_local, True), (dbc, True), (vec, False),
+            (pc, each), (taps, None), (rate, None), (act, each), (dy, each), (r_local, each), (pos, each), (lac, each),
+            (dtc, each), (g_end, each), (s_in, each), (s_local, turned), (dbc, each), (vec, None),
         ],
         [
-            ((slots, seg, channels), f32, True),
-            ((slots, 8, channels), f32, True),
-            ((slots, seg, lanes), bf16, True),
-            ((slots, seg, 2 * state), f32, True),
-            ((8, channels), f32, False),
-            ((8, lanes), f32, False),
+            ((slots, seg, channels), f32, each),
+            ((slots, 8, channels), f32, each),
+            ((slots, seg, lanes), bf16, each),
+            ((slots, seg, 2 * state), f32, each),
+            ((8, channels), f32, None),
+            ((8, lanes), f32, None),
         ],
         "carry",
+        ids=ids,
+        rows=piece,
         **statics,
     )
     behind = [(i, i - 1) for i in range(1, nq)]
@@ -446,8 +666,8 @@
     (dvalue,) = call(
         returned_kernel,
         slots,
-        [(dpre, True), (after, True), (taps[:, :channels], False)],
-        [((slots, seg, channels), bf16, True)],
+        [(dpre, each), (after, each), (taps[:, :channels], None)],
+        [((slots, seg, channels), bf16, each)],
         "returned",
     )
 
@@ -488,33 +708,84 @@
     block = jnp.pad(block, ((0, 0), (0, lanes - share - heads - extra)))
     gw_last = jnp.concatenate([grad_of(main, dlast), jnp.tile(block, (nf, 1))], axis=1)
 
+    unit = rows // nq
+
     def summed(g):
-        g = g.astype(bf16).reshape(nf, nq, rows // nq, -1).transpose(1, 0, 2, 3).reshape(width, -1)
-        g = lax.psum_scatter(g, "seq", scatter_dimension=0, tiled=True).reshape(nf, rows // nq, -1)
-        g = exchange(g, "fsdp")
-        g = lax.all_gather(g, "seq", axis=1)
-        return g.reshape(nf, rows, -1)
-
-    g_out = grad_of(gated_out, back_branch).astype(bf16)
-    g_out = lax.psum_scatter(g_out, "seq", scatter_dimension=0, tiled=True)
-    g_out = lax.all_gather(g_out, "seq", axis=0, tiled=True).astype(f32)
-    s_gate = summed(grad_of(main, dgate)).astype(f32)
-    s_value = summed(grad_of(main, dvalue)).astype(f32)
-    s_last = summed(gw_last).astype(f32)
-
-    def spread_columns(s):
-        return s.transpose(1, 0, 2).reshape(rows, -1)
-
-    g_in = jnp.concatenate(
-        [
-            spread_columns(s_gate),
-            spread_columns(s_value),
-            spread_columns(s_last[..., :share]),
-            spread_columns(s_last[..., share : share + heads]),
-        ],
-        axis=1,
-    )
-    got = s_last[..., share + heads : share + heads + extra]
+        g = scatter_sum(g.astype(bf16).reshape(nf, nq, unit, -1), "seq", 1)
+        return gathered(traded(g, "fsdp"), "seq")
+
+    def cut(value):
+        size = value.shape[-1] // 2
+        return [value] if size % lanes else [value[..., :size], value[..., size:]]
+
+    out_parts = [
+        gathered(scatter_sum(grad_of(gated_out, part).astype(bf16).reshape(nq, channels // nq, -1), "seq", 0), "seq")
+        for part in cut(back_branch)
+    ]
+    starts, bufs = [], []
+    for base, whole in ((0, dgate), (inner, dvalue)):
+        for part in cut(whole):
+            starts.append((base, channels))
+            base += part.shape[-1]
+            bufs.append(summed(grad_of(main, part)))
+    s_last = summed(gw_last)
+
+    by_place = (1, lambda s, i: reversed_bits(i[0] ^ s, nq))
+    place_of = jnp.stack([reversed_bits(place ^ q, nq) for q in range(nq)])
+    if unit % 16 == 0:
+        g_in, tail, norm_sum = call(
+            assemble_kernel,
+            nq,
+            [(buf, by_place) for buf in bufs] + [(s_last, by_place), (in_weight, (unit, lambda s, i: s))],
+            [
+                (in_weight.shape, f32, (unit, lambda s, i: s)),
+                ((nf, rows, lanes), f32, "rows"),
+                ((rows, 1), f32, (unit, lambda s, i: s)),
+            ],
+            "assemble",
+            ids=ids,
+            parts=starts,
+            share=share,
+            heads=heads,
+            inner=inner,
+        )
+        norm_sum = norm_sum[:, 0]
+    else:
+        order = me ^ jnp.arange(nf)
+
+        def natural(buf):
+            return buf[place_of][:, order].astype(f32).transpose(1, 0, 2, 3).reshape(nf, rows, -1)
+
+        def side_by_side(value):
+            return value.transpose(1, 0, 2).reshape(rows, -1)
+
+        count = len(bufs) // 2
+        joined = [side_by_side(jnp.concatenate([natural(b) for b in bs], axis=2)) for bs in (bufs[:count], bufs[count:])]
+        tail = natural(s_last)
+        joined += [side_by_side(tail[..., :share]), side_by_side(tail[..., share : share + heads])]
+        g_in = jnp.concatenate(joined, axis=1)
+        norm_sum = jnp.sum(g_in * in_weight.astype(f32), axis=1)
+    out_unit = channels // nq
+    if out_unit % 16 == 0:
+        sizes = [part.shape[-1] for part in out_parts]
+        g_out, gated_sum = call(
+            rows_kernel,
+            nq,
+            [(part, by_place) for part in out_parts] + [(out_weight, (out_unit, lambda s, i: s))],
+            [(out_weight.shape, f32, (out_unit, lambda s, i: s)), ((channels, 1), f32, (out_unit, lambda s, i: s))],
+            "rows",
+            ids=ids,
+            parts=[(sum(sizes[:i]), size) for i, size in enumerate(sizes)],
+        )
+        gated_sum = gated_sum[:, 0]
+    else:
+        g_out = jnp.concatenate([part[place_of].astype(f32).reshape(channels, -1) for part in out_parts], axis=1)
+        gated_sum = jnp.sum(g_out * out_weight.astype(f32), axis=1)
+
+    norm_grad = norm_sum / norm_gain.astype(f32)
+    gated_grad = gated_sum / gated_gain.astype(f32)
+
+    got = tail[..., share + heads : share + heads + extra]
     tap_grads = jnp.concatenate(
         [
             got[..., : 5 * per].reshape(nf, rows, per, 5).transpose(0, 2, 1, 3).reshape(inner, 5),
@@ -524,9 +795,6 @@
     )
     tap_grads = lax.dynamic_slice_in_dim(tap_grads, me * conv_own, conv_own, 0).T
     head_grads = lax.dynamic_index_in_dim(got, me, 0, False)[:heads, 5 * per + 5 :]
-
-    norm_grad = jnp.sum(g_in * in_weight.astype(f32), axis=1) / norm_gain.astype(f32)
-    gated_grad = jnp.sum(g_out * out_weight.astype(f32), axis=1) / gated_gain.astype(f32)
 
     branch = project(gated_out, out_weight)
     branch = to_owner([branch[j] for j in range(slots)], "fsdp")

time: 747 us -> 622 us (0.83)
  waiting for transfers between devices: 317 us -> 223 us
  starting transfers between devices: 61.8 us -> 152 us
  blocking collectives: 80 us -> 0 us
  other arithmetic: 63.1 us -> 34.7 us
  Pallas kernels: 57.8 us -> 73 us
  matrix products: 56.3 us -> 42.4 us
  between operations: 16.5 us -> 4.24 us
    ppermute x17 -> x117, waiting for transfers between devices: 31 us -> 213 us  [swap(): return lax.ppermute(value, axis, [(i, i ^ by) for i in range(count)])]
    ppermute x17 -> x117, starting transfers between devices: 8.51 us -> 145 us  [swap(): return lax.ppermute(value, axis, [(i, i ^ by) for i in range(count)])]
    reduce_scatter x4 -> x0, waiting for transfers between devices: 107 us -> none  [the longest x3 107 us: summed(): lax.psum_scatter(g, 'seq', scatter_dimension=0, tiled=True)]
    all_gather x3 -> x0, waiting for transfers between devices: 92.2 us -> none  [the longest x2 89.7 us: summed(): g = lax.all_gather(g, 'seq', axis=1)]
    all_gather x3 -> x0, blocking collectives: 80 us -> none  [the longest x1 42.6 us: per_device(): norm_all = lax.all_gather(norm_gain, 'fsdp', axis=0, tiled=True).astype(f32)]
    all_to_all x10 -> x0, waiting for transfers between devices: 71.2 us -> none  [exchange(): return lax.all_to_all(value, axis, 0, 0)]
    all_to_all x10 -> x0, starting transfers between devices: 45.3 us -> none  [exchange(): return lax.all_to_all(value, axis, 0, 0)]
    reshape x8 -> x1, local copies, waits for them, and re-layouts: 22.5 us -> 0.12 us  [per_device(): taps_all.reshape(nf, 5, conv_own).transpose(1, 0, 2).reshape(5, -1)]
  transfers between devices with their start and end apart: 37 -> 120, of which waited for: 19 -> 53; matrix products, arithmetic and copies ran while one was open for 17% -> 19% of each run, Pallas kernels for 6% -> 9%
where the time goes in v2:
time: 622 us; the launch traced here: 612 us
  waiting for transfers between devices  223 us (36%)
  starting transfers between devices  152 us (24%)
  local copies, waits for them, and re-layouts  82.5 us (13%)
  Pallas kernels  73 us (12%)
  matrix products  42.4 us (7%)
  other arithmetic  34.7 us (6%)
    ppermute x117, waiting for transfers between devices, swap(): return lax.ppermute(value, axis, [(i, i ^ by) for i in range(count)])  213 us
    ppermute x117, starting transfers between devices, swap(): return lax.ppermute(value, axis, [(i, i ^ by) for i in range(count)])  145 us
    pallas_call x13, Pallas kernels, call(): pl.pallas_call(functools.partial(kernel, **statics), grid_spec=pltpu.Pref...  73 us
    unnamed x213, local copies, waits for them, and re-layouts  34.9 us
    dot_general x3, matrix products, back(): lax.dot_general(dz, w, (((2,), (1,)), ((), ())), preferred_element_type=f32)  15.4 us
    dot_general x7, matrix products, grad_of(): lax.dot_general(x, dz, (((0, 1), (0, 1)), ((), ())), preferred_element_ty...  12.7 us
  transfers between devices with their start and end apart: 120, of which 53 were waited for; matrix products, arithmetic and copies ran while one was open for 19% of the time, Pallas kernels for 9%

profile of v2, /device:TPU:0, one launch (start us, length us, event | category | flops | bytes accessed | tf_op | source)
XLA Modules:
  0.0 612.0 jit_solution(255195818732080183)
XLA Ops:
  9.5 7.5 %copy.86.refs_5_ = bf16[384,6448]{1,0:T(8,128)(2,1)} copy(bf16[384,6448]{0,1:T(8,128)(2,1)} %param.15) | data formatting | bytes 9904128 | tf_op args[3]
  55.9 6.7 %collective-permute-done.10 = bf16[192,768]{1,0:T(8,128)(2,1)} collective-permute-done((bf16[192,768]{1,0:T(8,128)(2,1)}, bf16[192,768]{1,0:T(8,128)(2,1)}, u32[]{:S(2)}, u32[]{:S(2)}) %collective-permute-start.10) | collective-permute-done | bytes 294944 | tf_op jit(solution)/shard_map/ppermute | solution.py:345
  81.1 12.9 %forward.1 = (bf16[4,256,1024]{2,1,0:T(8,128)(2,1)S(1)}, f32[4,256,768]{2,1,0:T(8,128)S(1)}, bf16[8,400,128]{2,1,0:T(8,128)(2,1)S(1)}, f32[4,256,128]{2,1,0:T(8,...) custom-call(s32[2]{0:T(128)S(1)} %pad_add_fusion.ids_ref, ...), custom_call_target="tpu_custom_call" | custom-call | flops 402653184 | bytes 9785344 | tf_op jit(solution)/shard_map/forward/pallas_call | solution.py:324
  107.6 8.2 %collective-permute-start.21 = (bf16[400,128]{1,0:T(8,128)(2,1)S(1)}, bf16[400,128]{1,0:T(8,128)(2,1)S(1)}, u32[]{:S(2)}, u32[]{:S(2)}) collective-permute-start(bf16[400,128]{1,0:T(8,128)(2,1)S(1)} %get-tuple-element.138), channel_id=1, source_target_pairs={{0,28},{4,24},{8,20},{12,16},{16,12},{20,8},{24,4},{28,0},{1,29},{... | collective-permute-start | bytes 307208 | tf_op jit(solution)/shard_map/ppermute | solution.py:345
  135.4 7.8 %collective-permute-start.28 = (bf16[384,128]{1,0:T(8,128)(2,1)S(1)}, bf16[384,128]{1,0:T(8,128)(2,1)S(1)}, u32[]{:S(2)}, u32[]{:S(2)}) collective-permute-start(bf16[384,128]{1,0:T(8,128)(2,1)S(1)} %get-tuple-element.164), channel_id=1, source_target_pairs={{0,28},{4,24},{8,20},{12,16},{16,12},{20,8},{24,4},{28,0},{1,29},{... | collective-permute-start | bytes 294920 | tf_op jit(solution)/shard_map/ppermute | solution.py:345
  158.9 9.4 %norm.1 = (bf16[4,256,768]{2,1,0:T(8,128)(2,1)S(1)}, bf16[4,256,768]{2,1,0:T(8,128)(2,1)S(1)}, f32[4,256,768]{2,1,0:T(8,128)S(1)}, f32[4,256,128]{2,1,0:T(8,128)...) custom-call(s32[2]{0:T(128)S(1)} %pad_add_fusion.ids_ref, f32[4,256,768]{2,1,0:T(8,128)S(1)} %get-tuple-element.56.y_ref, ...), custom_call_target="tpu_custom_call" | custom-call | bytes 18268160 | tf_op jit(solution)/shard_map/norm/pallas_call | solution.py:324
  227.4 13.9 %backward.1 = (f32[4,256,768]{2,1,0:T(8,128)S(1)}, f32[4,256,256]{2,1,0:T(8,128)S(1)}) custom-call(bf16[4,256,1024]{2,1,0:T(8,128)(2,1)S(1)} %get-tuple-element.47.act_ref, f32[4,256,768]{2,1,0:T(8,128)S(1)} %copy-done.1, f32[4,256,128]{2,1,0:T(8,128)S(1)} %get-tuple-element.48.lac_ref, f32[4,16,256]{2,1,0:T(8,128)S(1)} %copy-done.29, ...), custom_call_target="tpu_custom_call" | custom-call | flops 805306368 | bytes 10878976 | tf_op jit(solution)/shard_map/backward/pallas_call | solution.py:324
  246.2 14.1 %carry.1 = (f32[4,256,768]{2,1,0:T(8,128)S(1)}, f32[4,8,768]{2,1,0:T(8,128)S(1)}, bf16[4,256,128]{2,1,0:T(8,128)(2,1)S(1)}, f32[4,256,256]{2,1,0:T(8,128)S(1)}, ...) custom-call(s32[2]{0:T(128)S(1)} %copy-done.34, bf16[4,272,1152]{2,1,0:T(8,128)(2,1)S(1)} %copy-done.4, ...), custom_call_target="tpu_custom_call" | custom-call | bytes 20553728 | tf_op jit(solution)/shard_map/carry/pallas_call | solution.py:324
  297.7 8.2 %collective-permute-done.58 = bf16[4,256,64]{2,1,0:T(8,128)(2,1)S(1)} collective-permute-done((bf16[4,256,64]{2,1,0:T(8,128)(2,1)S(1)}, bf16[4,256,64]{2,1,0:T(8,128)(2,1)S(1)}, u32[]{:S(2)}, u32[]{:S(2)}) %collective-permute-start.58) | collective-permute-done | bytes 131104 | tf_op jit(solution)/shard_map/ppermute | solution.py:345
  324.7 7.0 %fusion.98 = (bf16[4,256,1536]{2,1,0:T(8,128)(2,1)S(1)}, f32[4,256,1536]{2,1,0:T(8,128)S(1)}) fusion(f32[4,256,1536]{2,1,0:T(8,128)} %fusion.72, f32[4,256,1536]{2,1,0:T(8,128)} %fusion.7, bf16[4,256,768]{2,1,0:T(8,128)(2,1)S(1)} %copy-done.15, bf16[1536,768]{1,0:T(8,128)(2,1)} %copy-done.41), kind=kOutput, calls=%fused_computation.343 | convolution fusion | flops 2420637696 | bytes 25952256 | tf_op jit(solution)/shard_map/dot_general | solution.py:807
  339.4 9.7 %collective-permute-done.114 = bf16[4,96,768]{2,1,0:T(8,128)(2,1)S(1)} collective-permute-done((bf16[4,96,768]{2,1,0:T(8,128)(2,1)S(1)}, bf16[4,96,768]{2,1,0:T(8,128)(2,1)S(1)}, u32[]{:S(2)}, u32[]{:S(2)}) %collective-permute-start.114) | collective-permute-done | bytes 589856 | tf_op jit(solution)/shard_map/ppermute | solution.py:345
  368.4 7.6 %collective-permute-done.106 = bf16[2,4,48,128]{3,2,1,0:T(8,128)(2,1)S(1)} collective-permute-done((bf16[2,4,48,128]{3,2,1,0:T(8,128)(2,1)S(1)}, bf16[2,4,48,128]{3,2,1,0:T(8,128)(2,1)S(1)}, u32[]{:S(2)}, u32[]{:S(2)}) %collective-permute-start.106) | collective-permute-done | bytes 98336 | tf_op jit(solution)/shard_map/ppermute | solution.py:345
  378.2 7.7 %collective-permute-done.73 = bf16[4,2,48,384]{3,2,1,0:T(8,128)(2,1)S(1)} collective-permute-done((bf16[4,2,48,384]{3,2,1,0:T(8,128)(2,1)S(1)}, bf16[4,2,48,384]{3,2,1,0:T(8,128)(2,1)S(1)}, u32[]{:S(2)}, u32[]{:S(2)}) %collective-permute-start.73) | collective-permute-done | bytes 294944 | tf_op jit(solution)/shard_map/ppermute | solution.py:345
  403.3 11.7 %collective-permute-done.65 = bf16[4,1,48,384]{3,2,1,0:T(8,128)(2,1)S(1)} collective-permute-done((bf16[4,1,48,384]{3,2,1,0:T(8,128)(2,1)S(1)}, bf16[4,1,48,384]{3,2,1,0:T(8,128)(2,1)S(1)}, u32[]{:S(2)}, u32[]{:S(2)}) %collective-permute-start.65) | collective-permute-done | bytes 147488 | tf_op jit(solution)/shard_map/ppermute | solution.py:345
  441.0 9.8 %collective-permute-done.117 = bf16[1,96,768]{2,1,0:T(8,128)(2,1)S(1)} collective-permute-done((bf16[1,96,768]{2,1,0:T(8,128)(2,1)S(1)}, bf16[1,96,768]{2,1,0:T(8,128)(2,1)S(1)}, u32[]{:S(2)}, u32[]{:S(2)}) %collective-permute-start.117) | collective-permute-done | bytes 147488 | tf_op jit(solution)/shard_map/ppermute | solution.py:345
  474.2 7.7 %collective-permute-start.70 = (bf16[2,4,48,384]{3,2,1,0:T(8,128)(2,1)S(1)}, bf16[2,4,48,384]{3,2,1,0:T(8,128)(2,1)S(1)}, u32[]{:S(2)}, u32[]{:S(2)}) collective-permute-start(bf16[2,4,48,384]{3,2,1,0:T(8,128)(2,1)S(1)} %pad_maximum_fusion.18), channel_id=1, source_target_pairs={{0,8},{4,12},{8,0},{12,4},{16,24},{20,28},{24,16},{28,20},{1,9},{5... | collective-permute-start | bytes 884744 | tf_op jit(solution)/shard_map/ppermute | solution.py:345
  485.1 10.0 %collective-permute-done.87 = bf16[1,4,48,384]{3,2,1,0:T(8,128)(2,1)S(1)} collective-permute-done((bf16[1,4,48,384]{3,2,1,0:T(8,128)(2,1)S(1)}, bf16[1,4,48,384]{3,2,1,0:T(8,128)(2,1)S(1)}, u32[]{:S(2)}, u32[]{:S(2)}) %collective-permute-start.87) | collective-permute-done | bytes 147488 | tf_op jit(solution)/shard_map/ppermute | solution.py:345
  519.0 7.0 %collective-permute-done.40 = bf16[256,1536]{1,0:T(8,128)(2,1)S(1)} collective-permute-done((bf16[256,1536]{1,0:T(8,128)(2,1)S(1)}, bf16[256,1536]{1,0:T(8,128)(2,1)S(1)}, u32[]{:S(2)}, u32[]{:S(2)}) %collective-permute-start.40) | collective-permute-done | bytes 786464 | tf_op jit(solution)/shard_map/ppermute | solution.py:345
  530.9 11.3 %collective-permute-done.119 = bf16[4,96,768]{2,1,0:T(8,128)(2,1)S(1)} collective-permute-done((bf16[4,96,768]{2,1,0:T(8,128)(2,1)S(1)}, bf16[4,96,768]{2,1,0:T(8,128)(2,1)S(1)}, u32[]{:S(2)}, u32[]{:S(2)}) %collective-permute-start.119) | collective-permute-done | bytes 589856 | tf_op jit(solution)/shard_map/ppermute | solution.py:345
  547.8 7.1 %collective-permute-done.71 = bf16[4,4,48,384]{3,2,1,0:T(8,128)(2,1)} collective-permute-done((bf16[4,4,48,384]{3,2,1,0:T(8,128)(2,1)}, bf16[4,4,48,384]{3,2,1,0:T(8,128)(2,1)}, u32[]{:S(2)}, u32[]{:S(2)}) %collective-permute-start.71) | collective-permute-done | bytes 589856 | tf_op jit(solution)/shard_map/ppermute | solution.py:345
  556.2 11.4 %collective-permute-done.80 = bf16[4,4,48,384]{3,2,1,0:T(8,128)(2,1)} collective-permute-done((bf16[4,4,48,384]{3,2,1,0:T(8,128)(2,1)}, bf16[4,4,48,384]{3,2,1,0:T(8,128)(2,1)}, u32[]{:S(2)}, u32[]{:S(2)}) %collective-permute-start.80) | collective-permute-done | bytes 589856 | tf_op jit(solution)/shard_map/ppermute | solution.py:345
  568.8 11.4 %collective-permute-done.89 = bf16[4,4,48,384]{3,2,1,0:T(8,128)(2,1)} collective-permute-done((bf16[4,4,48,384]{3,2,1,0:T(8,128)(2,1)}, bf16[4,4,48,384]{3,2,1,0:T(8,128)(2,1)}, u32[]{:S(2)}, u32[]{:S(2)}) %collective-permute-start.89) | collective-permute-done | bytes 589856 | tf_op jit(solution)/shard_map/ppermute | solution.py:345
  581.5 6.6 %collective-permute-done.98 = bf16[4,4,48,384]{3,2,1,0:T(8,128)(2,1)} collective-permute-done((bf16[4,4,48,384]{3,2,1,0:T(8,128)(2,1)}, bf16[4,4,48,384]{3,2,1,0:T(8,128)(2,1)}, u32[]{:S(2)}, u32[]{:S(2)}) %collective-permute-start.98) | collective-permute-done | bytes 589856 | tf_op jit(solution)/shard_map/ppermute | solution.py:345
  600.1 10.7 %copy.126 = f32[384,6448]{0,1:T(8,128)} copy(f32[384,6448]{1,0:T(8,128)} %copy-done.5) | data formatting | bytes 19808256
  (652 shorter events, 382.3 us)
Async XLA Ops:
  1.6 40.4 %collective-permute-start.13 = (bf16[1,384,384]{1,2,0:T(8,128)(2,1)S(1)}, bf16[1,384,384]{1,2,0:T(8,128)(2,1)S(1)}, u32[]{:S(2)}, u32[]{:S(2)}) collective-permute-start(bf16[1,384,384]{1,2,0:T(8,128)(2,1)S(1)} %pad_bitcast_fusion), channel_id=1, source_target_pairs={{0,2},{1,3},{2,0},{3,1},{4,6},{5,7},{6,4},{7,5},{8,10},{9,11},{10,... | collective-permute-start | bytes 884744 | tf_op jit(solution)/shard_map/ppermute | solution.py:345
  4.7 39.5 %collective-permute-start.12 = (bf16[1,384,384]{1,2,0:T(8,128)(2,1)S(1)}, bf16[1,384,384]{1,2,0:T(8,128)(2,1)}, u32[]{:S(2)}, u32[]{:S(2)}) collective-permute-start(bf16[1,384,384]{1,2,0:T(8,128)(2,1)S(1)} %pad_bitcast_fusion), channel_id=1, source_target_pairs={{0,1},{1,0},{2,3},{3,2},{4,5},{5,4},{6,7},{7,6},{8,9},{9,8},{10,11... | collective-permute-start | bytes 884744 | tf_op jit(solution)/shard_map/ppermute | solution.py:345
  4.7 65.5 %collective-permute-start.1 = (bf16[1,256,1536]{2,1,0:T(8,128)(2,1)}, bf16[1,256,1536]{2,1,0:T(8,128)(2,1)}, u32[]{:S(2)}, u32[]{:S(2)}) collective-permute-start(bf16[1,256,1536]{2,1,0:T(8,128)(2,1)} %param.12), channel_id=1, source_target_pairs={{0,2},{1,3},{2,0},{3,1},{4,6},{5,7},{6,4},{7,5},{8,10},{9,11},{10,... | collective-permute-start | bytes 2359304 | tf_op jit(solution)/shard_map/ppermute | solution.py:345
  62.7 33.7 %collective-permute-start.29 = (bf16[384,768]{1,0:T(8,128)(2,1)}, bf16[384,768]{1,0:T(8,128)(2,1)S(1)}, u32[]{:S(2)}, u32[]{:S(2)}) collective-permute-start(bf16[384,768]{1,0:T(8,128)(2,1)} %get-tuple-element.52), channel_id=1, source_target_pairs={{0,1},{1,0},{2,3},{3,2},{4,5},{5,4},{6,7},{7,6},{8,9},{9,8},{10,11... | collective-permute-start | bytes 1769480 | tf_op jit(solution)/shard_map/ppermute | solution.py:345
  62.7 35.4 %collective-permute-start.30 = (bf16[384,768]{1,0:T(8,128)(2,1)}, bf16[384,768]{1,0:T(8,128)(2,1)S(1)}, u32[]{:S(2)}, u32[]{:S(2)}) collective-permute-start(bf16[384,768]{1,0:T(8,128)(2,1)} %get-tuple-element.53), channel_id=1, source_target_pairs={{0,2},{1,3},{2,0},{3,1},{4,6},{5,7},{6,4},{7,5},{8,10},{9,11},{10,... | collective-permute-start | bytes 1769480 | tf_op jit(solution)/shard_map/ppermute | solution.py:345
  67.4 54.4 %collective-permute-start.31 = (bf16[384,768]{1,0:T(8,128)(2,1)S(1)}, bf16[384,768]{1,0:T(8,128)(2,1)S(1)}, u32[]{:S(2)}, u32[]{:S(2)}) collective-permute-start(bf16[384,768]{1,0:T(8,128)(2,1)S(1)} %copy-done.71), channel_id=1, source_target_pairs={{0,3},{1,2},{2,1},{3,0},{4,7},{5,6},{6,5},{7,4},{8,11},{9,10},{10,... | collective-permute-start | bytes 1769480 | tf_op jit(solution)/shard_map/ppermute | solution.py:345
  71.8 50.1 %collective-permute-start.33 = (bf16[1,256,1536]{2,1,0:T(8,128)(2,1)S(1)}, bf16[1,256,1536]{2,1,0:T(8,128)(2,1)S(1)}, u32[]{:S(2)}, u32[]{:S(2)}) collective-permute-start(bf16[1,256,1536]{2,1,0:T(8,128)(2,1)S(1)} %bitcast.443), channel_id=1, source_target_pairs={{0,2},{1,3},{2,0},{3,1},{4,6},{5,7},{6,4},{7,5},{8,10},{9,11},{10,... | collective-permute-start | bytes 2359304 | tf_op jit(solution)/shard_map/ppermute | solution.py:345
  211.0 30.3 %collective-permute-start.50 = (bf16[384,128]{1,0:T(8,128)(2,1)}, bf16[384,128]{1,0:T(8,128)(2,1)}, u32[]{:S(2)}, u32[]{:S(2)}) collective-permute-start(bf16[384,128]{1,0:T(8,128)(2,1)} %get-tuple-element.152), channel_id=1, source_target_pairs={{0,12},{4,8},{8,4},{12,0},{16,28},{20,24},{24,20},{28,16},{1,13},{... | collective-permute-start | bytes 294920 | tf_op jit(solution)/shard_map/ppermute | solution.py:345
  211.0 30.4 %collective-permute-start.51 = (bf16[384,128]{1,0:T(8,128)(2,1)}, bf16[384,128]{1,0:T(8,128)(2,1)}, u32[]{:S(2)}, u32[]{:S(2)}) collective-permute-start(bf16[384,128]{1,0:T(8,128)(2,1)} %get-tuple-element.151), channel_id=1, source_target_pairs={{0,16},{4,20},{8,24},{12,28},{16,0},{20,4},{24,8},{28,12},{1,17},{... | collective-permute-start | bytes 294920 | tf_op jit(solution)/shard_map/ppermute | solution.py:345
  241.3 123.7 %collective-permute-start.39 = (bf16[256,1536]{1,0:T(8,128)(2,1)}, bf16[256,1536]{1,0:T(8,128)(2,1)}, u32[]{:S(2)}, u32[]{:S(2)}) collective-permute-start(bf16[256,1536]{1,0:T(8,128)(2,1)} %get-tuple-element.133), channel_id=1, source_target_pairs={{0,1},{1,0},{2,3},{3,2},{4,5},{5,4},{6,7},{7,6},{8,9},{9,8},{10,11... | collective-permute-start | bytes 2359304 | tf_op jit(solution)/shard_map/ppermute | solution.py:345
  241.4 92.7 %collective-permute-start.63 = (bf16[4,4,48,384]{3,2,1,0:T(8,128)(2,1)}, bf16[4,4,48,384]{3,2,1,0:T(8,128)(2,1)}, u32[]{:S(2)}, u32[]{:S(2)}) collective-permute-start(bf16[4,4,48,384]{3,2,1,0:T(8,128)(2,1)} %dynamic-slice_bitcast_fusion.5), channel_id=1, source_target_pairs={{0,4},{4,0},{8,12},{12,8},{16,20},{20,16},{24,28},{28,24},{1,5},{5... | collective-permute-start | bytes 1769480 | tf_op jit(solution)/shard_map/ppermute | solution.py:345
  242.4 94.1 %collective-permute-start.72 = (bf16[4,4,48,384]{3,2,1,0:T(8,128)(2,1)}, bf16[4,4,48,384]{3,2,1,0:T(8,128)(2,1)}, u32[]{:S(2)}, u32[]{:S(2)}) collective-permute-start(bf16[4,4,48,384]{3,2,1,0:T(8,128)(2,1)} %dynamic-slice_bitcast_fusion.4), channel_id=1, source_target_pairs={{0,4},{4,0},{8,12},{12,8},{16,20},{20,16},{24,28},{28,24},{1,5},{5... | collective-permute-start | bytes 1769480 | tf_op jit(solution)/shard_map/ppermute | solution.py:345
  243.5 94.6 %collective-permute-start.108 = (bf16[4,96,768]{2,1,0:T(8,128)(2,1)}, bf16[4,96,768]{2,1,0:T(8,128)(2,1)}, u32[]{:S(2)}, u32[]{:S(2)}) collective-permute-start(bf16[4,96,768]{2,1,0:T(8,128)(2,1)} %dynamic-slice_bitcast_fusion.1), channel_id=1, source_target_pairs={{0,4},{4,0},{8,12},{12,8},{16,20},{20,16},{24,28},{28,24},{1,5},{5... | collective-permute-start | bytes 1769480 | tf_op jit(solution)/shard_map/ppermute | solution.py:345
  334.2 64.1 %collective-permute-start.81 = (bf16[4,4,48,384]{3,2,1,0:T(8,128)(2,1)S(1)}, bf16[4,4,48,384]{3,2,1,0:T(8,128)(2,1)S(1)}, u32[]{:S(2)}, u32[]{:S(2)}) collective-permute-start(bf16[4,4,48,384]{3,2,1,0:T(8,128)(2,1)S(1)} %copy-done.74), channel_id=1, source_target_pairs={{0,4},{4,0},{8,12},{12,8},{16,20},{20,16},{24,28},{28,24},{1,5},{5... | collective-permute-start | bytes 1769480 | tf_op jit(solution)/shard_map/ppermute | solution.py:345
  357.9 42.1 %collective-permute-start.90 = (bf16[4,4,48,384]{3,2,1,0:T(8,128)(2,1)S(1)}, bf16[4,4,48,384]{3,2,1,0:T(8,128)(2,1)S(1)}, u32[]{:S(2)}, u32[]{:S(2)}) collective-permute-start(bf16[4,4,48,384]{3,2,1,0:T(8,128)(2,1)S(1)} %copy-done.73), channel_id=1, source_target_pairs={{0,4},{4,0},{8,12},{12,8},{16,20},{20,16},{24,28},{28,24},{1,5},{5... | collective-permute-start | bytes 1769480 | tf_op jit(solution)/shard_map/ppermute | solution.py:345
  358.8 73.5 %collective-permute-start.61 = (bf16[256,1536]{1,0:T(8,128)(2,1)S(1)}, bf16[256,1536]{1,0:T(8,128)(2,1)S(1)}, u32[]{:S(2)}, u32[]{:S(2)}) collective-permute-start(bf16[256,1536]{1,0:T(8,128)(2,1)S(1)} %get-tuple-element.131), channel_id=1, source_target_pairs={{0,1},{1,0},{2,3},{3,2},{4,5},{5,4},{6,7},{7,6},{8,9},{9,8},{10,11... | collective-permute-start | bytes 2359304 | tf_op jit(solution)/shard_map/ppermute | solution.py:345
  415.0 37.5 %collective-permute-start.82 = (bf16[4,2,48,384]{3,2,1,0:T(8,128)(2,1)S(1)}, bf16[4,2,48,384]{3,2,1,0:T(8,128)(2,1)S(1)}, u32[]{:S(2)}, u32[]{:S(2)}) collective-permute-start(bf16[4,2,48,384]{3,2,1,0:T(8,128)(2,1)S(1)} %dynamic-slice_bitcast_fusion.9), channel_id=1, source_target_pairs={{0,8},{4,12},{8,0},{12,4},{16,24},{20,28},{24,16},{28,20},{1,9},{5... | collective-permute-start | bytes 884744 | tf_op jit(solution)/shard_map/ppermute | solution.py:345
  450.8 31.1 %collective-permute-start.112 = (bf16[2,96,768]{2,1,0:T(8,128)(2,1)S(1)}, bf16[2,96,768]{2,1,0:T(8,128)(2,1)S(1)}, u32[]{:S(2)}, u32[]{:S(2)}) collective-permute-start(bf16[2,96,768]{2,1,0:T(8,128)(2,1)S(1)} %pad_maximum_fusion.22), channel_id=1, source_target_pairs={{0,8},{4,12},{8,0},{12,4},{16,24},{20,28},{24,16},{28,20},{1,9},{5... | collective-permute-start | bytes 884744 | tf_op jit(solution)/shard_map/ppermute | solution.py:345
  472.0 43.5 %collective-permute-start.60 = (bf16[256,1536]{1,0:T(8,128)(2,1)S(1)}, bf16[256,1536]{1,0:T(8,128)(2,1)S(1)}, u32[]{:S(2)}, u32[]{:S(2)}) collective-permute-start(bf16[256,1536]{1,0:T(8,128)(2,1)S(1)} %get-tuple-element.130), channel_id=1, source_target_pairs={{0,1},{1,0},{2,3},{3,2},{4,5},{5,4},{6,7},{7,6},{8,9},{9,8},{10,11... | collective-permute-start | bytes 2359304 | tf_op jit(solution)/shard_map/ppermute | solution.py:345
  473.3 42.9 %collective-permute-start.62 = (bf16[256,1536]{1,0:T(8,128)(2,1)S(1)}, bf16[256,1536]{1,0:T(8,128)(2,1)S(1)}, u32[]{:S(2)}, u32[]{:S(2)}) collective-permute-start(bf16[256,1536]{1,0:T(8,128)(2,1)S(1)} %fusion.30), channel_id=1, source_target_pairs={{0,2},{1,3},{2,0},{3,1},{4,6},{5,7},{6,4},{7,5},{8,10},{9,11},{10,... | collective-permute-start | bytes 2359304 | tf_op jit(solution)/shard_map/ppermute | solution.py:345
  516.3 38.7 %collective-permute-start.71 = (bf16[4,4,48,384]{3,2,1,0:T(8,128)(2,1)}, bf16[4,4,48,384]{3,2,1,0:T(8,128)(2,1)}, u32[]{:S(2)}, u32[]{:S(2)}) collective-permute-start(bf16[4,4,48,384]{3,2,1,0:T(8,128)(2,1)} %pad_maximum_fusion.10), channel_id=1, source_target_pairs={{0,4},{4,0},{8,12},{12,8},{16,20},{20,16},{24,28},{28,24},{1,5},{5... | collective-permute-start | bytes 1769480 | tf_op jit(solution)/shard_map/ppermute | solution.py:345
  518.1 49.5 %collective-permute-start.80 = (bf16[4,4,48,384]{3,2,1,0:T(8,128)(2,1)}, bf16[4,4,48,384]{3,2,1,0:T(8,128)(2,1)}, u32[]{:S(2)}, u32[]{:S(2)}) collective-permute-start(bf16[4,4,48,384]{3,2,1,0:T(8,128)(2,1)} %pad_maximum_fusion.11), channel_id=1, source_target_pairs={{0,4},{4,0},{8,12},{12,8},{16,20},{20,16},{24,28},{28,24},{1,5},{5... | collective-permute-start | bytes 1769480 | tf_op jit(solution)/shard_map/ppermute | solution.py:345
  526.0 54.2 %collective-permute-start.89 = (bf16[4,4,48,384]{3,2,1,0:T(8,128)(2,1)}, bf16[4,4,48,384]{3,2,1,0:T(8,128)(2,1)}, u32[]{:S(2)}, u32[]{:S(2)}) collective-permute-start(bf16[4,4,48,384]{3,2,1,0:T(8,128)(2,1)} %pad_maximum_fusion.12), channel_id=1, source_target_pairs={{0,4},{4,0},{8,12},{12,8},{16,20},{20,16},{24,28},{28,24},{1,5},{5... | collective-permute-start | bytes 1769480 | tf_op jit(solution)/shard_map/ppermute | solution.py:345
  529.8 58.3 %collective-permute-start.98 = (bf16[4,4,48,384]{3,2,1,0:T(8,128)(2,1)}, bf16[4,4,48,384]{3,2,1,0:T(8,128)(2,1)}, u32[]{:S(2)}, u32[]{:S(2)}) collective-permute-start(bf16[4,4,48,384]{3,2,1,0:T(8,128)(2,1)} %pad_maximum_fusion.13), channel_id=1, source_target_pairs={{0,4},{4,0},{8,12},{12,8},{16,20},{20,16},{24,28},{28,24},{1,5},{5... | collective-permute-start | bytes 1769480 | tf_op jit(solution)/shard_map/ppermute | solution.py:345
  (199 other events, 2516.0 us)

commit v3 on v2

v3 whole, which is shorter than its diff:
```python
import functools

import jax
import jax.numpy as jnp
from jax import lax
from jax.experimental import pallas as pl
from jax.experimental.pallas import tpu as pltpu
from jax.sharding import PartitionSpec as P

epsilon = 1e-05
bf16, f32 = jnp.bfloat16, jnp.float32
best = lax.Precision.HIGHEST
halo = 16
lanes = 128
head_size = 64


def dot(a, b, ca=1, cb=0, precision=None):
    return lax.dot_general(
        a, b, (((ca,), (cb,)), ((), ())), preferred_element_type=f32, precision=precision
    )


def sigmoid(v):
    return 1.0 / (1.0 + jnp.exp(-v))


def iota(shape, axis):
    return lax.broadcasted_iota(jnp.int32, shape, axis)


def spread(columns, pair):
    first, second = 2 * pair, 2 * pair + 1
    rows = columns.shape[0]
    return jnp.where(
        iota((rows, lanes), 1) < head_size,
        columns[:, first : first + 1],
        columns[:, second : second + 1],
    )


def per_head(total, products, pair):
    rows = products.shape[0]
    lane = iota((rows, lanes), 1)
    low = jnp.sum(jnp.where(lane < head_size, products, 0.0), axis=1, keepdims=True)
    high = jnp.sum(jnp.where(lane < head_size, 0.0, products), axis=1, keepdims=True)
    return total + jnp.where(lane == 2 * pair, low, jnp.where(lane == 2 * pair + 1, high, 0.0))


def in_heads(products, pair):
    rows = jnp.sum(products, axis=1, keepdims=True)
    low, high = jnp.sum(rows[:head_size]), jnp.sum(rows[head_size:])
    lane = iota((1, lanes), 1)
    return jnp.where(lane == 2 * pair, low, jnp.where(lane == 2 * pair + 1, high, 0.0))


def convolved(pc_ref, taps_ref, at):
    x = pc_ref[0, :, at : at + lanes].astype(f32)
    tapped = [pltpu.roll(x, 3 - k, 0)[halo:] for k in range(3)] + [x[halo:]]
    pre = taps_ref[4:5, at : at + lanes]
    for k in range(4):
        pre = pre + tapped[k] * taps_ref[k : k + 1, at : at + lanes]
    return tapped, pre


def pieces_out(out_ref, whole, rows):
    for p in range(out_ref.shape[0]):
        out_ref[p, :rows] = whole[p * rows : (p + 1) * rows]


def pieces_in(ref, rows):
    return jnp.concatenate([ref[p, :rows] for p in range(ref.shape[0])], axis=0)


def block_of(index, size):
    return pl.ds(pl.multiple_of(index * size, size), size)


def columns_of(ref, index, size):
    if size % lanes == 0:
        return ref[:, block_of(index, size)]
    value = ref[:, :size]
    for a in range(1, ref.shape[1] // size):
        value = jnp.where(index == a, ref[:, a * size : (a + 1) * size], value)
    return value


def normalize_kernel(ids_ref, main_ref, small_ref, gain_ref, out_ref, *, owners):
    size = out_ref.shape[2] // owners
    for ref, at in ((small_ref, 0), (main_ref, halo)):
        x = ref[0].astype(f32)
        inv = lax.rsqrt(jnp.mean(x * x, axis=1, keepdims=True) + epsilon)
        for j in range(owners):
            own = ids_ref[1] ^ j
            part = columns_of(ref.at[0], own, size).astype(f32) * inv * columns_of(gain_ref, own, size)
            out_ref[0, at : at + x.shape[0], j * size : (j + 1) * size] = part.astype(bf16)


def weight_kernel(ids_ref, *refs, owners, state, heads):
    rest_ref, out_ref = refs[-2:]
    size = rest_ref.shape[2]
    channels = out_ref.shape[0] - 2 * state - lanes
    n = 0
    for j in range(owners):
        own = slice(j * size, (j + 1) * size)
        if j < 2:
            out_ref[:channels, own] = refs[n][...]
            n += 1
        else:
            half = channels // 2
            for side in range(2):
                out_ref[block_of((ids_ref[0] % 2) ^ side, half), own] = refs[n][...]
                n += 1
        out_ref[channels : channels + 2 * state, own] = rest_ref[j, : 2 * state]
        rows = owners * heads
        pick = iota((lanes, rows), 1) == ids_ref[1] * heads + iota((lanes, rows), 0)
        pick = jnp.where(iota((lanes, rows), 0) < heads, pick.astype(f32), 0.0).astype(bf16)
        out_ref[channels + 2 * state :, own] = dot(pick, rest_ref[j, 2 * state : 2 * state + rows]).astype(bf16)


def input_kernel(ids_ref, bn_ref, gain_ref, tokens_ref, cot_ref, valid_ref, out_ref, *, owners):
    x = tokens_ref[...].astype(f32)
    width = x.shape[1]
    size = width // owners
    inv = lax.rsqrt(jnp.mean(x * x, axis=1, keepdims=True) + epsilon)
    lean = jnp.zeros_like(inv)
    for a in range(owners):
        here = slice(a * size, (a + 1) * size)
        bn = columns_of(bn_ref, ids_ref[1] ^ a, size) * gain_ref[:, here]
        lean = lean + jnp.sum(bn * x[:, here], axis=1, keepdims=True)
    lean = lean * (inv * inv * inv) * (1.0 / width)
    for a in range(owners):
        here = slice(a * size, (a + 1) * size)
        bn = columns_of(bn_ref, ids_ref[1] ^ a, size) * gain_ref[:, here]
        out_ref[:, here] = valid_ref[...] * cot_ref[:, here].astype(f32) + inv * bn - x[:, here] * lean


def of_rows(row, ids_ref, rows, count):
    head = ((ids_ref[0] % count) * rows + iota((rows, lanes), 0)) // head_size
    return jnp.sum(jnp.where(iota((rows, lanes), 1) == head, row, 0.0), axis=1, keepdims=True)


def chain_kernel(ids_ref, in_ref, out_ref, *, rows, count):
    carried = jnp.zeros((rows, lanes), f32)
    for i in range(in_ref.shape[0]):
        out_ref[i] = carried.astype(bf16)
        row = in_ref[i, rows : rows + 1].astype(f32) + in_ref[i, rows + 1 : rows + 2].astype(f32)
        carried = of_rows(row, ids_ref, rows, count) * carried + in_ref[i, :rows].astype(f32)


def back_chain_kernel(ids_ref, in_ref, decay_ref, out_ref, *, rows, count):
    carried = jnp.zeros((rows, lanes), f32)
    for i in reversed(range(in_ref.shape[0])):
        out_ref[i] = carried.astype(bf16)
        row = decay_ref[i, rows : rows + 1].astype(f32) + decay_ref[i, rows + 1 : rows + 2].astype(f32)
        carried = of_rows(row, ids_ref, rows, count) * carried + in_ref[i].astype(f32)


def forward_kernel(pc_ref, taps_ref, rate_ref, act_ref, y_ref, s_ref, lac_ref, dtc_ref, lar_ref, dtr_ref, *, channels, state, rows):
    width = channels + 2 * state
    for at in range(0, width, lanes):
        _, pre = convolved(pc_ref, taps_ref, at)
        act_ref[0, :, at : at + lanes] = (pre * sigmoid(pre)).astype(bf16)
    seg = act_ref.shape[1]
    z = pc_ref[0, halo:, width : width + lanes].astype(f32) + rate_ref[0:1]
    dtc = jnp.maximum(z, 0.0) + jnp.log1p(jnp.exp(-jnp.abs(z)))
    lower = iota((seg, seg), 0) >= iota((seg, seg), 1)
    lac = dot(lower.astype(f32), -dtc * rate_ref[1:2], precision=best)
    tall = lar_ref.shape[1]
    lar, dtr = lac.T[:tall], dtc.T[:tall]
    lac_ref[0], dtc_ref[0], lar_ref[0], dtr_ref[0] = lac, dtc, lar, dtr
    b_rows = act_ref[0, :, channels : channels + state]
    c_rows = act_ref[0, :, channels + state : width]
    both = dot(c_rows, b_rows, 1, 1)
    to_end = jnp.exp(lac[seg - 1 : seg] - lac) * dtc
    states = []
    for pair in range(channels // lanes):
        at = pair * lanes
        values = act_ref[0, :, at : at + lanes]
        parts = []
        for side in range(2):
            h = 2 * pair + side
            mix = jnp.where(lower, jnp.exp(lac[:, h : h + 1] - lar[h : h + 1]), 0.0) * both * dtr[h : h + 1]
            parts.append(dot(mix.astype(bf16), values[:, side * head_size : (side + 1) * head_size]))
        y_ref[0, :, at : at + lanes] = jnp.concatenate(parts, axis=1)
        weighted = (spread(to_end, pair) * values.astype(f32)).astype(bf16)
        states.append(dot(weighted, b_rows, 0, 0).astype(bf16))
    pieces_out(s_ref, jnp.concatenate(states, axis=0), rows)
    whole = jnp.exp(lac[seg - 1 : seg])
    high = whole.astype(bf16).astype(f32)
    row = iota((16, lanes), 0)
    tail = jnp.where(row == 0, high, jnp.where(row == 1, whole - high, 0.0)).astype(bf16)
    for p in range(s_ref.shape[0]):
        s_ref[p, rows:] = tail


def finish_kernel(y_ref, act_ref, lac_ref, sin_ref, gate_ref, bg_ref, vec_ref, y_out, stat_ref, *, channels, state):
    seg = y_ref.shape[1]
    c_rows = act_ref[0, :, channels + state : channels + 2 * state]
    decay = jnp.exp(lac_ref[0])
    first = jnp.zeros((seg, 1), f32)
    second = jnp.zeros((seg, 1), f32)
    for pair in range(channels // lanes):
        at = pair * lanes
        here = slice(at, at + lanes)
        carried = dot(c_rows, sin_ref[0, here], 1, 1)
        y = y_ref[0, :, here] + spread(decay, pair) * carried
        y_out[0, :, here] = y
        gate = gate_ref[0, :, here].astype(f32)
        heads = y + vec_ref[0:1, here] * act_ref[0, :, here].astype(f32)
        gated = heads * gate * sigmoid(gate)
        first = first + jnp.sum(gated * gated, axis=1, keepdims=True)
        second = second + jnp.sum(gated * bg_ref[0, :, here] * vec_ref[1:2, here], axis=1, keepdims=True)
    lane = iota((seg, lanes), 1)
    both = jnp.where(lane == 0, first, jnp.where(lane == 1, second, 0.0))
    stat_ref[0] = both.T[:8]


def norm_kernel(y_ref, act_ref, lac_ref, gate_ref, bg_ref, vec_ref, *refs, channels, state, inner, rows):
    stat_refs, (out_ref, dgate_ref, dy_ref, pos_ref, dsin_ref, dskip_ref) = refs[:-6], refs[-6:]
    seg = y_ref.shape[1]
    stats = sum(ref[0] for ref in stat_refs).T
    states = []
    inv = lax.rsqrt(stats[:, 0:1] * (1.0 / inner) + epsilon)
    lean = inv * inv * inv * (stats[:, 1:2] * (1.0 / inner))
    c_rows = act_ref[0, :, channels + state : channels + 2 * state]
    decay = jnp.exp(lac_ref[0])
    pos = jnp.zeros((seg, lanes), f32)

    @pl.when(pl.program_id(0) == 0)
    def _():
        dskip_ref[...] = jnp.zeros_like(dskip_ref)

    for pair in range(channels // lanes):
        at = pair * lanes
        here = slice(at, at + lanes)
        y = y_ref[0, :, here]
        values = act_ref[0, :, here].astype(f32)
        heads = y + vec_ref[0:1, here] * values
        gate = gate_ref[0, :, here].astype(f32)
        sg = sigmoid(gate)
        gated = heads * gate * sg
        gain = vec_ref[1:2, here]
        out_ref[0, :, here] = (gated * inv * gain).astype(bf16)
        dgated = inv * (bg_ref[0, :, here] * gain) - gated * lean
        dgate_ref[0, :, here] = (dgated * heads * (sg * (1.0 + gate * (1.0 - sg)))).astype(bf16)
        dy = dgated * gate * sg
        dy_ref[0, :, here] = dy
        pos = per_head(pos, dy * y, pair)
        states.append(dot((spread(decay, pair) * dy).astype(bf16), c_rows, 0, 0).astype(bf16))
        dskip_ref[0:1, here] += jnp.sum(dy * values, axis=0, keepdims=True)
    pos_ref[0] = pos
    pieces_out(dsin_ref, jnp.concatenate(states, axis=0), rows)


def backward_kernel(act_ref, dy_ref, lac_ref, lar_ref, dtr_ref, sin_ref, r_ref, dbc_ref, *, channels, state):
    seg = dy_ref.shape[1]
    b_rows = act_ref[0, :, channels : channels + state]
    c_rows = act_ref[0, :, channels + state : channels + 2 * state]
    both = dot(c_rows, b_rows, 1, 1)
    lower = iota((seg, seg), 0) >= iota((seg, seg), 1)
    lac, lar, dtr = lac_ref[0], lar_ref[0], dtr_ref[0]
    decay = jnp.exp(lac)
    dboth = jnp.zeros((seg, seg), f32)
    dc = jnp.zeros((seg, state), f32)
    for pair in range(channels // lanes):
        at = pair * lanes
        here = slice(at, at + lanes)
        values = act_ref[0, :, here]
        dy = dy_ref[0, :, here]
        dyl = dy.astype(bf16)
        parts = []
        for side in range(2):
            h = 2 * pair + side
            own = slice(side * head_size, (side + 1) * head_size)
            weights = jnp.where(lower, jnp.exp(lac[:, h : h + 1] - lar[h : h + 1]), 0.0)
            parts.append(dot((weights * both).astype(bf16), dyl[:, own], 0, 0))
            dboth = dboth + dot(dyl[:, own], values[:, own], 1, 1) * (weights * dtr[h : h + 1])
        r_ref[0, :, here] = jnp.concatenate(parts, axis=1)
        dc = dc + dot((spread(decay, pair) * dy).astype(bf16), sin_ref[0, here])
    dlow = dboth.astype(bf16)
    dbc_ref[0, :, :state] = dot(dlow, c_rows, 0, 0)
    dbc_ref[0, :, state:] = dc + dot(dlow, b_rows)


def rows_grad_kernel(ids_ref, act_ref, lac_ref, dtc_ref, g_ref, dbc_ref, *refs, channels, state):
    out_refs, hold = refs[:-1], refs[-1]
    seg = act_ref.shape[1]
    lac, dtc = lac_ref[0], dtc_ref[0]
    weights = jnp.exp(lac[seg - 1 : seg] - lac) * dtc
    db = dbc_ref[0, :, :state]
    for pair in range(channels // lanes):
        here = slice(pair * lanes, (pair + 1) * lanes)
        db = db + dot((spread(weights, pair) * act_ref[0, :, here].astype(f32)).astype(bf16), g_ref[0, here])
    hold[:state] = db.T
    hold[state:] = dbc_ref[0, :, state:].T
    share = out_refs[0].shape[1]
    for j, out_ref in enumerate(out_refs):
        out_ref[0] = hold[block_of(ids_ref[1] ^ j, share)].astype(bf16)


def share_kernel(ids_ref, pc_ref, taps_ref, *refs, channels, state):
    parts, (dpre_ref, first_ref, dtaps_ref, hold) = refs[:-4], refs[-4:]
    seg = pc_ref.shape[1] - halo
    share = parts[0].shape[1]
    own = block_of(ids_ref[1], share)
    hold[...] = pc_ref[0, :, channels : channels + 2 * state].astype(f32)[halo:].T
    x = hold[own]
    hold[:, :halo] = pc_ref[0, :halo, channels : channels + 2 * state].astype(f32).T
    edge = hold[own, :halo]
    lane = iota((share, seg), 1)
    tapped = []
    for k in range(3):
        value = pltpu.roll(x, 3 - k, 1)
        for t in range(3 - k):
            value = jnp.where(lane == t, edge[:, halo - 3 + k + t : halo - 2 + k + t], value)
        tapped.append(value)
    tapped.append(x)
    pre = taps_ref[:, 4:5] + sum(tapped[k] * taps_ref[:, k : k + 1] for k in range(4))
    sg = sigmoid(pre)
    dpre = sum(ref[0].astype(f32) for ref in parts) * (sg * (1.0 + pre * (1.0 - sg)))

    @pl.when(pl.program_id(0) == 0)
    def _():
        dtaps_ref[...] = jnp.zeros_like(dtaps_ref)

    lane = iota((share, lanes), 1)
    total = jnp.zeros((share, lanes), f32)
    for k in range(5):
        column = jnp.sum(dpre * tapped[k] if k < 4 else dpre, axis=1, keepdims=True)
        total = jnp.where(lane == k, column, total)
    dtaps_ref[...] += total
    rows = jnp.concatenate([dpre, jnp.zeros((lanes - share, seg), f32)], axis=0).T
    dpre_ref[0] = rows
    first_ref[0] = rows[:8]


def carry_kernel(pc_ref, taps_ref, rate_ref, act_ref, dy_ref, r_ref, pos_ref, lac_ref, dtc_ref, g_ref, sin_ref, s_ref, vec_ref, dpre_ref, first_ref, dstep_ref, dtaps_ref, drate_ref, *, channels, state, rows):
    seg = dy_ref.shape[1]
    width = channels + 2 * state
    b_rows = act_ref[0, :, channels : channels + state]
    lac, dtc = lac_ref[0], dtc_ref[0]
    last = lac[seg - 1 : seg]
    to_last = jnp.exp(last - lac)
    neg = jnp.zeros((seg, lanes), f32)
    through = jnp.zeros((1, lanes), f32)
    local = jnp.zeros((1, lanes), f32)
    states = pieces_in(s_ref, rows)

    @pl.when(pl.program_id(0) == 0)
    def _():
        dtaps_ref[...] = jnp.zeros_like(dtaps_ref)
        drate_ref[...] = jnp.zeros_like(drate_ref)

    for pair in range(channels // lanes):
        at = pair * lanes
        here = slice(at, at + lanes)
        grad = g_ref[0, here]
        values = act_ref[0, :, here].astype(f32)
        r = r_ref[0, :, here] + spread(to_last, pair) * dot(b_rows, grad, 1, 1)
        neg = per_head(neg, values * r, pair)
        wide = grad.astype(f32)
        through = through + in_heads(wide * sin_ref[0, here].astype(f32), pair)
        local = local + in_heads(wide * states[here].astype(f32), pair)
        tapped, pre = convolved(pc_ref, taps_ref, at)
        sg = sigmoid(pre)
        dpre = (spread(dtc, pair) * r + vec_ref[0:1, here] * dy_ref[0, :, here]) * (sg * (1.0 + pre * (1.0 - sg)))
        dpre_ref[0, :, here] = dpre
        for k in range(4):
            dtaps_ref[k : k + 1, here] += jnp.sum(dpre * tapped[k], axis=0, keepdims=True)
        dtaps_ref[4:5, here] += jnp.sum(dpre, axis=0, keepdims=True)
    first_ref[0] = dpre_ref[0, :8]
    seed = jnp.exp(last) * through + local
    upper = (iota((seg, seg), 0) <= iota((seg, seg), 1)).astype(f32)
    q = dot(upper, pos_ref[0] - dtc * neg, precision=best) + seed
    rates = rate_ref[1:2]
    z = pc_ref[0, halo:, width : width + lanes].astype(f32) + rate_ref[0:1]
    draw = (neg - rates * q) * sigmoid(z)
    dstep_ref[0] = draw.astype(bf16)
    drate_ref[0:1] += jnp.sum(draw, axis=0, keepdims=True)
    drate_ref[1:2] += jnp.sum(q * (-dtc * rates), axis=0, keepdims=True)


def returned_kernel(dpre_ref, dshare_ref, next_ref, taps_ref, dstep_ref, out_ref, *, share, heads):
    seg, width = dpre_ref.shape[1:]
    for at in range(0, width + lanes, lanes):
        here = slice(at, at + lanes)
        own = dpre_ref[0, :, here] if at < width else dshare_ref[0]
        x = jnp.concatenate([own, next_ref[0, :, here]], axis=0)
        total = x[:seg] * taps_ref[3:4, here]
        for k in range(3):
            by = 3 - k
            total = total + pltpu.roll(x, seg + 8 - by, 0)[:seg] * taps_ref[k : k + 1, here]
        if at == width:
            step = pltpu.roll(dstep_ref[0].astype(f32), share, 1)
            lane = iota((seg, lanes), 1)
            total = jnp.where(lane < share, total, jnp.where(lane < share + heads, step, 0.0))
        out_ref[0, :, here] = total.astype(bf16)


def call(kernel, grid, ins, outs, name, ids=None, flops=0, scratch=(), far=False, **statics):
    def spec(shape, index):
        if index is None:
            return pl.BlockSpec(tuple(shape), lambda s, *i: (0,) * len(shape))
        block, at = index
        return pl.BlockSpec((block,) + tuple(shape[1:]), lambda s, *i: (at(s, *i),) + (0,) * (len(shape) - 1))

    moved = sum(a.size * a.dtype.itemsize for a, _ in ins)
    for shape, dtype, _ in outs:
        size = 1
        for d in shape:
            size *= d
        moved += size * jnp.dtype(dtype).itemsize
    return pl.pallas_call(
        functools.partial(kernel, **statics),
        grid_spec=pltpu.PrefetchScalarGridSpec(
            num_scalar_prefetch=0 if ids is None else 1,
            grid=(grid,),
            in_specs=[spec(a.shape, index) for a, index in ins],
            out_specs=[spec(shape, index) for shape, _, index in outs],
            scratch_shapes=list(scratch),
        ),
        out_shape=[(pltpu.HBM if far else jax.ShapeDtypeStruct)(shape, dtype) for shape, dtype, _ in outs],
        compiler_params=pltpu.CompilerParams(vmem_limit_bytes=24 << 20),
        cost_estimate=pl.CostEstimate(flops=flops, bytes_accessed=moved, transcendentals=0),
        name=name,
    )(*([] if ids is None else [ids]), *[pltpu.with_memory_space_constraint(a, pltpu.HBM) if far else a for a, _ in ins])


each = (1, lambda s, *i: s)


def swap(value, axis, by):
    count = lax.axis_size(axis)
    return lax.ppermute(value, axis, [(i, i ^ by) for i in range(count)])


def all_slots(value, axis, first=None):
    count = lax.axis_size(axis)
    by = count // 2
    offsets = [0]
    while by:
        value = jnp.concatenate([value, swap(value, axis, by)], axis=0)
        if first is not None:
            value, first = tied(value, first), None
        offsets += [j ^ by for j in offsets]
        by //= 2
    size = value.shape[0] // count
    where = [offsets.index(j) for j in range(count)]
    return jnp.concatenate([value[i * size : (i + 1) * size] for i in where], axis=0)


def blocks_turned(value, by, owners):
    size = value.shape[-1] // owners
    return jnp.concatenate([value[..., (j ^ by) * size : ((j ^ by) + 1) * size] for j in range(owners)], axis=-1)


def to_owner(value, axis, turn=False):
    count = lax.axis_size(axis)
    by = 1
    while by < count:
        value = value.reshape((value.shape[0] // 2, 2) + value.shape[1:])
        other = swap(value[:, 1].astype(bf16), axis, by).astype(f32)
        value = value[:, 0] + (blocks_turned(other, by, count) if turn else other)
        by *= 2
    return value[0]


def halved(value, axis, by):
    value = value.reshape((value.shape[0] // 2, 2) + value.shape[1:])
    bit = (lax.axis_index(axis) // by) % 2
    keep = lax.dynamic_index_in_dim(value, bit, 1, False)
    give = lax.dynamic_index_in_dim(value, 1 - bit, 1, False)
    return (keep.astype(f32) + swap(give, axis, by).astype(f32)).astype(bf16)


def halved_from(value, axis, by):
    while value.shape[0] > 1:
        value = halved(value, axis, by)
        by *= 2
    return value[0]


def tied(value, *others):
    return lax.optimization_barrier((value, others))[0]


def gather_step(value, axis, by):
    return jnp.concatenate([value, swap(value, axis, by)], axis=0)


def gathered(value, axis, by):
    while by:
        value = gather_step(value, axis, by)
        by //= 2
    return value


def reversed_bits(j, count):
    out, by = 0, 1
    while by < count:
        out = out * 2 + (j // by) % 2
        by *= 2
    return out


def traded(value, axis):
    count = lax.axis_size(axis)
    size = value.shape[-1] // count
    parts = [value[:, j * size : (j + 1) * size] for j in range(count)]
    return jnp.stack([swap(part, axis, j) if j else part for j, part in enumerate(parts)])


def exchange(value, axis):
    return lax.all_to_all(value, axis, 0, 0)


def in_order(parts, index):
    stacked = jnp.stack(parts)
    return jnp.concatenate([lax.dynamic_index_in_dim(stacked, index ^ a, 0) for a in range(len(parts))])


def assemble_kernel(ids_ref, gate_ref, *refs, share, heads):
    conv_refs, (weight_ref, out_ref, tail_ref, sum_ref) = refs[:-4], refs[-4:]
    step = pl.program_id(0)
    count, owners = gate_ref.shape[:2]
    channels = out_ref.shape[0]

    def place_of(q):
        return reversed_bits(ids_ref[0] ^ q, count)

    @pl.when(step == 0)
    def _():
        sum_ref[...] = jnp.zeros_like(sum_ref)

    def put(at, value):
        size = value.shape[0]
        out_ref[at : at + size] = value
        sum_ref[0:1] += jnp.sum(value * weight_ref[at : at + size].astype(f32), axis=0, keepdims=True)

    def parts():
        at = 0
        for ref in conv_refs:
            for q in range(count):
                yield at, ref, q
                at += ref.shape[2]

    @pl.when(step < owners)
    def _():
        rows = gate_ref.shape[2]
        for q in range(count):
            put(q * rows, gate_ref[place_of(q), ids_ref[1] ^ step].astype(f32))

    @pl.when(step // owners == 1)
    def _():
        for at, ref, q in parts():
            size = min(ref.shape[2], channels - at)
            if size > 0:
                put(at, ref[place_of(q), ids_ref[1] ^ (step % owners), :size].astype(f32))

    @pl.when(step == 2 * owners)
    def _():
        for a in range(owners):
            found = []
            for at, ref, q in parts():
                skip = max(0, channels - at)
                if skip < ref.shape[2]:
                    found.append(ref[place_of(q), ids_ref[1] ^ a].astype(f32)[skip:])
            value = jnp.concatenate(found, axis=0)
            tail_ref[a] = value
            put(a * share, value[:share])
            put(owners * share + a * heads, value[share : share + heads])


def rows_kernel(ids_ref, *refs, parts):
    bufs, (weight_ref, out_ref, sum_ref) = refs[: len(parts)], refs[len(parts) :]
    total = jnp.zeros((out_ref.shape[0], 1), f32)
    for ref, (start, size) in zip(bufs, parts, strict=True):
        value = ref[0].astype(f32)
        out_ref[:, start : start + size] = value
        total = total + jnp.sum(value * weight_ref[:, start : start + size].astype(f32), axis=1, keepdims=True)
    sum_ref[...] = total


def per_device(tokens, lengths, norm_gain, in_weight, conv_weight, conv_bias, dt_bias, decay_log, skip_gain, gated_gain, out_weight, cotangent):
    nf, nq = lax.axis_size("fsdp"), lax.axis_size("seq")
    me, place = lax.axis_index("fsdp"), lax.axis_index("seq")
    _, seg, width = tokens.shape
    rows = in_weight.shape[0]
    channels = out_weight.shape[0]
    inner = channels * nf
    heads = dt_bias.shape[0]
    conv_own = conv_weight.shape[1]
    state = (conv_own * nf - inner) // 2
    share = 2 * state // nf
    slots = nf

    ids = jnp.stack([place, me]).astype(jnp.int32)
    per_slot = nq // slots
    piece = channels // per_slot

    weight = in_weight.T
    half, side = channels // 2, place % 2
    got = []
    for j in range(nf):
        start = inner + (me ^ j) * channels
        if j < 2:
            give = lax.dynamic_slice_in_dim(weight, start, channels, 0)
            got.append(swap(give, "fsdp", j) if j else give)
        else:
            mine = swap(lax.dynamic_slice_in_dim(weight, start + side * half, half, 0), "fsdp", j)
            got += [mine, swap(mine, "seq", 1)]
    own_tokens = tied(tokens, got[2::2])
    x_main = all_slots(own_tokens, "fsdp", got[3::2])
    before = lax.ppermute(tokens[0, seg - 3 :], "seq", [(i, i + 1) for i in range(nq - 1)])

    def padded(rows_):
        return jnp.pad(rows_, ((0, 0), (0, width - rows_.shape[1])))

    small = jnp.concatenate(
        [padded(conv_weight), padded(conv_bias[None]), padded(norm_gain[None]), jnp.zeros((7, width), bf16), before], axis=0
    )
    x_small = all_slots(small[None], "fsdp")
    listed = [x_small[j] for j in range(nf)]
    norm_all = in_order([part[5, :rows] for part in listed], me).astype(f32).reshape(1, width)
    taps_all = in_order([part[:5, :conv_own] for part in listed], me).astype(f32)
    taps_all = taps_all.reshape(nf, 5, conv_own).transpose(1, 0, 2).reshape(5, -1)
    taps_all = jnp.pad(taps_all, ((0, 3), (0, 0)))
    taps = jnp.concatenate([lax.dynamic_slice_in_dim(taps_all, me * channels, channels, 1), taps_all[:, inner:]], axis=1)
    taps_share = lax.dynamic_slice_in_dim(taps_all, inner + me * share, share, 1)
    rate = jnp.stack([dt_bias.astype(f32), jnp.exp(decay_log.astype(f32))])
    rate = jnp.pad(rate, ((0, 6), (0, lanes - heads)))
    vec = jnp.stack([jnp.repeat(skip_gain.astype(f32), head_size), gated_gain.astype(f32)])
    vec = jnp.pad(vec, ((0, 6), (0, 0)))

    rest = all_slots(weight[2 * inner :][None], "fsdp")
    cw = channels + 2 * state
    (w_conv,) = call(
        weight_kernel,
        1,
        [(part, None) for part in got] + [(rest, None)],
        [((cw + lanes, width), bf16, None)],
        "weights",
        ids=ids,
        owners=nf,
        state=state,
        heads=heads,
    )

    (normed,) = call(
        normalize_kernel,
        slots,
        [(x_main, each), (x_small, each), (norm_all, None)],
        [((slots, halo + seg, width), bf16, each)],
        "normalize",
        ids=ids,
        owners=nf,
    )
    inputs = tokens[0].astype(f32)
    valid = (place * seg + jnp.arange(seg) < lengths[0]).astype(f32)[:, None]
    upstream = valid * cotangent[0].astype(f32)

    gives = [lax.dynamic_slice_in_dim(weight, (me ^ j) * channels, channels, 0) for j in range(nf)]
    gives, later = tied((gives, upstream.astype(bf16)), got[-1])
    w_gate = jnp.concatenate([swap(g, "fsdp", j) if j else g for j, g in enumerate(gives)], axis=1)
    back_branch = all_slots(later[None], "fsdp")

    def project(x, w):
        return lax.dot_general(x, w, (((2,), (1,)), ((), ())), preferred_element_type=f32)

    pc = project(normed, w_conv).astype(bf16)
    main = normed[:, halo:]
    tall = 16
    statics = dict(channels=channels, state=state)
    turned = (per_slot, lambda s, *i: s)
    act, y_local, s_local, lac, dtc, lar, dtr = call(
        forward_kernel,
        slots,
        [(pc, each), (taps, None), (rate, None)],
        [
            ((slots, seg, cw), bf16, each),
            ((slots, seg, channels), f32, each),
            ((nq, piece + 16, state), bf16, turned),
            ((slots, seg, lanes), f32, each),
            ((slots, seg, lanes), f32, each),
            ((slots, tall, seg), f32, each),
            ((slots, tall, seg), f32, each),
        ],
        "forward",
        far=True,
        flops=2 * slots * seg * seg * channels,
        rows=piece,
        **statics,
    )

    came = exchange(s_local, "seq")
    (reached,) = call(
        chain_kernel, 1, [(came, None)], [((nq, piece, state), bf16, None)], "chain", ids=ids, rows=piece, count=per_slot
    )
    s_in = exchange(reached, "seq").reshape(slots, channels, state)

    gate = project(main, w_gate).astype(bf16)
    bg = lax.dot_general(back_branch, out_weight, (((2,), (1,)), ((), ())), preferred_element_type=f32)
    y, stats = call(
        finish_kernel,
        slots,
        [(y_local, each), (act, each), (lac, each), (s_in, each), (gate, each), (bg, each), (vec, None)],
        [((slots, seg, channels), f32, each), ((slots, 8, seg), f32, each)],
        "finish",
        far=True,
        **statics,
    )
    shares = [(swap(stats, "fsdp", j) if j else stats, (1, lambda s, j=j: s ^ j)) for j in range(nf)]
    gated_out, dgate, dy, pos, dsin, dskip = call(
        norm_kernel,
        slots,
        [(y, each), (act, each), (lac, each), (gate, each), (bg, each), (vec, None)] + shares,
        [
            ((slots, seg, channels), bf16, each),
            ((slots, seg, channels), bf16, each),
            ((slots, seg, channels), f32, each),
            ((slots, seg, lanes), f32, each),
            ((nq, piece, state), bf16, turned),
            ((8, channels), f32, None),
        ],
        "norm",
        far=True,
        inner=inner,
        rows=piece,
        **statics,
    )

    def grad_of(dz, x):
        return lax.dot_general(dz, x, (((0, 1), (0, 1)), ((), ())), preferred_element_type=f32).astype(bf16)

    def cut(value):
        size = value.shape[-1] // 2
        return [value] if size // nq % 8 else [value[..., :size], value[..., size:]]

    def pieces(g):
        return g.reshape((nq, g.shape[0] // nq) + g.shape[1:])

    back_came = exchange(dsin, "seq")
    out_sum = lax.psum_scatter(pieces(grad_of(gated_out, back_branch)), "seq", scatter_dimension=0)
    gate_sum = halved(pieces(grad_of(dgate, main)), "seq", 1)
    back_came, gate_sum = lax.optimization_barrier((back_came, gate_sum))
    gate_sum = halved(gate_sum, "seq", 2)
    (reached,) = call(
        back_chain_kernel,
        1,
        [(back_came, None), (came, None)],
        [((nq, piece, state), bf16, None)],
        "back_chain",
        ids=ids,
        rows=piece,
        count=per_slot,
    )
    g_end = exchange(reached, "seq").reshape(slots, channels, state)
    g_end, gate_sum = lax.optimization_barrier((g_end, gate_sum))
    gate_sum = halved_from(gate_sum, "seq", 4)

    r_local, dbc = call(
        backward_kernel,
        slots,
        [(act, each), (dy, each), (lac, each), (lar, each), (dtr, each), (s_in, each)],
        [((slots, seg, channels), f32, each), ((slots, seg, 2 * state), f32, each)],
        "backward",
        far=True,
        flops=4 * slots * seg * seg * channels,
        **statics,
    )
    d_shares = call(
        rows_grad_kernel,
        slots,
        [(act, each), (lac, each), (dtc, each), (g_end, each), (dbc, each)],
        [((slots, share, seg), bf16, each)] * nf,
        "rows_grad",
        ids=ids,
        scratch=[pltpu.VMEM((2 * state, seg), f32)],
        **statics,
    )
    d_shares = [(swap(d, "fsdp", j) if j else d, (1, lambda s, i, j=j: s ^ j)) for j, d in enumerate(d_shares)]
    r_local, gate_sum = lax.optimization_barrier((r_local, gate_sum))
    gate_sum = traded(gate_sum, "fsdp")
    dpre, first, dstep, dtaps, drate = call(
        carry_kernel,
        slots,
        [
            (pc, each), (taps, None), (rate, None), (act, each), (dy, each), (r_local, each), (pos, each), (lac, each),
            (dtc, each), (g_end, each), (s_in, each), (s_local, turned), (vec, None),
        ],
        [
            ((slots, seg, channels), f32, each),
            ((slots, 8, channels), f32, each),
            ((slots, seg, lanes), bf16, each),
            ((8, channels), f32, None),
            ((8, lanes), f32, None),
        ],
        "carry",
        far=True,
        rows=piece,
        **statics,
    )
    dstep, gate_sum = lax.optimization_barrier((dstep, gate_sum))
    pc_later, dpre = lax.optimization_barrier((pc, dpre))
    gate_sum = gather_step(gate_sum[None], "seq", nq // 2)
    dpre_share, first_share, dtaps_share = call(
        share_kernel,
        slots,
        [(pc_later, each), (taps_share.T, None)] + d_shares,
        [((slots, seg, lanes), f32, each), ((slots, 8, lanes), f32, each), ((share, lanes), f32, None)],
        "share",
        ids=ids,
        scratch=[pltpu.VMEM((2 * state, seg), f32)],
        **statics,
    )
    behind = [(i, i - 1) for i in range(1, nq)]
    after = lax.ppermute(jnp.concatenate([first, first_share], axis=2), "seq", behind)
    after, gate_sum = lax.optimization_barrier((after, gate_sum))
    gate_sum = gather_step(gate_sum, "seq", nq // 4)
    taps_back = jnp.concatenate([taps[:, :channels], jnp.pad(taps_share, ((0, 0), (0, lanes - share)))], axis=1)
    (dconv,) = call(
        returned_kernel,
        slots,
        [(dpre, each), (dpre_share, each), (after, each), (taps_back, None), (dstep, each)],
        [((slots, seg, channels + lanes), bf16, each)],
        "returned",
        share=share,
        heads=heads,
    )

    dconv, gate_sum = lax.optimization_barrier((dconv, gate_sum))
    gate_bufs = [gathered(gate_sum, "seq", nq // 8)]

    per = channels // rows
    head_rows = jnp.stack([drate[0, :heads], drate[1, :heads], jnp.sum(dskip[0].reshape(heads, head_size), axis=1)])
    block = jnp.concatenate(
        [
            dtaps[:5].reshape(5 * per, rows),
            jnp.pad(dtaps_share[:, :5].T, ((0, 0), (0, rows - share))),
            jnp.pad(head_rows, ((0, 0), (0, rows - heads))),
        ],
        axis=0,
    )
    extra = block.shape[0]
    block = jnp.tile(block, (1, nf)).astype(bf16)
    conv_grads = [grad_of(part, main) for part in cut(dconv)]
    spare = channels + share + heads - sum(g.shape[0] for g in conv_grads[:-1])
    conv_grads[-1] = lax.dynamic_update_slice_in_dim(conv_grads[-1], block, spare, 0)

    def shared(g):
        return gathered(traded(g, "fsdp")[None], "seq", nq // 2)

    out_unit = channels // nq
    out_parts = [lax.all_gather(out_sum, "seq")]
    conv_sums = [halved_from(pieces(g), "seq", 1) for g in conv_grads]
    conv_sums, out_parts = lax.optimization_barrier((conv_sums, out_parts))
    conv_bufs = [shared(g) for g in conv_sums]
    place_of = jnp.stack([reversed_bits(place ^ q, nq) for q in range(nq)])
    if all(buf.shape[2] % 8 == 0 for buf in gate_bufs + conv_bufs):
        g_in, tail, norm_sum = call(
            assemble_kernel,
            2 * nf + 1,
            [(buf, None) for buf in gate_bufs + conv_bufs] + [(weight, (channels, lambda s, i: s))],
            [
                (weight.shape, f32, (channels, lambda s, i: s)),
                ((nf, lanes, rows), f32, None),
                ((8, rows), f32, None),
            ],
            "assemble",
            ids=ids,
            share=share,
            heads=heads,
        )
        norm_sum = norm_sum[0]
    else:
        order = me ^ jnp.arange(nf)

        def natural(bufs):
            bufs = [buf[place_of][:, order].astype(f32).transpose(1, 0, 2, 3).reshape(nf, -1, rows) for buf in bufs]
            return jnp.concatenate(bufs, axis=1)

        gate_all, conv_all = natural(gate_bufs), natural(conv_bufs)
        tail = conv_all[:, channels:]
        joined = [gate_all.reshape(inner, rows), conv_all[:, :channels].reshape(inner, rows)]
        joined += [tail[:, :share].reshape(nf * share, rows), tail[:, share : share + heads].reshape(nf * heads, rows)]
        g_in = jnp.concatenate(joined, axis=0)
        norm_sum = jnp.sum(g_in * weight.astype(f32), axis=0)
    if out_unit % 16 == 0:
        sizes = [part.shape[-1] for part in out_parts]
        g_out, gated_sum = call(
            rows_kernel,
            nq,
            [(part, (1, lambda s, i: s)) for part in out_parts] + [(out_weight, (out_unit, lambda s, i: s))],
            [(out_weight.shape, f32, (out_unit, lambda s, i: s)), ((channels, 1), f32, (out_unit, lambda s, i: s))],
            "rows",
            ids=ids,
            parts=[(sum(sizes[:i]), size) for i, size in enumerate(sizes)],
        )
        gated_sum = gated_sum[:, 0]
    else:
        g_out = jnp.concatenate([part.astype(f32).reshape(channels, -1) for part in out_parts], axis=1)
        gated_sum = jnp.sum(g_out * out_weight.astype(f32), axis=1)

    norm_grad = norm_sum / norm_gain.astype(f32)
    gated_grad = gated_sum / gated_gain.astype(f32)

    got = tail[:, share + heads : share + heads + extra]
    tap_grads = jnp.concatenate(
        [
            got[:, : 5 * per].reshape(nf, 5, channels).transpose(1, 0, 2).reshape(5, inner),
            got[:, 5 * per : 5 * per + 5, :share].transpose(1, 0, 2).reshape(5, 2 * state),
        ],
        axis=1,
    )
    tap_grads = lax.dynamic_slice_in_dim(tap_grads, me * conv_own, conv_own, 1)
    head_grads = lax.dynamic_index_in_dim(got, me, 0, False)[5 * per + 5 :, :heads]

    branch = lax.dot_general(gated_out, out_weight, (((2,), (0,)), ((), ())), preferred_element_type=f32)
    branch = to_owner(branch, "fsdp")
    mixed = (valid * (inputs + branch)).astype(bf16)

    w_share = lax.dynamic_slice_in_dim(w_conv, channels + me * share, share, 0)
    w_last = jnp.concatenate([w_share, w_conv[cw : cw + lanes - share]], axis=0)

    def back(dz, w):
        return lax.dot_general(dz, w, (((2,), (0,)), ((), ())), preferred_element_type=f32)

    bn = back(dgate, w_gate) + back(dconv[..., :channels], w_conv[:channels]) + back(dconv[..., channels:], w_last)
    bn = to_owner(bn, "fsdp", turn=True)
    (input_grad,) = call(
        input_kernel,
        1,
        [(bn, None), (norm_all, None), (tokens[0], None), (cotangent[0], None), (valid, None)],
        [((seg, width), f32, None)],
        "input",
        ids=ids,
        owners=nf,
    )
    return (
        mixed[None],
        input_grad[None],
        norm_grad,
        g_in.T,
        tap_grads[:4],
        tap_grads[4],
        head_grads[0],
        head_grads[1],
        head_grads[2],
        gated_grad,
        g_out,
    )


def solution(mesh):
    whole, rows = P("fsdp", "seq", None), P("fsdp", None)
    one, columns = P("fsdp"), P(None, "fsdp")
    return jax.shard_map(
        per_device,
        mesh=mesh,
        in_specs=(whole, one, one, rows, columns, one, one, one, one, one, rows, whole),
        out_specs=(whole, whole, one, rows, columns, one, one, one, one, one, rows),
        check_vma=False,
    )
```

time: 622 us -> 538 us (0.86)
  starting transfers between devices: 152 us -> 76.7 us
  local copies, waits for them, and re-layouts: 82.5 us -> 48.7 us
  Pallas kernels: 73 us -> 102 us
  waiting for transfers between devices: 223 us -> 194 us
  between operations: 4.24 us -> 16.6 us
  matrix products: 42.4 us -> 51.6 us
    ppermute x117 -> x53, starting transfers between devices: 145 us -> 44.3 us  [swap(): return lax.ppermute(value, axis, [(i, i ^ by) for i in range(count)])]
    ppermute x117 -> x53, waiting for transfers between devices: 213 us -> 177 us  [swap(): return lax.ppermute(value, axis, [(i, i ^ by) for i in range(count)])]
    pallas_call x13 -> x15, Pallas kernels: 73 us -> 102 us  [call(): pl.pallas_call(functools.partial(kernel, **statics), grid_spec=pltpu.Pref...]
    all_to_all x0 -> x4, starting transfers between devices: none -> 17.6 us  [exchange(): return lax.all_to_all(value, axis, 0, 0)]
    unnamed x213 -> x164, local copies, waits for them, and re-layouts: 34.9 us -> 18 us
    all_to_all x0 -> x4, waiting for transfers between devices: none -> 12.5 us  [exchange(): return lax.all_to_all(value, axis, 0, 0)]
    dynamic_slice x15 -> x3, local copies, waits for them, and re-layouts: 17.7 us -> 6.67 us  [the longest x1 3.93 us: per_device(): lax.dynamic_slice_in_dim(weight, (me ^ j) * channels, channels, 0)]
    reduce_scatter x0 -> x1, starting transfers between devices: none -> 9.9 us  [per_device(): lax.psum_scatter(pieces(grad_of(gated_out, back_branch)), 'seq', scatter_...]
  transfers between devices with their start and end apart: 120 -> 61, of which waited for: 53 -> 26; matrix products, arithmetic and copies ran while one was open for 19% -> 21% of each run, Pallas kernels for 9% -> 14%
where the time goes in v3:
time: 538 us; the launch traced here: 529 us
  waiting for transfers between devices  194 us (36%)
  Pallas kernels  102 us (19%)
  starting transfers between devices  76.7 us (14%)
  matrix products  51.6 us (10%)
  local copies, waits for them, and re-layouts  48.7 us (9%)
  other arithmetic  39.3 us (7%)
  between operations  16.6 us (3%)
    ppermute x53, waiting for transfers between devices, swap(): return lax.ppermute(value, axis, [(i, i ^ by) for i in range(count)])  177 us
    pallas_call x15, Pallas kernels, call(): pl.pallas_call(functools.partial(kernel, **statics), grid_spec=pltpu.Pref...  102 us
    ppermute x53, starting transfers between devices, swap(): return lax.ppermute(value, axis, [(i, i ^ by) for i in range(count)])  44.3 us
    unnamed x164, local copies, waits for them, and re-layouts  18 us
    all_to_all x4, starting transfers between devices, exchange(): return lax.all_to_all(value, axis, 0, 0)  17.6 us
    dot_general x4, matrix products, grad_of(): lax.dot_general(dz, x, (((0, 1), (0, 1)), ((), ())), preferred_element_ty...  16.8 us
    dot_general x3, matrix products, back(): lax.dot_general(dz, w, (((2,), (0,)), ((), ())), preferred_element_type=f32)  12.8 us
    all_to_all x4, waiting for transfers between devices, exchange(): return lax.all_to_all(value, axis, 0, 0)  12.5 us
  transfers between devices with their start and end apart: 61, of which 26 were waited for; matrix products, arithmetic and copies ran while one was open for 21% of the time, Pallas kernels for 14%

profile of v3, /device:TPU:0, one launch (start us, length us, event | category | flops | bytes accessed | tf_op | source)
XLA Modules:
  0.0 528.6 jit_solution(9710867759111575169)
XLA Ops:
  38.6 15.5 %collective-permute-done.2 = bf16[1,256,1536]{2,1,0:T(8,128)(2,1)S(1)} collective-permute-done((bf16[1,256,1536]{2,1,0:T(8,128)(2,1)S(1)}, bf16[1,256,1536]{2,1,0:T(8,128)(2,1)S(1)}, u32[]{:S(2)}, u32[]{:S(2)}) %collective-permute-start.2) | collective-permute-done | bytes 786464 | tf_op jit(solution)/shard_map/ppermute | solution.py:435
  64.5 5.9 %convolution_convert_fusion.pc_ref = bf16[4,272,1152]{2,1,0:T(8,128)(2,1)} fusion(bf16[4,272,1536]{2,1,0:T(8,128)(2,1)S(1)} %normalize.1, bf16[1152,1536]{1,0:T(8,128)(2,1)S(1)} %weights.1), kind=kOutput, calls=%fused_computation.3 | convolution fusion | flops 3851624448 | bytes 9388032 | tf_op jit(solution)/shard_map/dot_general | solution.py:669
  70.3 14.5 %forward.1 = (bf16[4,256,1024]{2,1,0:T(8,128)(2,1)}, f32[4,256,768]{2,1,0:T(8,128)}, bf16[8,400,128]{2,1,0:T(8,128)(2,1)}, f32[4,256,128]{2,1,0:T(8,128)}, f32[4...) custom-call(bf16[4,272,1152]{2,1,0:T(8,128)(2,1)} %convolution_convert_fusion.pc_ref, ...), custom_call_target="tpu_custom_call" | custom-call | flops 402653184 | bytes 9785344 | tf_op jit(solution)/shard_map/forward/pallas_call | solution.py:414
  84.8 6.0 %all-to-all-start = ((bf16[8,400,128]{2,1,0:T(8,128)(2,1)}), bf16[8,400,128]{2,1,0:T(8,128)(2,1)}, u32[]{:S(2)}, u32[]{:S(2)}) async-start(bf16[8,400,128]{2,1,0:T(8,128)(2,1)} %get-tuple-element.74.s_ref), calls=%async_computation | async-start | bytes 1638400 | tf_op jit(solution)/shard_map/all_to_all | solution.py:515
  103.7 8.4 %all-to-all-done.in_ref.decay_ref = bf16[8,400,128]{2,1,0:T(8,128)(2,1)} async-done(((bf16[8,400,128]{2,1,0:T(8,128)(2,1)}), bf16[8,400,128]{2,1,0:T(8,128)(2,1)}, u32[]{:S(2)}, u32[]{:S(2)}) %all-to-all-start) | async-done | bytes 819232 | tf_op jit(solution)/shard_map/all_to_all | solution.py:515
  121.3 6.3 %fusion.16.gate_ref = bf16[4,256,768]{2,1,0:T(8,128)(2,1)} fusion(bf16[4,272,1536]{2,1,0:T(8,128)(2,1)} %copy-done.9, bf16[768,384]{1,0:T(8,128)(2,1)} %collective-permute-done.14, bf16[768,384]{1,0:T(8,128)(2,1)} %collective-permute-done.13, bf16[768,384]{1,0:T(8,128)(2,1)} %collective-permute-done.12, bf16[768,384]{1,0:T(8,128)(2,1)} %get-tuple-element.75), kind=kOutput, calls=%fused_computation.32 | convolution fusion | flops 2426142720 | bytes 7077888 | tf_op jit(solution)/shard_map/dot_general | solution.py:669
  130.5 5.8 %fusion.9.bg_ref = f32[4,256,768]{2,1,0:T(8,128)} fusion(bf16[768,1536]{1,0:T(8,128)(2,1)S(1)} %copy-done.16, bf16[1,256,1536]{2,1,0:T(8,128)(2,1)S(1)} %get-tuple-element.144, bf16[1,256,1536]{2,1,0:T(8,128)(2,1)} %collective-permute-done.15, bf16[1,256,1536]{2,1,0:T(8,128)(2,1)S(1)} %get-tuple-element.143, bf16[1,256,1536]{2,1,0:T(8,128)(2,1)} %bitcast.29), kind=kOutput, calls=%fused_computation.25 | convolution fusion | flops 2420637696 | bytes 8650752 | tf_op jit(solution)/shard_map/dot_general | solution.py:703
  140.3 8.9 %finish.1 = (f32[4,256,768]{2,1,0:T(8,128)}, f32[4,8,256]{2,1,0:T(8,128)}) custom-call(f32[4,256,768]{2,1,0:T(8,128)} %get-tuple-element.71.y_ref, bf16[4,256,1024]{2,1,0:T(8,128)(2,1)} %get-tuple-element.72.act_ref, f32[4,256,128]{2,1,0:T(8,128)} %get-tuple-element.73.lac_ref, bf16[4,768,128]{2,1,0:T(8,128)(2,1)} %bitcast.22.sin_ref, ...), custom_call_target="tpu_custom_call" | custom-call | bytes 14475264 | tf_op jit(solution)/shard_map/finish/pallas_call | solution.py:414
  155.0 11.7 %norm.1 = (bf16[4,256,768]{2,1,0:T(8,128)(2,1)}, bf16[4,256,768]{2,1,0:T(8,128)(2,1)}, f32[4,256,768]{2,1,0:T(8,128)}, f32[4,256,128]{2,1,0:T(8,128)}, bf16[8,384,128]{2,1,0:T(8,128)(2,1)}, /*index=5*/f32[8,768]{1,0:T(8,128)}) custom-call(f32[4,256,768]{2,1,0:T(8,128)} %get-tuple-element.80.y_ref, bf16[4,256,1024]{2,1,0:T(8,128)(2,1)} %get-tuple-element.72.act_ref, ...), custom_call_target="tpu_custom_call" | custom-call | bytes 18268160 | tf_op jit(solution)/shard_map/norm/pallas_call | solution.py:414
  183.9 25.2 %collective-permute-done.22 = bf16[4,96,1536]{2,1,0:T(8,128)(2,1)} collective-permute-done((bf16[4,96,1536]{2,1,0:T(8,128)(2,1)}, bf16[4,96,1536]{2,1,0:T(8,128)(2,1)}, u32[]{:S(2)}, u32[]{:S(2)}) %collective-permute-start.22) | collective-permute-done | bytes 1179680 | tf_op jit(solution)/shard_map/ppermute | solution.py:435
  218.0 9.9 %reduce-scatter.2.cloned.1.call-start = ((), (), s32[]{:S(2)}) async-start(), calls=%async_computation.5 | async-start | bytes 2654208 | tf_op jit(solution)/shard_map/reduce_scatter | solution.py:744
  230.5 6.0 %bitcast_convert_fusion = bf16[768,1536]{1,0:T(8,128)(2,1)} fusion(bf16[4,256,768]{2,1,0:T(8,128)(2,1)} %get-tuple-element.82, bf16[1,256,1536]{2,1,0:T(8,128)(2,1)S(1)} %copy-done.56, bf16[1,256,1536]{2,1,0:T(8,128)(2,1)} %collective-permute-done.15, bf16[1,256,1536]{2,1,0:T(8,128)(2,1)S(1)} %copy-done.54, bf16[1,256,1536]{2,1,0:T(8,128)(2,1)} %bitcast.29), kind=kOutput, calls=%fused_computation.1 | convolution fusion | flops 2421817344 | bytes 7077888 | tf_op jit(solution)/shard_map/dot_general | solution.py:734
  236.6 16.1 %backward.1 = (f32[4,256,768]{2,1,0:T(8,128)}, f32[4,256,256]{2,1,0:T(8,128)}) custom-call(bf16[4,256,1024]{2,1,0:T(8,128)(2,1)} %get-tuple-element.72.act_ref, f32[4,256,768]{2,1,0:T(8,128)} %get-tuple-element.84.dy_ref, f32[4,256,128]{2,1,0:T(8,128)} %get-tuple-element.73.lac_ref, f32[4,16,256]{2,1,0:T(8,128)} %get-tuple-element.85.lar_ref, ...), custom_call_target="tpu_custom_call" | custom-call | flops 805306368 | bytes 10878976 | tf_op jit(solution)/shard_map/backward/pallas_call | solution.py:414
  259.7 20.3 %collective-permute-done.24 = bf16[1,96,1536]{2,1,0:T(8,128)(2,1)S(1)} collective-permute-done((bf16[1,96,1536]{2,1,0:T(8,128)(2,1)S(1)}, bf16[1,96,1536]{2,1,0:T(8,128)(2,1)S(1)}, u32[]{:S(2)}, u32[]{:S(2)}) %collective-permute-start.24) | collective-permute-done | bytes 294944 | tf_op jit(solution)/shard_map/ppermute | solution.py:435
  288.4 16.4 %carry.1 = (f32[4,256,768]{2,1,0:T(8,128)}, f32[4,8,768]{2,1,0:T(8,128)}, bf16[4,256,128]{2,1,0:T(8,128)(2,1)}, f32[8,768]{1,0:T(8,128)}, f32[8,128]{1,0:T(8,128)}) custom-call(bf16[4,272,1152]{2,1,0:T(8,128)(2,1)} %convolution_convert_fusion.pc_ref, f32[8,1024]{1,0:T(8,128)} %pad_maximum_fusion.22.taps_ref, f32[8,128]{1,0:T(8,128)} %select_maximum_fusion.2.rate_ref, ...), custom_call_target="tpu_custom_call" | custom-call | bytes 18456576 | tf_op jit(solution)/shard_map/carry/pallas_call | solution.py:414
  307.6 6.9 %fusion.32 = f32[4,256,1536]{2,1,0:T(8,128)} fusion(bf16[4,256,768]{2,1,0:T(8,128)(2,1)S(1)} %copy-done.75, bf16[768,384]{1,0:T(8,128)(2,1)} %collective-permute-done.14, bf16[768,384]{1,0:T(8,128)(2,1)} %collective-permute-done.13, bf16[768,384]{1,0:T(8,128)(2,1)} %collective-permute-done.12, bf16[768,384]{1,0:T(8,128)(2,1)S(1)} %copy-done.59), kind=kOutput, calls=%fused_computation.60 | convolution fusion | flops 2425356288 | bytes 10223616 | tf_op jit(solution)/shard_map/dot_general | solution.py:927
  373.2 13.8 %collective-permute-done.37 = bf16[4,56,1536]{2,1,0:T(8,128)(2,1)} collective-permute-done((bf16[4,56,1536]{2,1,0:T(8,128)(2,1)}, bf16[4,56,1536]{2,1,0:T(8,128)(2,1)}, u32[]{:S(2)}, u32[]{:S(2)}) %collective-permute-start.37) | collective-permute-done | bytes 688160 | tf_op jit(solution)/shard_map/ppermute | solution.py:435
  391.3 11.9 %collective-permute-done.38 = bf16[2,56,1536]{2,1,0:T(8,128)(2,1)S(1)} collective-permute-done((bf16[2,56,1536]{2,1,0:T(8,128)(2,1)S(1)}, bf16[2,56,1536]{2,1,0:T(8,128)(2,1)S(1)}, u32[]{:S(2)}, u32[]{:S(2)}) %collective-permute-start.38) | collective-permute-done | bytes 344096 | tf_op jit(solution)/shard_map/ppermute | solution.py:435
  404.0 17.8 %collective-permute-done.39 = bf16[1,56,1536]{2,1,0:T(8,128)(2,1)S(1)} collective-permute-done((bf16[1,56,1536]{2,1,0:T(8,128)(2,1)S(1)}, bf16[1,56,1536]{2,1,0:T(8,128)(2,1)S(1)}, u32[]{:S(2)}, u32[]{:S(2)}) %collective-permute-start.39) | collective-permute-done | bytes 172064 | tf_op jit(solution)/shard_map/ppermute | solution.py:435
  435.5 12.4 %collective-permute-done.50 = bf16[56,384]{1,0:T(8,128)(2,1)S(1)} collective-permute-done((bf16[56,384]{1,0:T(8,128)(2,1)S(1)}, bf16[56,384]{1,0:T(8,128)(2,1)S(1)}, u32[]{:S(2)}, u32[]{:S(2)}) %collective-permute-start.50) | collective-permute-done | bytes 43040 | tf_op jit(solution)/shard_map/ppermute | solution.py:435
  456.5 7.8 %collective-permute-done.52 = bf16[1,4,56,384]{3,2,1,0:T(8,128)(2,1)S(1)} collective-permute-done((bf16[1,4,56,384]{3,2,1,0:T(8,128)(2,1)S(1)}, bf16[1,4,56,384]{3,2,1,0:T(8,128)(2,1)S(1)}, u32[]{:S(2)}, u32[]{:S(2)}) %collective-permute-start.52) | collective-permute-done | bytes 172064 | tf_op jit(solution)/shard_map/ppermute | solution.py:435
  468.3 7.1 %collective-permute-done.53 = bf16[2,4,56,384]{3,2,1,0:T(8,128)(2,1)S(1)} collective-permute-done((bf16[2,4,56,384]{3,2,1,0:T(8,128)(2,1)S(1)}, bf16[2,4,56,384]{3,2,1,0:T(8,128)(2,1)S(1)}, u32[]{:S(2)}, u32[]{:S(2)}) %collective-permute-start.53) | collective-permute-done | bytes 344096 | tf_op jit(solution)/shard_map/ppermute | solution.py:435
  496.4 12.3 %collective-permute-done.48 = bf16[4,4,56,384]{3,2,1,0:T(8,128)(2,1)} collective-permute-done((bf16[4,4,56,384]{3,2,1,0:T(8,128)(2,1)}, bf16[4,4,56,384]{3,2,1,0:T(8,128)(2,1)}, u32[]{:S(2)}, u32[]{:S(2)}) %collective-permute-start.48) | collective-permute-done | bytes 688160 | tf_op jit(solution)/shard_map/ppermute | solution.py:435
  512.4 6.3 %assemble.1 = (f32[6448,384]{1,0:T(8,128)}, f32[4,128,384]{2,1,0:T(8,128)S(1)}, f32[8,384]{1,0:T(8,128)S(1)}) custom-call(s32[2]{0:T(128)S(1)} %pad_add_fusion.ids_ref, bf16[8,4,96,384]{3,2,1,0:T(8,128)(2,1)S(1)} %pad_maximum_fusion.2.gate_ref, bf16[8,4,56,384]{3,2,1,0:T(8,128)(2,1)S(1)} %pad_maximum_fusion.5.refs_0_, ...), custom_call_target="tpu_custom_call" | custom-call | bytes 20766720 | tf_op jit(solution)/shard_map/assemble/pallas_call | solution.py:414
  (421 shorter events, 238.6 us)
Async XLA Ops:
  20.3 38.3 %collective-permute-start.9 = (bf16[768,384]{1,0:T(8,128)(2,1)}, bf16[768,384]{1,0:T(8,128)(2,1)S(1)}, u32[]{:S(2)}, u32[]{:S(2)}) collective-permute-start(bf16[768,384]{1,0:T(8,128)(2,1)} %get-tuple-element.130), channel_id=1, source_target_pairs={{0,1},{1,0},{2,3},{3,2},{4,5},{5,4},{6,7},{7,6},{8,9},{9,8},{10,11... | collective-permute-start | bytes 1769480 | tf_op jit(solution)/shard_map/ppermute | solution.py:435
  21.4 32.9 %collective-permute-start.10 = (bf16[1,304,384]{2,1,0:T(8,128)(2,1)S(1)}, bf16[1,304,384]{2,1,0:T(8,128)(2,1)S(1)}, u32[]{:S(2)}, u32[]{:S(2)}) collective-permute-start(bf16[1,304,384]{2,1,0:T(8,128)(2,1)S(1)} %slice_bitcast_fusion.10), channel_id=1, source_target_pairs={{0,2},{1,3},{2,0},{3,1},{4,6},{5,7},{6,4},{7,5},{8,10},{9,11},{10,... | collective-permute-start | bytes 700424 | tf_op jit(solution)/shard_map/ppermute | solution.py:435
  56.6 34.3 %collective-permute-start.15 = (bf16[1,256,1536]{2,1,0:T(8,128)(2,1)}, bf16[1,256,1536]{2,1,0:T(8,128)(2,1)}, u32[]{:S(2)}, u32[]{:S(2)}) collective-permute-start(bf16[1,256,1536]{2,1,0:T(8,128)(2,1)} %bitcast.29), channel_id=1, source_target_pairs={{0,2},{1,3},{2,0},{3,1},{4,6},{5,7},{6,4},{7,5},{8,10},{9,11},{10,... | collective-permute-start | bytes 2359304 | tf_op jit(solution)/shard_map/ppermute | solution.py:435
  84.8 27.3 %all-to-all-start = ((bf16[8,400,128]{2,1,0:T(8,128)(2,1)}), bf16[8,400,128]{2,1,0:T(8,128)(2,1)}, u32[]{:S(2)}, u32[]{:S(2)}) async-start(bf16[8,400,128]{2,1,0:T(8,128)(2,1)} %get-tuple-element.74.s_ref), calls=%async_computation | async-start | bytes 1638400 | tf_op jit(solution)/shard_map/all_to_all | solution.py:515
  93.5 34.1 %collective-permute-start.16 = (bf16[2,256,1536]{2,1,0:T(8,128)(2,1)}, bf16[2,256,1536]{2,1,0:T(8,128)(2,1)}, u32[]{:S(2)}, u32[]{:S(2)}) collective-permute-start(bf16[2,256,1536]{2,1,0:T(8,128)(2,1)} %pad_maximum_fusion.4), channel_id=1, source_target_pairs={{0,1},{1,0},{2,3},{3,2},{4,5},{5,4},{6,7},{7,6},{8,9},{9,8},{10,11... | collective-permute-start | bytes 4718600 | tf_op jit(solution)/shard_map/ppermute | solution.py:435
  93.5 26.8 %collective-permute-start.12 = (bf16[768,384]{1,0:T(8,128)(2,1)}, bf16[768,384]{1,0:T(8,128)(2,1)}, u32[]{:S(2)}, u32[]{:S(2)}) collective-permute-start(bf16[768,384]{1,0:T(8,128)(2,1)} %get-tuple-element.76), channel_id=1, source_target_pairs={{0,1},{1,0},{2,3},{3,2},{4,5},{5,4},{6,7},{7,6},{8,9},{9,8},{10,11... | collective-permute-start | bytes 1769480 | tf_op jit(solution)/shard_map/ppermute | solution.py:435
  94.0 26.3 %collective-permute-start.13 = (bf16[768,384]{1,0:T(8,128)(2,1)}, bf16[768,384]{1,0:T(8,128)(2,1)}, u32[]{:S(2)}, u32[]{:S(2)}) collective-permute-start(bf16[768,384]{1,0:T(8,128)(2,1)} %get-tuple-element.77), channel_id=1, source_target_pairs={{0,2},{1,3},{2,0},{3,1},{4,6},{5,7},{6,4},{7,5},{8,10},{9,11},{10,... | collective-permute-start | bytes 1769480 | tf_op jit(solution)/shard_map/ppermute | solution.py:435
  95.6 25.7 %collective-permute-start.14 = (bf16[768,384]{1,0:T(8,128)(2,1)}, bf16[768,384]{1,0:T(8,128)(2,1)}, u32[]{:S(2)}, u32[]{:S(2)}) collective-permute-start(bf16[768,384]{1,0:T(8,128)(2,1)} %get-tuple-element.78), channel_id=1, source_target_pairs={{0,3},{1,2},{2,1},{3,0},{4,7},{5,6},{6,5},{7,4},{8,11},{9,10},{10,... | collective-permute-start | bytes 1769480 | tf_op jit(solution)/shard_map/ppermute | solution.py:435
  173.7 35.4 %collective-permute-start.22 = (bf16[4,96,1536]{2,1,0:T(8,128)(2,1)}, bf16[4,96,1536]{2,1,0:T(8,128)(2,1)}, u32[]{:S(2)}, u32[]{:S(2)}) collective-permute-start(bf16[4,96,1536]{2,1,0:T(8,128)(2,1)} %dynamic-slice_bitcast_fusion), channel_id=1, source_target_pairs={{0,4},{4,0},{8,12},{12,8},{16,20},{20,16},{24,28},{28,24},{1,5},{5... | collective-permute-start | bytes 3538952 | tf_op jit(solution)/shard_map/ppermute | solution.py:435
  175.0 35.7 %all-to-all-start.2 = ((bf16[8,384,128]{2,1,0:T(8,128)(2,1)}), bf16[8,384,128]{2,1,0:T(8,128)(2,1)S(1)}, u32[]{:S(2)}, u32[]{:S(2)}) async-start(bf16[8,384,128]{2,1,0:T(8,128)(2,1)} %get-tuple-element.88), calls=%async_computation.2 | async-start | bytes 1572864 | tf_op jit(solution)/shard_map/all_to_all | solution.py:515
  183.9 72.8 %collective-permute-start.20 = (bf16[2,256,1536]{2,1,0:T(8,128)(2,1)}, bf16[2,256,1536]{2,1,0:T(8,128)(2,1)}, u32[]{:S(2)}, u32[]{:S(2)}) collective-permute-start(bf16[2,256,1536]{2,1,0:T(8,128)(2,1)} %fusion.19), channel_id=1, source_target_pairs={{0,1},{1,0},{2,3},{3,2},{4,5},{5,4},{6,7},{7,6},{8,9},{9,8},{10,11... | collective-permute-start | bytes 4718600 | tf_op jit(solution)/shard_map/ppermute | solution.py:435
  214.5 39.5 %all-to-all-start.3 = ((bf16[8,384,128]{2,1,0:T(8,128)(2,1)}), bf16[8,384,128]{2,1,0:T(8,128)(2,1)S(1)}, u32[]{:S(2)}, u32[]{:S(2)}) async-start(bf16[8,384,128]{2,1,0:T(8,128)(2,1)} %back_chain.1), calls=%async_computation.3 | async-start | bytes 1572864 | tf_op jit(solution)/shard_map/all_to_all | solution.py:515
  218.0 155.1 %reduce-scatter.2.cloned.1.call-start = ((), (), s32[]{:S(2)}) async-start(), calls=%async_computation.5 | async-start | bytes 2654208 | tf_op jit(solution)/shard_map/reduce_scatter | solution.py:744
  236.6 196.5 %all-gather.2.cloned.1.call-start = ((), (), s32[]{:S(2)}) async-start(), calls=%async_computation.6 | async-start | bytes 2654208 | tf_op jit(solution)/shard_map/all_gather | solution.py:855
  254.0 26.0 %collective-permute-start.24 = (bf16[1,96,1536]{2,1,0:T(8,128)(2,1)S(1)}, bf16[1,96,1536]{2,1,0:T(8,128)(2,1)S(1)}, u32[]{:S(2)}, u32[]{:S(2)}) collective-permute-start(bf16[1,96,1536]{2,1,0:T(8,128)(2,1)S(1)} %constant_dynamic-slice_fusion.4), channel_id=1, source_target_pairs={{0,16},{4,20},{8,24},{12,28},{16,0},{20,4},{24,8},{28,12},{1,17},{... | collective-permute-start | bytes 884744 | tf_op jit(solution)/shard_map/ppermute | solution.py:435
  280.2 25.8 %collective-permute-start.30 = (bf16[96,384]{1,0:T(8,128)(2,1)S(1)}, bf16[96,384]{1,0:T(8,128)(2,1)S(1)}, u32[]{:S(2)}, u32[]{:S(2)}) collective-permute-start(bf16[96,384]{1,0:T(8,128)(2,1)S(1)} %get-tuple-element.153), channel_id=1, source_target_pairs={{0,2},{1,3},{2,0},{3,1},{4,6},{5,7},{6,4},{7,5},{8,10},{9,11},{10,... | collective-permute-start | bytes 221192 | tf_op jit(solution)/shard_map/ppermute | solution.py:435
  281.2 25.6 %collective-permute-start.31 = (bf16[96,384]{1,0:T(8,128)(2,1)S(1)}, bf16[96,384]{1,0:T(8,128)(2,1)S(1)}, u32[]{:S(2)}, u32[]{:S(2)}) collective-permute-start(bf16[96,384]{1,0:T(8,128)(2,1)S(1)} %get-tuple-element.152), channel_id=1, source_target_pairs={{0,3},{1,2},{2,1},{3,0},{4,7},{5,6},{6,5},{7,4},{8,11},{9,10},{10,... | collective-permute-start | bytes 221192 | tf_op jit(solution)/shard_map/ppermute | solution.py:435
  283.0 46.7 %collective-permute-start.21 = (bf16[1,256,1536]{2,1,0:T(8,128)(2,1)}, bf16[1,256,1536]{2,1,0:T(8,128)(2,1)}, u32[]{:S(2)}, u32[]{:S(2)}) collective-permute-start(bf16[1,256,1536]{2,1,0:T(8,128)(2,1)} %fusion.33), channel_id=1, source_target_pairs={{0,2},{1,3},{2,0},{3,1},{4,6},{5,7},{6,4},{7,5},{8,10},{9,11},{10,... | collective-permute-start | bytes 2359304 | tf_op jit(solution)/shard_map/ppermute | solution.py:435
  288.4 27.1 %collective-permute-start.25 = (bf16[4,64,256]{2,1,0:T(8,128)(2,1)}, bf16[4,64,256]{2,1,0:T(8,128)(2,1)}, u32[]{:S(2)}, u32[]{:S(2)}) collective-permute-start(bf16[4,64,256]{2,1,0:T(8,128)(2,1)} %get-tuple-element.101), channel_id=1, source_target_pairs={{0,1},{1,0},{2,3},{3,2},{4,5},{5,4},{6,7},{7,6},{8,9},{9,8},{10,11... | collective-permute-start | bytes 393224 | tf_op jit(solution)/shard_map/ppermute | solution.py:435
  357.6 29.4 %collective-permute-start.37 = (bf16[4,56,1536]{2,1,0:T(8,128)(2,1)}, bf16[4,56,1536]{2,1,0:T(8,128)(2,1)}, u32[]{:S(2)}, u32[]{:S(2)}) collective-permute-start(bf16[4,56,1536]{2,1,0:T(8,128)(2,1)} %dynamic-slice_bitcast_fusion.2), channel_id=1, source_target_pairs={{0,4},{4,0},{8,12},{12,8},{16,20},{20,16},{24,28},{28,24},{1,5},{5... | collective-permute-start | bytes 2064392 | tf_op jit(solution)/shard_map/ppermute | solution.py:435
  357.9 95.4 %collective-permute-start.36 = (bf16[4,4,96,384]{3,2,1,0:T(8,128)(2,1)}, bf16[4,4,96,384]{3,2,1,0:T(8,128)(2,1)}, u32[]{:S(2)}, u32[]{:S(2)}) collective-permute-start(bf16[4,4,96,384]{3,2,1,0:T(8,128)(2,1)} %pad_maximum_fusion.7), channel_id=1, source_target_pairs={{0,4},{4,0},{8,12},{12,8},{16,20},{20,16},{24,28},{28,24},{1,5},{5... | collective-permute-start | bytes 3538952 | tf_op jit(solution)/shard_map/ppermute | solution.py:435
  370.6 51.2 %collective-permute-start.34 = (bf16[2,256,1536]{2,1,0:T(8,128)(2,1)}, bf16[2,256,1536]{2,1,0:T(8,128)(2,1)}, u32[]{:S(2)}, u32[]{:S(2)}) collective-permute-start(bf16[2,256,1536]{2,1,0:T(8,128)(2,1)} %fusion.20), channel_id=1, source_target_pairs={{0,1},{1,0},{2,3},{3,2},{4,5},{5,4},{6,7},{7,6},{8,9},{9,8},{10,11... | collective-permute-start | bytes 4718600 | tf_op jit(solution)/shard_map/ppermute | solution.py:435
  427.2 28.0 %collective-permute-start.35 = (bf16[1,256,1536]{2,1,0:T(8,128)(2,1)}, bf16[1,256,1536]{2,1,0:T(8,128)(2,1)}, u32[]{:S(2)}, u32[]{:S(2)}) collective-permute-start(bf16[1,256,1536]{2,1,0:T(8,128)(2,1)} %fusion.34), channel_id=1, source_target_pairs={{0,2},{1,3},{2,0},{3,1},{4,6},{5,7},{6,4},{7,5},{8,10},{9,11},{10,... | collective-permute-start | bytes 2359304 | tf_op jit(solution)/shard_map/ppermute | solution.py:435
  483.7 25.1 %collective-permute-start.48 = (bf16[4,4,56,384]{3,2,1,0:T(8,128)(2,1)}, bf16[4,4,56,384]{3,2,1,0:T(8,128)(2,1)}, u32[]{:S(2)}, u32[]{:S(2)}) collective-permute-start(bf16[4,4,56,384]{3,2,1,0:T(8,128)(2,1)} %pad_maximum_fusion.9), channel_id=1, source_target_pairs={{0,4},{4,0},{8,12},{12,8},{16,20},{20,16},{24,28},{28,24},{1,5},{5... | collective-permute-start | bytes 2064392 | tf_op jit(solution)/shard_map/ppermute | solution.py:435
  (117 other events, 1364.1 us)
Sparse Core Ops, SparseCore 0:
  236.7 84.0 reduce-scatter.1
  373.3 59.7 all-gather.1

commit v4 on v3

--- a/solution.py
+++ b/solution.py
@@ -455,28 +455,35 @@
     return jnp.concatenate([value[..., (j ^ by) * size : ((j ^ by) + 1) * size] for j in range(owners)], axis=-1)
 
 
-def to_owner(value, axis, turn=False):
+def to_owner(value, axis, turn=False, first=None):
     count = lax.axis_size(axis)
     by = 1
     while by < count:
         value = value.reshape((value.shape[0] // 2, 2) + value.shape[1:])
         other = swap(value[:, 1].astype(bf16), axis, by).astype(f32)
         value = value[:, 0] + (blocks_turned(other, by, count) if turn else other)
+        if first is not None:
+            value, first = tied(value, first), None
         by *= 2
     return value[0]
 
 
-def halved(value, axis, by):
+def halved_start(value, axis, by):
     value = value.reshape((value.shape[0] // 2, 2) + value.shape[1:])
     bit = (lax.axis_index(axis) // by) % 2
     keep = lax.dynamic_index_in_dim(value, bit, 1, False)
     give = lax.dynamic_index_in_dim(value, 1 - bit, 1, False)
-    return (keep.astype(f32) + swap(give, axis, by).astype(f32)).astype(bf16)
+    return keep, swap(give, axis, by)
+
+
+def halved_end(pair, *others):
+    keep, came = tied(pair, others) if others else pair
+    return (keep.astype(f32) + came.astype(f32)).astype(bf16)
 
 
 def halved_from(value, axis, by):
     while value.shape[0] > 1:
-        value = halved(value, axis, by)
+        value = halved_end(halved_start(value, axis, by))
         by *= 2
     return value[0]
 
@@ -485,8 +492,9 @@
     return lax.optimization_barrier((value, others))[0]
 
 
-def gather_step(value, axis, by):
-    return jnp.concatenate([value, swap(value, axis, by)], axis=0)
+def gather_step(value, axis, by, *others):
+    came = swap(value, axis, by)
+    return jnp.concatenate([value, tied(came, others) if others else came], axis=0)
 
 
 def gathered(value, axis, by):
@@ -740,11 +748,13 @@
     def pieces(g):
         return g.reshape((nq, g.shape[0] // nq) + g.shape[1:])
 
-    back_came = exchange(dsin, "seq")
-    out_sum = lax.psum_scatter(pieces(grad_of(gated_out, back_branch)), "seq", scatter_dimension=0)
-    gate_sum = halved(pieces(grad_of(dgate, main)), "seq", 1)
-    back_came, gate_sum = lax.optimization_barrier((back_came, gate_sum))
-    gate_sum = halved(gate_sum, "seq", 2)
+    barrier = lax.optimization_barrier
+    gate_grad, out_grad = grad_of(dgate, main), grad_of(gated_out, back_branch)
+    back_came = exchange(tied(dsin, gate_grad), "seq")
+    gate_step = halved_start(pieces(gate_grad), "seq", 1)
+    out_step = halved_start(pieces(out_grad), "seq", 1)
+    branch = lax.dot_general(gated_out, out_weight, (((2,), (0,)), ((), ())), preferred_element_type=f32)
+    branch = to_owner(branch, "fsdp")
     (reached,) = call(
         back_chain_kernel,
         1,
@@ -756,19 +766,23 @@
         count=per_slot,
     )
     g_end = exchange(reached, "seq").reshape(slots, channels, state)
-    g_end, gate_sum = lax.optimization_barrier((g_end, gate_sum))
-    gate_sum = halved_from(gate_sum, "seq", 4)
+    gate_sum = halved_end(gate_step, reached)
+    dy_later, gate_sum = barrier((dy, gate_sum))
+    gate_step = halved_start(gate_sum, "seq", 2)
 
     r_local, dbc = call(
         backward_kernel,
         slots,
-        [(act, each), (dy, each), (lac, each), (lar, each), (dtr, each), (s_in, each)],
+        [(act, each), (dy_later, each), (lac, each), (lar, each), (dtr, each), (s_in, each)],
         [((slots, seg, channels), f32, each), ((slots, seg, 2 * state), f32, each)],
         "backward",
         far=True,
         flops=4 * slots * seg * seg * channels,
         **statics,
     )
+    gate_sum = halved_end(gate_step, dbc)
+    dbc, gate_sum = barrier((dbc, gate_sum))
+    gate_step = halved_start(gate_sum, "seq", 4)
     d_shares = call(
         rows_grad_kernel,
         slots,
@@ -779,9 +793,10 @@
         scratch=[pltpu.VMEM((2 * state, seg), f32)],
         **statics,
     )
-    d_shares = [(swap(d, "fsdp", j) if j else d, (1, lambda s, i, j=j: s ^ j)) for j, d in enumerate(d_shares)]
-    r_local, gate_sum = lax.optimization_barrier((r_local, gate_sum))
-    gate_sum = traded(gate_sum, "fsdp")
+    out_sum = halved_end(out_step, d_shares[0])
+    r_local, out_sum, own_share = barrier((r_local, out_sum, d_shares[0]))
+    out_step = halved_start(out_sum, "seq", 2)
+    d_shares = [own_share] + [swap(d, "fsdp", j) for j, d in enumerate(d_shares) if j]
     dpre, first, dstep, dtaps, drate = call(
         carry_kernel,
         slots,
@@ -801,23 +816,28 @@
         rows=piece,
         **statics,
     )
-    dstep, gate_sum = lax.optimization_barrier((dstep, gate_sum))
-    pc_later, dpre = lax.optimization_barrier((pc, dpre))
-    gate_sum = gather_step(gate_sum[None], "seq", nq // 2)
+    dpre, gate_step, out_step, d_shares, branch = barrier((dpre, gate_step, out_step, d_shares, branch))
+    gate_sum, out_sum = halved_from(halved_end(gate_step), "seq", 8), halved_end(out_step)
+    pc_later, gate_sum, out_sum, d_shares = barrier((pc, gate_sum, out_sum, d_shares))
+    out_step = halved_start(out_sum, "seq", 4)
+    gate_sum = traded(gate_sum, "fsdp")[None]
     dpre_share, first_share, dtaps_share = call(
         share_kernel,
         slots,
-        [(pc_later, each), (taps_share.T, None)] + d_shares,
+        [(pc_later, each), (taps_share.T, None)]
+        + [(d, (1, lambda s, i, j=j: s ^ j)) for j, d in enumerate(d_shares)],
         [((slots, seg, lanes), f32, each), ((slots, 8, lanes), f32, each), ((share, lanes), f32, None)],
         "share",
         ids=ids,
         scratch=[pltpu.VMEM((2 * state, seg), f32)],
         **statics,
     )
+    first, first_share, gate_sum = barrier((first, first_share, gate_sum))
     behind = [(i, i - 1) for i in range(1, nq)]
     after = lax.ppermute(jnp.concatenate([first, first_share], axis=2), "seq", behind)
-    after, gate_sum = lax.optimization_barrier((after, gate_sum))
-    gate_sum = gather_step(gate_sum, "seq", nq // 4)
+    gate_more = swap(gate_sum, "seq", nq // 2)
+    after, gate_more = barrier((after, gate_more))
+    gate_sum = jnp.concatenate([gate_sum, gate_more], axis=0)
     taps_back = jnp.concatenate([taps[:, :channels], jnp.pad(taps_share, ((0, 0), (0, lanes - share)))], axis=1)
     (dconv,) = call(
         returned_kernel,
@@ -829,9 +849,6 @@
         heads=heads,
     )
 
-    dconv, gate_sum = lax.optimization_barrier((dconv, gate_sum))
-    gate_bufs = [gathered(gate_sum, "seq", nq // 8)]
-
     per = channels // rows
     head_rows = jnp.stack([drate[0, :heads], drate[1, :heads], jnp.sum(dskip[0].reshape(heads, head_size), axis=1)])
     block = jnp.concatenate(
@@ -848,14 +865,27 @@
     spare = channels + share + heads - sum(g.shape[0] for g in conv_grads[:-1])
     conv_grads[-1] = lax.dynamic_update_slice_in_dim(conv_grads[-1], block, spare, 0)
 
-    def shared(g):
-        return gathered(traded(g, "fsdp")[None], "seq", nq // 2)
-
     out_unit = channels // nq
-    out_parts = [lax.all_gather(out_sum, "seq")]
-    conv_sums = [halved_from(pieces(g), "seq", 1) for g in conv_grads]
-    conv_sums, out_parts = lax.optimization_barrier((conv_sums, out_parts))
-    conv_bufs = [shared(g) for g in conv_sums]
+    conv_steps = [halved_start(pieces(g), "seq", 1) for g in conv_grads]
+    out_sum = halved_from(halved_end(out_step, conv_grads), "seq", 8)[None]
+    gate_sum = gather_step(gate_sum, "seq", nq // 4, out_sum)
+    conv_sums = [halved_end(step, gate_sum) for step in conv_steps]
+    late_conv = tied(dconv, conv_sums[0])
+    out_sum = gather_step(out_sum, "seq", nq // 2, conv_sums)
+    gate_bufs = [gathered(gate_sum, "seq", nq // 8)]
+    conv_steps = [halved_start(g, "seq", 2) for g in conv_sums]
+    conv_sums = [halved_end(step, out_sum) for step in conv_steps]
+    out_sum = gather_step(out_sum, "seq", nq // 4, conv_sums[-1])
+    conv_steps = [halved_start(g, "seq", 4) for g in conv_sums]
+    conv_sums = [halved_from(halved_end(step, out_sum), "seq", 8) for step in conv_steps]
+    out_parts = [gathered(out_sum, "seq", nq // 8)]
+    conv_sums, gate_bufs = barrier((conv_sums, gate_bufs))
+    conv_sums = [traded(g, "fsdp") for g in conv_sums]
+    conv_bufs = [gather_step(g[None], "seq", nq // 2) for g in conv_sums]
+    tied_bufs = conv_bufs
+    conv_bufs = [gather_step(g, "seq", nq // 4) for g in conv_bufs]
+    conv_bufs, out_parts = barrier((conv_bufs, out_parts))
+    conv_bufs = [gathered(g, "seq", nq // 8) for g in conv_bufs]
     place_of = jnp.stack([reversed_bits(place ^ q, nq) for q in range(nq)])
     if all(buf.shape[2] % 8 == 0 for buf in gate_bufs + conv_bufs):
         g_in, tail, norm_sum = call(
@@ -891,7 +921,7 @@
         g_out, gated_sum = call(
             rows_kernel,
             nq,
-            [(part, (1, lambda s, i: s)) for part in out_parts] + [(out_weight, (out_unit, lambda s, i: s))],
+            [(part, (1, lambda s, i: reversed_bits(i[0] ^ s, nq))) for part in out_parts] + [(out_weight, (out_unit, lambda s, i: s))],
             [(out_weight.shape, f32, (out_unit, lambda s, i: s)), ((channels, 1), f32, (out_unit, lambda s, i: s))],
             "rows",
             ids=ids,
@@ -899,7 +929,7 @@
         )
         gated_sum = gated_sum[:, 0]
     else:
-        g_out = jnp.concatenate([part.astype(f32).reshape(channels, -1) for part in out_parts], axis=1)
+        g_out = jnp.concatenate([part[place_of].astype(f32).reshape(channels, -1) for part in out_parts], axis=1)
         gated_sum = jnp.sum(g_out * out_weight.astype(f32), axis=1)
 
     norm_grad = norm_sum / norm_gain.astype(f32)
@@ -916,8 +946,6 @@
     tap_grads = lax.dynamic_slice_in_dim(tap_grads, me * conv_own, conv_own, 1)
     head_grads = lax.dynamic_index_in_dim(got, me, 0, False)[5 * per + 5 :, :heads]
 
-    branch = lax.dot_general(gated_out, out_weight, (((2,), (0,)), ((), ())), preferred_element_type=f32)
-    branch = to_owner(branch, "fsdp")
     mixed = (valid * (inputs + branch)).astype(bf16)
 
     w_share = lax.dynamic_slice_in_dim(w_conv, channels + me * share, share, 0)
@@ -926,8 +954,8 @@
     def back(dz, w):
         return lax.dot_general(dz, w, (((2,), (0,)), ((), ())), preferred_element_type=f32)
 
-    bn = back(dgate, w_gate) + back(dconv[..., :channels], w_conv[:channels]) + back(dconv[..., channels:], w_last)
-    bn = to_owner(bn, "fsdp", turn=True)
+    bn = back(dgate, w_gate) + back(late_conv[..., :channels], w_conv[:channels]) + back(late_conv[..., channels:], w_last)
+    bn = to_owner(bn, "fsdp", turn=True, first=tied_bufs)
     (input_grad,) = call(
         input_kernel,
         1,

time: 538 us -> 491 us (0.913)
  waiting for transfers between devices: 194 us -> 149 us
  between operations: 16.6 us -> 3.38 us
  starting transfers between devices: 76.7 us -> 85.5 us
    ppermute x53 -> x59, waiting for transfers between devices: 177 us -> 128 us  [swap(): return lax.ppermute(value, axis, [(i, i ^ by) for i in range(count)])]
    ppermute x53 -> x59, starting transfers between devices: 44.3 us -> 60.6 us  [swap(): return lax.ppermute(value, axis, [(i, i ^ by) for i in range(count)])]
    reduce_scatter x1 -> x0, starting transfers between devices: 9.9 us -> none  [per_device(): lax.psum_scatter(pieces(grad_of(gated_out, back_branch)), 'seq', scatter_...]
    concatenate x9 -> x11, other arithmetic: 10.9 us -> 7.93 us  [the longest x10 7.87 us: gather_step(): jnp.concatenate([value, tied(came, others) if others else came], axis=0)]
    unnamed x164 -> x154, local copies, waits for them, and re-layouts: 18 us -> 16.6 us
  transfers between devices with their start and end apart: 61 -> 65, of which waited for: 26 -> 26; matrix products, arithmetic and copies ran while one was open for 21% -> 23% of each run, Pallas kernels for 14% -> 15%
where the time goes in v4:
time: 491 us; the launch traced here: 481 us
  waiting for transfers between devices  149 us (30%)
  Pallas kernels  100 us (20%)
  starting transfers between devices  85.5 us (17%)
  local copies, waits for them, and re-layouts  53.3 us (11%)
  matrix products  48.3 us (10%)
  other arithmetic  41.2 us (8%)
    ppermute x59, waiting for transfers between devices, swap(): return lax.ppermute(value, axis, [(i, i ^ by) for i in range(count)])  128 us
    pallas_call x15, Pallas kernels, call(): pl.pallas_call(functools.partial(kernel, **statics), grid_spec=pltpu.Pref...  100 us
    ppermute x59, starting transfers between devices, swap(): return lax.ppermute(value, axis, [(i, i ^ by) for i in range(count)])  60.6 us
    all_to_all x4, starting transfers between devices, exchange(): return lax.all_to_all(value, axis, 0, 0)  20 us
    all_to_all x4, waiting for transfers between devices, exchange(): return lax.all_to_all(value, axis, 0, 0)  17 us
    dot_general x4, matrix products, grad_of(): lax.dot_general(dz, x, (((0, 1), (0, 1)), ((), ())), preferred_element_ty...  16.9 us
    unnamed x154, local copies, waits for them, and re-layouts  16.6 us
    dot_general x2, matrix products, project(): lax.dot_general(x, w, (((2,), (1,)), ((), ())), preferred_element_type=f32)  12.1 us
  transfers between devices with their start and end apart: 65, of which 26 were waited for; matrix products, arithmetic and copies ran while one was open for 23% of the time, Pallas kernels for 15%

profile of v4, /device:TPU:0, one launch (start us, length us, event | category | flops | bytes accessed | tf_op | source)
XLA Modules:
  0.0 481.3 jit_solution(18276976494395274359)
XLA Ops:
  19.8 5.4 %collective-permute-done.7 = bf16[1,16,1536]{2,1,0:T(8,128)(2,1)S(1)} collective-permute-done((bf16[1,16,1536]{2,1,0:T(8,128)(2,1)S(1)}, bf16[1,16,1536]{2,1,0:T(8,128)(2,1)S(1)}, u32[]{:S(2)}, u32[]{:S(2)}) %collective-permute-start.7) | collective-permute-done | bytes 49184 | tf_op jit(solution)/shard_map/ppermute | solution.py:435
  32.0 15.5 %collective-permute-done.2 = bf16[1,256,1536]{2,1,0:T(8,128)(2,1)S(1)} collective-permute-done((bf16[1,256,1536]{2,1,0:T(8,128)(2,1)S(1)}, bf16[1,256,1536]{2,1,0:T(8,128)(2,1)S(1)}, u32[]{:S(2)}, u32[]{:S(2)}) %collective-permute-start.2) | collective-permute-done | bytes 786464 | tf_op jit(solution)/shard_map/ppermute | solution.py:435
  57.9 5.8 %convolution_convert_fusion.pc_ref = bf16[4,272,1152]{2,1,0:T(8,128)(2,1)} fusion(bf16[4,272,1536]{2,1,0:T(8,128)(2,1)S(1)} %normalize.1, bf16[1152,1536]{1,0:T(8,128)(2,1)S(1)} %weights.1), kind=kOutput, calls=%fused_computation.3 | convolution fusion | flops 3851624448 | bytes 9388032 | tf_op jit(solution)/shard_map/dot_general | solution.py:677
  63.7 14.5 %forward.1 = (bf16[4,256,1024]{2,1,0:T(8,128)(2,1)}, f32[4,256,768]{2,1,0:T(8,128)}, bf16[8,400,128]{2,1,0:T(8,128)(2,1)}, f32[4,256,128]{2,1,0:T(8,128)}, f32[4...) custom-call(bf16[4,272,1152]{2,1,0:T(8,128)(2,1)} %convolution_convert_fusion.pc_ref, ...), custom_call_target="tpu_custom_call" | custom-call | flops 402653184 | bytes 9785344 | tf_op jit(solution)/shard_map/forward/pallas_call | solution.py:414
  78.2 6.0 %all-to-all-start = ((bf16[8,400,128]{2,1,0:T(8,128)(2,1)}), bf16[8,400,128]{2,1,0:T(8,128)(2,1)}, u32[]{:S(2)}, u32[]{:S(2)}) async-start(bf16[8,400,128]{2,1,0:T(8,128)(2,1)} %get-tuple-element.118.s_ref), calls=%async_computation | async-start | bytes 1638400 | tf_op jit(solution)/shard_map/all_to_all | solution.py:523
  97.2 8.4 %all-to-all-done.in_ref.decay_ref = bf16[8,400,128]{2,1,0:T(8,128)(2,1)} async-done(((bf16[8,400,128]{2,1,0:T(8,128)(2,1)}), bf16[8,400,128]{2,1,0:T(8,128)(2,1)}, u32[]{:S(2)}, u32[]{:S(2)}) %all-to-all-start) | async-done | bytes 819232 | tf_op jit(solution)/shard_map/all_to_all | solution.py:523
  114.7 6.3 %fusion.15.gate_ref = bf16[4,256,768]{2,1,0:T(8,128)(2,1)} fusion(bf16[4,272,1536]{2,1,0:T(8,128)(2,1)} %copy-done.8, bf16[768,384]{1,0:T(8,128)(2,1)} %collective-permute-done.14, bf16[768,384]{1,0:T(8,128)(2,1)} %collective-permute-done.13, bf16[768,384]{1,0:T(8,128)(2,1)} %collective-permute-done.12, bf16[768,384]{1,0:T(8,128)(2,1)} %get-tuple-element.119), kind=kOutput, calls=%fused_computation.33 | convolution fusion | flops 2426142720 | bytes 7077888 | tf_op jit(solution)/shard_map/dot_general | solution.py:677
  123.9 5.7 %fusion.8.bg_ref = f32[4,256,768]{2,1,0:T(8,128)} fusion(bf16[768,1536]{1,0:T(8,128)(2,1)S(1)} %copy-done.15, bf16[1,256,1536]{2,1,0:T(8,128)(2,1)S(1)} %get-tuple-element.236, bf16[1,256,1536]{2,1,0:T(8,128)(2,1)} %collective-permute-done.15, bf16[1,256,1536]{2,1,0:T(8,128)(2,1)S(1)} %get-tuple-element.235, bf16[1,256,1536]{2,1,0:T(8,128)(2,1)} %bitcast.30), kind=kOutput, calls=%fused_computation.24 | convolution fusion | flops 2420637696 | bytes 8650752 | tf_op jit(solution)/shard_map/dot_general | solution.py:711
  134.0 9.0 %finish.1 = (f32[4,256,768]{2,1,0:T(8,128)}, f32[4,8,256]{2,1,0:T(8,128)}) custom-call(f32[4,256,768]{2,1,0:T(8,128)} %get-tuple-element.116.y_ref, bf16[4,256,1024]{2,1,0:T(8,128)(2,1)} %get-tuple-element.115.act_ref, f32[4,256,128]{2,1,0:T(8,128)} %get-tuple-element.117.lac_ref, bf16[4,768,128]{2,1,0:T(8,128)(2,1)} %bitcast.23.sin_ref, ...), custom_call_target="tpu_custom_call" | custom-call | bytes 14475264 | tf_op jit(solution)/shard_map/finish/pallas_call | solution.py:414
  148.7 11.7 %norm.1 = (bf16[4,256,768]{2,1,0:T(8,128)(2,1)}, bf16[4,256,768]{2,1,0:T(8,128)(2,1)}, f32[4,256,768]{2,1,0:T(8,128)}, f32[4,256,128]{2,1,0:T(8,128)}, bf16[8,384,128]{2,1,0:T(8,128)(2,1)}, /*index=5*/f32[8,768]{1,0:T(8,128)}) custom-call(f32[4,256,768]{2,1,0:T(8,128)} %get-tuple-element.124.y_ref, bf16[4,256,1024]{2,1,0:T(8,128)(2,1)} %get-tuple-element.115.act_ref, ...), custom_call_target="tpu_custom_call" | custom-call | bytes 18268160 | tf_op jit(solution)/shard_map/norm/pallas_call | solution.py:414
  186.1 7.3 %fusion.26 = f32[4,256,1536]{2,1,0:T(8,128)} fusion(bf16[4,256,768]{2,1,0:T(8,128)(2,1)} %get-tuple-element.127, bf16[768,384]{1,0:T(8,128)(2,1)} %collective-permute-done.14, bf16[768,384]{1,0:T(8,128)(2,1)} %collective-permute-done.13, bf16[768,384]{1,0:T(8,128)(2,1)} %collective-permute-done.12, bf16[768,384]{1,0:T(8,128)(2,1)} %get-tuple-element.119), kind=kOutput, calls=%fused_computation.61 | convolution fusion | flops 2425356288 | bytes 10223616 | tf_op jit(solution)/shard_map/dot_general | solution.py:955
  197.2 5.5 %all-to-all-start.3 = ((bf16[8,384,128]{2,1,0:T(8,128)(2,1)}), bf16[8,384,128]{2,1,0:T(8,128)(2,1)S(1)}, u32[]{:S(2)}, u32[]{:S(2)}) async-start(bf16[8,384,128]{2,1,0:T(8,128)(2,1)} %back_chain.1), calls=%async_computation.3 | async-start | bytes 1572864 | tf_op jit(solution)/shard_map/all_to_all | solution.py:523
  209.4 16.1 %backward.1 = (f32[4,256,768]{2,1,0:T(8,128)}, f32[4,256,256]{2,1,0:T(8,128)}) custom-call(bf16[4,256,1024]{2,1,0:T(8,128)(2,1)} %get-tuple-element.115.act_ref, f32[4,256,768]{2,1,0:T(8,128)} %get-tuple-element.132.dy_ref, f32[4,256,128]{2,1,0:T(8,128)} %get-tuple-element.117.lac_ref, f32[4,16,256]{2,1,0:T(8,128)} %get-tuple-element.133.lar_ref, ...), custom_call_target="tpu_custom_call" | custom-call | flops 805306368 | bytes 10878976 | tf_op jit(solution)/shard_map/backward/pallas_call | solution.py:414
  255.4 16.2 %carry.1 = (f32[4,256,768]{2,1,0:T(8,128)}, f32[4,8,768]{2,1,0:T(8,128)}, bf16[4,256,128]{2,1,0:T(8,128)(2,1)}, f32[8,768]{1,0:T(8,128)}, f32[8,128]{1,0:T(8,128)}) custom-call(bf16[4,272,1152]{2,1,0:T(8,128)(2,1)} %convolution_convert_fusion.pc_ref, f32[8,1024]{1,0:T(8,128)} %pad_maximum_fusion.23.taps_ref, f32[8,128]{1,0:T(8,128)} %select_maximum_fusion.2.rate_ref, ...), custom_call_target="tpu_custom_call" | custom-call | bytes 18456576 | tf_op jit(solution)/shard_map/carry/pallas_call | solution.py:414
  298.4 11.4 %collective-permute-done.34 = bf16[1,4,96,384]{3,2,1,0:T(8,128)(2,1)S(1)} collective-permute-done((bf16[1,4,96,384]{3,2,1,0:T(8,128)(2,1)S(1)}, bf16[1,4,96,384]{3,2,1,0:T(8,128)(2,1)S(1)}, u32[]{:S(2)}, u32[]{:S(2)}) %collective-permute-start.34) | collective-permute-done | bytes 294944 | tf_op jit(solution)/shard_map/ppermute | solution.py:435
  324.9 10.2 %collective-permute-start.36 = (bf16[2,4,96,384]{3,2,1,0:T(8,128)(2,1)S(1)}, bf16[2,4,96,384]{3,2,1,0:T(8,128)(2,1)S(1)}, u32[]{:S(2)}, u32[]{:S(2)}) collective-permute-start(bf16[2,4,96,384]{3,2,1,0:T(8,128)(2,1)S(1)} %pad_maximum_fusion.12), channel_id=1, source_target_pairs={{0,8},{4,12},{8,0},{12,4},{16,24},{20,28},{24,16},{28,20},{1,9},{5... | collective-permute-start | bytes 1769480 | tf_op jit(solution)/shard_map/ppermute | solution.py:435
  337.4 17.4 %collective-permute-done.36 = bf16[2,4,96,384]{3,2,1,0:T(8,128)(2,1)S(1)} collective-permute-done((bf16[2,4,96,384]{3,2,1,0:T(8,128)(2,1)S(1)}, bf16[2,4,96,384]{3,2,1,0:T(8,128)(2,1)S(1)}, u32[]{:S(2)}, u32[]{:S(2)}) %collective-permute-start.36) | collective-permute-done | bytes 589856 | tf_op jit(solution)/shard_map/ppermute | solution.py:435
  357.4 6.1 %collective-permute-start.43 = (bf16[2,96,1536]{2,1,0:T(8,128)(2,1)}, bf16[2,96,1536]{2,1,0:T(8,128)(2,1)S(1)}, u32[]{:S(2)}, u32[]{:S(2)}) collective-permute-start(bf16[2,96,1536]{2,1,0:T(8,128)(2,1)} %pad_maximum_fusion.13), channel_id=1, source_target_pairs={{0,8},{4,12},{8,0},{12,4},{16,24},{20,28},{24,16},{28,20},{1,9},{5... | collective-permute-start | bytes 1769480 | tf_op jit(solution)/shard_map/ppermute | solution.py:435
  372.1 17.2 %collective-permute-done.39 = bf16[2,56,1536]{2,1,0:T(8,128)(2,1)S(1)} collective-permute-done((bf16[2,56,1536]{2,1,0:T(8,128)(2,1)}, bf16[2,56,1536]{2,1,0:T(8,128)(2,1)S(1)}, u32[]{:S(2)}, u32[]{:S(2)}) %collective-permute-start.39) | collective-permute-done | bytes 344096 | tf_op jit(solution)/shard_map/ppermute | solution.py:435
  389.6 8.1 %collective-permute-done.42 = bf16[1,56,1536]{2,1,0:T(8,128)(2,1)S(1)} collective-permute-done((bf16[1,56,1536]{2,1,0:T(8,128)(2,1)S(1)}, bf16[1,56,1536]{2,1,0:T(8,128)(2,1)S(1)}, u32[]{:S(2)}, u32[]{:S(2)}) %collective-permute-start.42) | collective-permute-done | bytes 172064 | tf_op jit(solution)/shard_map/ppermute | solution.py:435
  410.2 7.9 %collective-permute-done.54 = bf16[1,4,56,384]{3,2,1,0:T(8,128)(2,1)S(1)} collective-permute-done((bf16[1,4,56,384]{3,2,1,0:T(8,128)(2,1)S(1)}, bf16[1,4,56,384]{3,2,1,0:T(8,128)(2,1)S(1)}, u32[]{:S(2)}, u32[]{:S(2)}) %collective-permute-start.54) | collective-permute-done | bytes 172064 | tf_op jit(solution)/shard_map/ppermute | solution.py:435
  430.2 6.3 %collective-permute-done.56 = bf16[2,4,56,384]{3,2,1,0:T(8,128)(2,1)S(1)} collective-permute-done((bf16[2,4,56,384]{3,2,1,0:T(8,128)(2,1)S(1)}, bf16[2,4,56,384]{3,2,1,0:T(8,128)(2,1)S(1)}, u32[]{:S(2)}, u32[]{:S(2)}) %collective-permute-start.56) | collective-permute-done | bytes 344096 | tf_op jit(solution)/shard_map/ppermute | solution.py:435
  457.8 12.5 %collective-permute-done.59 = bf16[4,4,56,384]{3,2,1,0:T(8,128)(2,1)} collective-permute-done((bf16[4,4,56,384]{3,2,1,0:T(8,128)(2,1)}, bf16[4,4,56,384]{3,2,1,0:T(8,128)(2,1)}, u32[]{:S(2)}, u32[]{:S(2)}) %collective-permute-start.59) | collective-permute-done | bytes 688160 | tf_op jit(solution)/shard_map/ppermute | solution.py:435
  471.8 6.3 %assemble.1 = (f32[6448,384]{1,0:T(8,128)}, f32[4,128,384]{2,1,0:T(8,128)S(1)}, f32[8,384]{1,0:T(8,128)S(1)}) custom-call(s32[2]{0:T(128)S(1)} %pad_add_fusion.ids_ref, bf16[8,4,96,384]{3,2,1,0:T(8,128)(2,1)S(1)} %pad_maximum_fusion.2.gate_ref, bf16[8,4,56,384]{3,2,1,0:T(8,128)(2,1)S(1)} %pad_maximum_fusion.6.refs_0_, ...), custom_call_target="tpu_custom_call" | custom-call | bytes 20766720 | tf_op jit(solution)/shard_map/assemble/pallas_call | solution.py:414
  (427 shorter events, 241.1 us)
Async XLA Ops:
  13.8 38.3 %collective-permute-start.9 = (bf16[768,384]{1,0:T(8,128)(2,1)}, bf16[768,384]{1,0:T(8,128)(2,1)S(1)}, u32[]{:S(2)}, u32[]{:S(2)}) collective-permute-start(bf16[768,384]{1,0:T(8,128)(2,1)} %get-tuple-element.218), channel_id=1, source_target_pairs={{0,1},{1,0},{2,3},{3,2},{4,5},{5,4},{6,7},{7,6},{8,9},{9,8},{10,11... | collective-permute-start | bytes 1769480 | tf_op jit(solution)/shard_map/ppermute | solution.py:435
  14.8 33.0 %collective-permute-start.10 = (bf16[1,304,384]{2,1,0:T(8,128)(2,1)S(1)}, bf16[1,304,384]{2,1,0:T(8,128)(2,1)S(1)}, u32[]{:S(2)}, u32[]{:S(2)}) collective-permute-start(bf16[1,304,384]{2,1,0:T(8,128)(2,1)S(1)} %slice_bitcast_fusion.6), channel_id=1, source_target_pairs={{0,2},{1,3},{2,0},{3,1},{4,6},{5,7},{6,4},{7,5},{8,10},{9,11},{10,... | collective-permute-start | bytes 700424 | tf_op jit(solution)/shard_map/ppermute | solution.py:435
  50.0 34.2 %collective-permute-start.15 = (bf16[1,256,1536]{2,1,0:T(8,128)(2,1)}, bf16[1,256,1536]{2,1,0:T(8,128)(2,1)}, u32[]{:S(2)}, u32[]{:S(2)}) collective-permute-start(bf16[1,256,1536]{2,1,0:T(8,128)(2,1)} %bitcast.30), channel_id=1, source_target_pairs={{0,2},{1,3},{2,0},{3,1},{4,6},{5,7},{6,4},{7,5},{8,10},{9,11},{10,... | collective-permute-start | bytes 2359304 | tf_op jit(solution)/shard_map/ppermute | solution.py:435
  78.2 27.3 %all-to-all-start = ((bf16[8,400,128]{2,1,0:T(8,128)(2,1)}), bf16[8,400,128]{2,1,0:T(8,128)(2,1)}, u32[]{:S(2)}, u32[]{:S(2)}) async-start(bf16[8,400,128]{2,1,0:T(8,128)(2,1)} %get-tuple-element.118.s_ref), calls=%async_computation | async-start | bytes 1638400 | tf_op jit(solution)/shard_map/all_to_all | solution.py:523
  86.9 34.1 %collective-permute-start.16 = (bf16[2,256,1536]{2,1,0:T(8,128)(2,1)}, bf16[2,256,1536]{2,1,0:T(8,128)(2,1)}, u32[]{:S(2)}, u32[]{:S(2)}) collective-permute-start(bf16[2,256,1536]{2,1,0:T(8,128)(2,1)} %pad_maximum_fusion.5), channel_id=1, source_target_pairs={{0,1},{1,0},{2,3},{3,2},{4,5},{5,4},{6,7},{7,6},{8,9},{9,8},{10,11... | collective-permute-start | bytes 4718600 | tf_op jit(solution)/shard_map/ppermute | solution.py:435
  86.9 27.1 %collective-permute-start.12 = (bf16[768,384]{1,0:T(8,128)(2,1)}, bf16[768,384]{1,0:T(8,128)(2,1)}, u32[]{:S(2)}, u32[]{:S(2)}) collective-permute-start(bf16[768,384]{1,0:T(8,128)(2,1)} %get-tuple-element.120), channel_id=1, source_target_pairs={{0,1},{1,0},{2,3},{3,2},{4,5},{5,4},{6,7},{7,6},{8,9},{9,8},{10,11... | collective-permute-start | bytes 1769480 | tf_op jit(solution)/shard_map/ppermute | solution.py:435
  87.5 26.6 %collective-permute-start.13 = (bf16[768,384]{1,0:T(8,128)(2,1)}, bf16[768,384]{1,0:T(8,128)(2,1)}, u32[]{:S(2)}, u32[]{:S(2)}) collective-permute-start(bf16[768,384]{1,0:T(8,128)(2,1)} %get-tuple-element.121), channel_id=1, source_target_pairs={{0,2},{1,3},{2,0},{3,1},{4,6},{5,7},{6,4},{7,5},{8,10},{9,11},{10,... | collective-permute-start | bytes 1769480 | tf_op jit(solution)/shard_map/ppermute | solution.py:435
  89.0 25.7 %collective-permute-start.14 = (bf16[768,384]{1,0:T(8,128)(2,1)}, bf16[768,384]{1,0:T(8,128)(2,1)}, u32[]{:S(2)}, u32[]{:S(2)}) collective-permute-start(bf16[768,384]{1,0:T(8,128)(2,1)} %get-tuple-element.122), channel_id=1, source_target_pairs={{0,3},{1,2},{2,1},{3,0},{4,7},{5,6},{6,5},{7,4},{8,11},{9,10},{10,... | collective-permute-start | bytes 1769480 | tf_op jit(solution)/shard_map/ppermute | solution.py:435
  109.3 24.7 %all-to-all-start.1 = ((bf16[8,384,128]{2,1,0:T(8,128)(2,1)}), bf16[8,384,128]{2,1,0:T(8,128)(2,1)}, u32[]{:S(2)}, u32[]{:S(2)}) async-start(bf16[8,384,128]{2,1,0:T(8,128)(2,1)} %copy-done.12), calls=%async_computation.1 | async-start | bytes 1572864 | tf_op jit(solution)/shard_map/all_to_all | solution.py:523
  165.8 27.7 %all-to-all-start.2 = ((bf16[8,384,128]{2,1,0:T(8,128)(2,1)}), bf16[8,384,128]{2,1,0:T(8,128)(2,1)S(1)}, u32[]{:S(2)}, u32[]{:S(2)}) async-start(bf16[8,384,128]{2,1,0:T(8,128)(2,1)} %get-tuple-element.129), calls=%async_computation.2 | async-start | bytes 1572864 | tf_op jit(solution)/shard_map/all_to_all | solution.py:523
  171.6 34.7 %collective-permute-start.20 = (bf16[4,96,1536]{2,1,0:T(8,128)(2,1)S(1)}, bf16[4,96,1536]{2,1,0:T(8,128)(2,1)}, u32[]{:S(2)}, u32[]{:S(2)}) collective-permute-start(bf16[4,96,1536]{2,1,0:T(8,128)(2,1)S(1)} %get-tuple-element.227), channel_id=1, source_target_pairs={{0,4},{4,0},{8,12},{12,8},{16,20},{20,16},{24,28},{28,24},{1,5},{5... | collective-permute-start | bytes 3538952 | tf_op jit(solution)/shard_map/ppermute | solution.py:435
  183.1 63.6 %collective-permute-start.21 = (bf16[4,96,1536]{2,1,0:T(8,128)(2,1)}, bf16[4,96,1536]{2,1,0:T(8,128)(2,1)}, u32[]{:S(2)}, u32[]{:S(2)}) collective-permute-start(bf16[4,96,1536]{2,1,0:T(8,128)(2,1)} %get-tuple-element.225), channel_id=1, source_target_pairs={{0,4},{4,0},{8,12},{12,8},{16,20},{20,16},{24,28},{28,24},{1,5},{5... | collective-permute-start | bytes 3538952 | tf_op jit(solution)/shard_map/ppermute | solution.py:435
  185.2 40.4 %collective-permute-start.28 = (bf16[2,256,1536]{2,1,0:T(8,128)(2,1)}, bf16[2,256,1536]{2,1,0:T(8,128)(2,1)}, u32[]{:S(2)}, u32[]{:S(2)}) collective-permute-start(bf16[2,256,1536]{2,1,0:T(8,128)(2,1)} %fusion.18), channel_id=1, source_target_pairs={{0,1},{1,0},{2,3},{3,2},{4,5},{5,4},{6,7},{7,6},{8,9},{9,8},{10,11... | collective-permute-start | bytes 4718600 | tf_op jit(solution)/shard_map/ppermute | solution.py:435
  197.2 42.6 %all-to-all-start.3 = ((bf16[8,384,128]{2,1,0:T(8,128)(2,1)}), bf16[8,384,128]{2,1,0:T(8,128)(2,1)S(1)}, u32[]{:S(2)}, u32[]{:S(2)}) async-start(bf16[8,384,128]{2,1,0:T(8,128)(2,1)} %back_chain.1), calls=%async_computation.3 | async-start | bytes 1572864 | tf_op jit(solution)/shard_map/all_to_all | solution.py:523
  232.0 41.8 %collective-permute-start.23 = (bf16[1,96,1536]{2,1,0:T(8,128)(2,1)}, bf16[1,96,1536]{2,1,0:T(8,128)(2,1)}, u32[]{:S(2)}, u32[]{:S(2)}) collective-permute-start(bf16[1,96,1536]{2,1,0:T(8,128)(2,1)} %get-tuple-element.255), channel_id=1, source_target_pairs={{0,16},{4,20},{8,24},{12,28},{16,0},{20,4},{24,8},{28,12},{1,17},{... | collective-permute-start | bytes 884744 | tf_op jit(solution)/shard_map/ppermute | solution.py:435
  290.0 34.8 %collective-permute-start.37 = (bf16[1,96,1536]{2,1,0:T(8,128)(2,1)}, bf16[1,96,1536]{2,1,0:T(8,128)(2,1)}, u32[]{:S(2)}, u32[]{:S(2)}) collective-permute-start(bf16[1,96,1536]{2,1,0:T(8,128)(2,1)} %get-tuple-element.253), channel_id=1, source_target_pairs={{0,16},{4,20},{8,24},{12,28},{16,0},{20,4},{24,8},{28,12},{1,17},{... | collective-permute-start | bytes 884744 | tf_op jit(solution)/shard_map/ppermute | solution.py:435
  320.6 35.4 %collective-permute-start.41 = (bf16[4,56,1536]{2,1,0:T(8,128)(2,1)S(1)}, bf16[4,56,1536]{2,1,0:T(8,128)(2,1)S(1)}, u32[]{:S(2)}, u32[]{:S(2)}) collective-permute-start(bf16[4,56,1536]{2,1,0:T(8,128)(2,1)S(1)} %get-tuple-element.241), channel_id=1, source_target_pairs={{0,4},{4,0},{8,12},{12,8},{16,20},{20,16},{24,28},{28,24},{1,5},{5... | collective-permute-start | bytes 2064392 | tf_op jit(solution)/shard_map/ppermute | solution.py:435
  324.9 29.8 %collective-permute-start.36 = (bf16[2,4,96,384]{3,2,1,0:T(8,128)(2,1)S(1)}, bf16[2,4,96,384]{3,2,1,0:T(8,128)(2,1)S(1)}, u32[]{:S(2)}, u32[]{:S(2)}) collective-permute-start(bf16[2,4,96,384]{3,2,1,0:T(8,128)(2,1)S(1)} %pad_maximum_fusion.12), channel_id=1, source_target_pairs={{0,8},{4,12},{8,0},{12,4},{16,24},{20,28},{24,16},{28,20},{1,9},{5... | collective-permute-start | bytes 1769480 | tf_op jit(solution)/shard_map/ppermute | solution.py:435
  355.7 42.2 %collective-permute-start.46 = (bf16[4,4,96,384]{3,2,1,0:T(8,128)(2,1)}, bf16[4,4,96,384]{3,2,1,0:T(8,128)(2,1)}, u32[]{:S(2)}, u32[]{:S(2)}) collective-permute-start(bf16[4,4,96,384]{3,2,1,0:T(8,128)(2,1)} %constant_dynamic-update-slice_fusion), channel_id=1, source_target_pairs={{0,4},{4,0},{8,12},{12,8},{16,20},{20,16},{24,28},{28,24},{1,5},{5... | collective-permute-start | bytes 3538952 | tf_op jit(solution)/shard_map/ppermute | solution.py:435
  357.4 32.1 %collective-permute-start.43 = (bf16[2,96,1536]{2,1,0:T(8,128)(2,1)}, bf16[2,96,1536]{2,1,0:T(8,128)(2,1)S(1)}, u32[]{:S(2)}, u32[]{:S(2)}) collective-permute-start(bf16[2,96,1536]{2,1,0:T(8,128)(2,1)} %pad_maximum_fusion.13), channel_id=1, source_target_pairs={{0,8},{4,12},{8,0},{12,4},{16,24},{20,28},{24,16},{28,20},{1,9},{5... | collective-permute-start | bytes 1769480 | tf_op jit(solution)/shard_map/ppermute | solution.py:435
  364.3 25.0 %collective-permute-start.39 = (bf16[2,56,1536]{2,1,0:T(8,128)(2,1)}, bf16[2,56,1536]{2,1,0:T(8,128)(2,1)S(1)}, u32[]{:S(2)}, u32[]{:S(2)}) collective-permute-start(bf16[2,56,1536]{2,1,0:T(8,128)(2,1)} %get-tuple-element.251), channel_id=1, source_target_pairs={{0,8},{4,12},{8,0},{12,4},{16,24},{20,28},{24,16},{28,20},{1,9},{5... | collective-permute-start | bytes 1032200 | tf_op jit(solution)/shard_map/ppermute | solution.py:435
  369.2 52.8 %collective-permute-start.38 = (bf16[2,256,1536]{2,1,0:T(8,128)(2,1)S(1)}, bf16[2,256,1536]{2,1,0:T(8,128)(2,1)S(1)}, u32[]{:S(2)}, u32[]{:S(2)}) collective-permute-start(bf16[2,256,1536]{2,1,0:T(8,128)(2,1)S(1)} %fusion.19), channel_id=1, source_target_pairs={{0,1},{1,0},{2,3},{3,2},{4,5},{5,4},{6,7},{7,6},{8,9},{9,8},{10,11... | collective-permute-start | bytes 4718600 | tf_op jit(solution)/shard_map/ppermute | solution.py:435
  408.9 28.6 %collective-permute-start.58 = (bf16[4,96,1536]{2,1,0:T(8,128)(2,1)S(1)}, bf16[4,96,1536]{2,1,0:T(8,128)(2,1)S(1)}, u32[]{:S(2)}, u32[]{:S(2)}) collective-permute-start(bf16[4,96,1536]{2,1,0:T(8,128)(2,1)S(1)} %pad_maximum_fusion.8), channel_id=1, source_target_pairs={{0,4},{4,0},{8,12},{12,8},{16,20},{20,16},{24,28},{28,24},{1,5},{5... | collective-permute-start | bytes 3538952 | tf_op jit(solution)/shard_map/ppermute | solution.py:435
  438.9 31.4 %collective-permute-start.59 = (bf16[4,4,56,384]{3,2,1,0:T(8,128)(2,1)}, bf16[4,4,56,384]{3,2,1,0:T(8,128)(2,1)}, u32[]{:S(2)}, u32[]{:S(2)}) collective-permute-start(bf16[4,4,56,384]{3,2,1,0:T(8,128)(2,1)} %pad_maximum_fusion.10), channel_id=1, source_target_pairs={{0,4},{4,0},{8,12},{12,8},{16,20},{20,16},{24,28},{28,24},{1,5},{5... | collective-permute-start | bytes 2064392 | tf_op jit(solution)/shard_map/ppermute | solution.py:435
  (115 other events, 1192.5 us)
